TPU v7x, 512 devices: a whole 4x4x16 slice. The times are simulated.
512 devices in a mesh: grp: 32 (over y, z_lo), tp: 16 (over z_hi, x, core).
Axes of the slice: x: 4, y: 4, z: 16 (z_hi: 2, z_lo: 8; z = z_hi * 8 + z_lo), core: 2. Of those that a mesh axis runs over, the one named last changes fastest.
Arguments:
- tokens: bfloat16 [65536, 1536], P(('grp', 'tp')), may hold values from -6 to 6
- attn_gain: float32 [1536], replicated, may hold values from 0.1 to 1.9
- ffn_gain: float32 [1536], replicated, may hold values from 0.1 to 1.9
- w_query: bfloat16 [1536, 1024], P(None, 'tp')
- key_value_weight: bfloat16 [1536, 1024], P(None, 'tp'), may hold values from -0.15625 to 0.15625
- w_out: bfloat16 [1024, 1536], P('tp'), may hold values from -0.1875 to 0.1875
- segment_ids: int32 [65536], P(('grp', 'tp')), may hold values from 0 to 65535, as said below
- expert_ids: int32 [65536, 2], P(('grp', 'tp')), may hold values from 0 to 7, all different within a row; in each aligned block of 128 rows (0 to 127, 128 to 255, ...) at most 48 rows name the same one
- route_weights: float32 [65536, 2], P(('grp', 'tp')), may hold values from 0.2 to 1
- w_gate: bfloat16 [1536, 4096], P(None, 'tp'), may hold values from -0.15625 to 0.15625
- w_up: bfloat16 [1536, 4096], P(None, 'tp'), may hold values from -0.15625 to 0.15625
- w_down: bfloat16 [4096, 1536], P('tp'), may hold values from -0.25 to 0.25
- page_table: int32 [32, 128], P('grp'), may hold values from 0 to 127, each once within a row
Outputs:
- hidden_out: bfloat16 [65536, 1536], P(('grp', 'tp'))
- kv_cache: bfloat16 [4096, 16, 1024], P(('grp', 'tp'))
Inputs may be any that keep to these rules, and one draw needn't show every extreme that they name: `segment_ids`: each token's number is the stream position of its prompt's first token, so numbers never fall along the stream; a prompt covers at most 1024 tokens and some prompt exactly 1024; a prompt runs from every group into the next; the last token of the stream is a prompt of its own. `expert_ids`: in the tokens of one device no expert is named more than 48 times; in some device's tokens one expert is named exactly 48 times. `page_table`: each row names every page of the group once.
All inputs are finite; a program needn't handle non-finite values.
Results may differ from a plain program's by a relative error of at most 0.015.
The roundings to bfloat16 on the way count: a program that leaves them out, or rounds other values in their place, can miss the bound.
Values may be sent and summed in bfloat16 or wider, within the bound.
No kernel may reach another device: no remote copies, remote signals or barrier semaphores. Data moves between devices by JAX's collectives and lax.ppermute only.
A program may use at most 64 MiB of HBM per device.

v0:
```python
import jax
import jax.numpy as jnp
from jax import lax
from jax.sharding import PartitionSpec as P

HEAD_SIZE = 64
PAGE = 16


def partner_2(block, axis, bit):
    count = lax.axis_size(axis)
    route = []
    for low in range(count):
        high = low | 1 << bit
        if high != low and high < count:
            route += [(low, high), (high, low)]
    return lax.ppermute(block, axis, route)


def from_behind(block, axis, distance):
    devices = range(lax.axis_size(axis))
    route = [(i - distance, i) for i in devices if i - distance in devices]
    return lax.ppermute(block, axis, route)


def rms_scale(row_data, gain_vec):
    values = row_data.astype(jnp.float32)
    inverse = lax.rsqrt(jnp.mean(values * values, axis=-1, keepdims=True) + 1e-05)
    return (values * inverse * gain_vec).astype(jnp.bfloat16)


def attend_blocks(query_rows, key_cat, value_cat, seg_query, seg_cat, maxlen, offset, block_rows):
    group_tok = query_rows.shape[0]
    key_span = maxlen + block_rows

    def one_block(block_index):
        first_row = block_index * block_rows
        query_block = lax.dynamic_slice_in_dim(query_rows, first_row, block_rows, 0)
        seg_block = lax.dynamic_slice_in_dim(seg_query, first_row, block_rows, 0)
        key_block = lax.dynamic_slice_in_dim(key_cat, first_row + offset, key_span, 0)
        value_block = lax.dynamic_slice_in_dim(value_cat, first_row + offset, key_span, 0)
        seg_keys = lax.dynamic_slice_in_dim(seg_cat, first_row + offset, key_span, 0)
        key_pos = first_row - maxlen + jnp.arange(key_span, dtype=jnp.int32)
        query_pos = first_row + jnp.arange(block_rows, dtype=jnp.int32)
        scores = (
            jnp.einsum("qhd,khd->hqk", query_block, key_block, preferred_element_type=jnp.float32)
            * 0.125
        )
        allowed = (seg_block[:, None] == seg_keys[None, :]) & (
            key_pos[None, :] <= query_pos[:, None]
        )
        scores = jnp.where(allowed[None], scores, -1e30)
        row_max = jnp.max(scores, axis=-1, keepdims=True)
        exponent = jnp.exp(scores - row_max)
        attention = (exponent / jnp.sum(exponent, axis=-1, keepdims=True)).astype(jnp.bfloat16)
        result = jnp.einsum(
            "hqk,khd->qhd", attention, value_block, preferred_element_type=jnp.float32
        )
        return result.astype(jnp.bfloat16)

    blocks = lax.map(one_block, jnp.arange(group_tok // block_rows, dtype=jnp.int32))
    return blocks.reshape(group_tok, -1)


def body(
    tokens,
    attn_gain,
    ffn_gain,
    w_query,
    key_value_weight,
    w_out,
    segment_ids,
    expert_ids,
    route_weights,
    w_gate,
    w_up,
    w_down,
    page_table,
):
    tok_rows = tokens.shape[0]
    tp_size = lax.axis_size("tp")
    head_cols = w_query.shape[1]
    heads_here = head_cols // HEAD_SIZE
    normed_in = rms_scale(tokens, attn_gain)
    both_cols = jnp.concatenate([w_query, key_value_weight], axis=1)
    projected = jnp.dot(
        lax.all_gather(normed_in, "tp", axis=0, tiled=True),
        both_cols,
        preferred_element_type=jnp.float32,
    ).astype(jnp.bfloat16)
    group_tok = projected.shape[0]
    query_rows = projected[:, :head_cols].reshape(group_tok, heads_here, HEAD_SIZE)
    own_slice = projected[:, head_cols:]
    page_count = group_tok // PAGE
    page_order = page_table[0]
    page_ids = jnp.arange(page_count, dtype=jnp.int32)
    source_block = jnp.sum(
        jnp.where(page_order[None, :] == page_ids[:, None], page_ids[None, :], 0), axis=1
    )
    ordered_pages = own_slice.reshape(page_count, PAGE, head_cols)[source_block]
    kv_cache = lax.all_to_all(ordered_pages, "tp", split_axis=0, concat_axis=2, tiled=True)
    seg_all = lax.all_gather(segment_ids, "tp", axis=0, tiled=True)
    maxlen = group_tok // 2
    block_rows = min(512, group_tok)
    low_half = lax.axis_index("tp") < tp_size // 2
    pair_bit = tp_size.bit_length() - 2
    partner = partner_2(own_slice, "tp", pair_bit)
    key_rows = jnp.where(low_half, own_slice, partner)
    value_rows = jnp.where(low_half, partner, own_slice)
    tail_keys, tail_values, tail_seg = from_behind((key_rows, value_rows, seg_all), "grp", 1)
    tail_seg = jnp.where(lax.axis_index("grp") > 0, tail_seg, -1)
    key_cat = jnp.concatenate([tail_keys, key_rows], 0).reshape(-1, heads_here, HEAD_SIZE)
    value_cat = jnp.concatenate([tail_values, value_rows], 0).reshape(-1, heads_here, HEAD_SIZE)
    seg_cat = jnp.concatenate([tail_seg, seg_all], 0)
    attended = attend_blocks(
        query_rows, key_cat, value_cat, seg_all, seg_cat, maxlen, group_tok - maxlen, block_rows
    )
    token_heads = lax.all_to_all(attended, "tp", split_axis=0, concat_axis=1, tiled=True)
    out_sum = jnp.dot(
        token_heads,
        lax.all_gather(w_out, "tp", axis=0, tiled=True),
        preferred_element_type=jnp.float32,
    )
    mid_state = (tokens.astype(jnp.float32) + out_sum).astype(jnp.bfloat16)
    normed_mid = rms_scale(mid_state, ffn_gain)
    expert_count = tp_size // 2
    choice_count = expert_ids.shape[1]
    capacity = min(tok_rows, 3 * tok_rows * choice_count // (2 * expert_count))
    routes_flat = expert_ids.reshape(-1)
    onehot = (routes_flat[:, None] == jnp.arange(expert_count, dtype=jnp.int32)[None, :]).astype(
        jnp.int32
    )
    earlier = jnp.cumsum(onehot, axis=0) - onehot
    slot_index = jnp.sum(earlier * onehot, axis=-1)
    target_slot = routes_flat * capacity + slot_index
    placement_map = (
        target_slot[:, None] == jnp.arange(expert_count * capacity, dtype=jnp.int32)[None, :]
    )
    placement_map = placement_map.reshape(tok_rows, choice_count, expert_count * capacity)
    select_map = jnp.sum(placement_map.astype(jnp.int32), axis=1).astype(jnp.bfloat16)
    model_width = normed_mid.shape[1]
    buffers = jnp.einsum(
        "te,td->ed", select_map, normed_mid, preferred_element_type=jnp.float32
    ).astype(jnp.bfloat16)
    send_buf = jnp.broadcast_to(
        buffers.reshape(expert_count, 1, capacity, model_width),
        (expert_count, 2, capacity, model_width),
    )
    send_buf = send_buf.reshape(2 * expert_count, capacity, model_width)
    row_data = lax.all_to_all(send_buf, "tp", split_axis=0, concat_axis=0, tiled=True)
    slot_count = row_data.shape[1]
    flat_rows = row_data.reshape(-1, model_width)
    gate_act = jnp.dot(flat_rows, w_gate, preferred_element_type=jnp.float32)
    up_act = jnp.dot(flat_rows, w_up, preferred_element_type=jnp.float32)
    activated = (jax.nn.silu(gate_act) * up_act).astype(jnp.bfloat16)
    half_out = jnp.dot(activated, w_down, preferred_element_type=jnp.float32).astype(jnp.bfloat16)
    half_out = half_out.reshape(row_data.shape[0], slot_count, model_width)
    returned = lax.all_to_all(half_out, "tp", split_axis=0, concat_axis=0, tiled=True)
    halves = returned.reshape(expert_count, 2, capacity, model_width)
    summed = (halves[:, 0].astype(jnp.float32) + halves[:, 1].astype(jnp.float32)).reshape(
        expert_count * capacity, model_width
    )
    picked = summed[target_slot].reshape(tok_rows, choice_count, model_width)
    expert_sum = jnp.sum(picked * route_weights[..., None], axis=1)
    hidden_out = (mid_state.astype(jnp.float32) + expert_sum).astype(jnp.bfloat16)
    return (hidden_out, kv_cache)


def solution(mesh):
    in_specs = (
        P(("grp", "tp"), None),
        P(),
        P(),
        P(None, "tp"),
        P(None, "tp"),
        P("tp", None),
        P(("grp", "tp")),
        P(("grp", "tp"), None),
        P(("grp", "tp"), None),
        P(None, "tp"),
        P(None, "tp"),
        P("tp", None),
        P("grp", None),
    )
    out_specs = (P(("grp", "tp"), None), P(("grp", "tp"), None, None))
    return jax.shard_map(body, mesh=mesh, in_specs=in_specs, out_specs=out_specs, check_vma=False)
```

profile of v0, /device:TPU:103, one launch (start us, length us, event | category | flops | bytes accessed | tf_op | source)
XLA Modules:
  0.0 620.0 jit_solution(16437475761888153532)
XLA Ops:
  7.2 1.2 fusion.17
  8.5 1.9 fusion.19
  10.4 152.5 %all-gather.4.cloned.1.call-done = bf16[2048,1536]{1,0:T(8,128)(2,1)} async-done(((bf16[128,1536]{1,0:T(8,128)(2,1)}), bf16[2048,1536]{1,0:T(8,128)(2,1)}) %all-gather.4.cloned.1.call-update) | async-done | bytes 6291472 | tf_op jit(solution)/shard_map/all_gather | solution.py:87
  163.0 4.9 convolution_convert_fusion.2
  167.9 1.9 collective-permute-start
  169.9 43.4 %all-gather = s32[16,1,128]{2,1,0:T(1,128)S(1)} all-gather(s32[1,1,128]{2,1,0:T(1,128)S(1)} %bitcast.102), channel_id=1, replica_groups=mesh['grp'=32,'tp'=16] {'tp'}, dimensions={0}, use_global_device_ids=true | all-gather | bytes 8704 | tf_op jit(solution)/shard_map/all_gather | solution.py:102
  213.2 1.9 collective-permute-start.2
  215.3 1.9 collective-permute-start.3
  217.2 3.0 collective-permute-done.2
  220.2 1.9 collective-permute-start.1
  222.1 5.5 collective-permute-done.3
  227.7 5.6 collective-permute-done.1
  233.4 15.4 %while.12 = (s32[]{:T(128)}, bf16[4,512,1,64]{1,3,2,0:T(8,128)(2,1)S(1)}, s32[4]{0:T(128)S(1)}, bf16[4096,1,64]{0,2,1:T(8,128)(2,1)S(1)}, s32[2048]{0:T(1024)S(1...) while((s32[]{:T(128)}, ...), condition=%wide.region_4.5_spmd, body=%wide.region_1.4_spmd.sunk | while | flops 210011136 | bytes 10017057 | solution.py:61
  233.4 0.6 dynamic_slice.62
  234.8 1.0 fusion.54
  235.8 0.6 fusion.55
  236.4 0.8 fusion.56
  237.2 0.6 dynamic_slice.62
  238.6 1.0 fusion.54
  239.6 0.6 fusion.55
  240.2 0.8 fusion.56
  241.1 0.6 dynamic_slice.62
  242.5 1.0 fusion.54
  243.5 0.6 fusion.55
  244.1 0.8 fusion.56
  244.9 0.6 dynamic_slice.62
  246.3 1.0 fusion.54
  247.3 0.6 fusion.55
  247.9 0.8 fusion.56
  248.8 0.2 copy.43
  249.1 0.8 copy.44
  249.9 20.4 %all-to-all-start = ((bf16[16,128,64]{1,2,0:T(8,128)(2,1)}), bf16[16,128,64]{1,2,0:T(8,128)(2,1)S(1)}, u32[]{:S(2)}, u32[]{:S(2)}) async-start(bf16[16,128,64]{1,2,0:T(8,128)(2,1)} %copy.44), calls=%async_computation | async-start | bytes 524288 | tf_op jit(solution)/shard_map/all_to_all | solution.py:118
  270.3 0.1 eq.80
  270.5 0.1 eq.76
  270.6 0.6 reduce-window.6
  271.2 0.2 slice_reduce_fusion
  271.6 0.1 reduce_sum.71
  271.8 0.1 convert_reduce_fusion
  271.9 55.3 %all-gather.6.cloned.1.call-done = bf16[1024,1536]{1,0:T(8,128)(2,1)} async-done(((bf16[64,1536]{1,0:T(8,128)(2,1)}), bf16[1024,1536]{1,0:T(8,128)(2,1)}) %all-gather.6.cloned.1.call-update) | async-done | bytes 3145744 | tf_op jit(solution)/shard_map/all_gather | solution.py:121
  327.2 2.6 multiply_reduce_fusion.1
  329.8 0.9 copy-done.2
  330.7 0.5 convolution_convert_fusion.1
  331.2 1.6 broadcast_in_dim.43
  332.9 6.5 %all-to-all-start.1 = ((bf16[16,48,1536]{2,1,0:T(8,128)(2,1)}), bf16[16,48,1536]{2,1,0:T(8,128)(2,1)S(1)}, u32[]{:S(2)}, u32[]{:S(2)}) async-start(bf16[16,48,1536]{2,1,0:T(8,128)(2,1)} %bitcast.17), calls=%async_computation.1 | async-start | bytes 4718592 | tf_op jit(solution)/shard_map/all_to_all | solution.py:150
  339.5 1.0 copy.52
  340.5 2.5 gather_fusion.1
  343.0 2.1 reshape.219
  345.2 109.4 %all-to-all-done.1 = bf16[16,48,1536]{2,1,0:T(8,128)(2,1)S(1)} async-done(((bf16[16,48,1536]{2,1,0:T(8,128)(2,1)}), bf16[16,48,1536]{2,1,0:T(8,128)(2,1)S(1)}, u32[]{:S(2)}, u32[]{:S(2)}) %all-to-all-start.1) | async-done | bytes 2359328 | tf_op jit(solution)/shard_map/all_to_all | solution.py:150
  454.6 10.4 %all-to-all-start.3 = ((bf16[16,2,4096]{2,1,0:T(2,128)(2,1)}), bf16[16,2,4096]{2,1,0:T(2,128)(2,1)S(1)}, u32[]{:S(2)}, u32[]{:S(2)}) async-start(bf16[16,2,4096]{2,1,0:T(2,128)(2,1)} %reshape.219), calls=%async_computation.3 | async-start | bytes 524288 | tf_op jit(solution)/shard_map/all_to_all | solution.py:101
  465.0 2.8 fusion.40
  467.8 5.3 convolution_convert_fusion
  473.1 85.0 %all-to-all-done.3 = bf16[16,2,4096]{2,1,0:T(2,128)(2,1)S(1)} async-done(((bf16[16,2,4096]{2,1,0:T(2,128)(2,1)}), bf16[16,2,4096]{2,1,0:T(2,128)(2,1)S(1)}, u32[]{:S(2)}, u32[]{:S(2)}) %all-to-all-start.3) | async-done | bytes 262176 | tf_op jit(solution)/shard_map/all_to_all | solution.py:101
  558.1 4.5 all-to-all-start.2
  562.7 0.1 mul.106
  563.0 1.2 reshape.220
  564.1 2.2 copy.53
  566.3 2.1 all_to_all.42
  568.5 33.7 %all-to-all-done.2 = bf16[16,48,1536]{2,1,0:T(8,128)(2,1)S(1)} async-done(((bf16[16,48,1536]{2,1,0:T(8,128)(2,1)}), bf16[16,48,1536]{2,1,0:T(8,128)(2,1)S(1)}, u32[]{:S(2)}, u32[]{:S(2)}) %all-to-all-start.2) | async-done | bytes 2359328 | tf_op jit(solution)/shard_map/all_to_all | solution.py:158
  602.2 1.4 copy-done.1
  603.6 1.9 convert_add_fusion
  605.5 2.3 gather_fusion
  607.9 2.3 reshape.198
  610.2 2.2 multiply_reduce_fusion
  612.4 0.8 add_convert_fusion
  (64 shorter events, 1.6 us)
Async XLA Ops:
  7.2 460.7 %copy-start = (bf16[256,1536]{1,0:T(8,128)(2,1)S(1)}, bf16[256,1536]{1,0:T(8,128)(2,1)}, u32[]{:S(2)}) copy-start(bf16[256,1536]{1,0:T(8,128)(2,1)} %param.26) | copy-start | bytes 2359300
  7.2 155.8 %all-gather.4.cloned.1.call-start = ((), (), s32[]{:S(2)}) async-start(), calls=%async_computation.4 | async-start | bytes 6684672 | tf_op jit(solution)/shard_map/all_gather | solution.py:87
  10.4 159.5 %copy-start.8 = (s32[128]{0:T(128)S(1)}, s32[128]{0:T(128)}, u32[]{:S(2)}) copy-start(s32[128]{0:T(128)} %param.21) | copy-start | bytes 1540
  10.4 316.8 %all-gather.6.cloned.1.call-start = ((), (), s32[]{:S(2)}) async-start(), calls=%async_computation.5 | async-start | bytes 3342336 | tf_op jit(solution)/shard_map/all_gather | solution.py:121
  167.9 47.3 %collective-permute-start = (bf16[2048,64]{0,1:T(8,128)(2,1)S(1)}, bf16[2048,64]{0,1:T(8,128)(2,1)S(1)}, u32[]{:S(2)}, u32[]{:S(2)}) collective-permute-start(bf16[2048,64]{0,1:T(8,128)(2,1)S(1)} %slice.28), channel_id=1, source_target_pairs={{0,8},{8,0},{1,9},{9,1},{2,10},{10,2},{3,11},{11,3},{4,12},{12,4},... | collective-permute-start | bytes 786440 | tf_op jit(solution)/shard_map/ppermute | solution.py:17
  213.2 7.0 %collective-permute-start.2 = (s32[2048]{0:T(1024)S(1)}, s32[2048]{0:T(1024)S(1)}, u32[]{:S(2)}, u32[]{:S(2)}) collective-permute-start(s32[2048]{0:T(1024)S(1)} %bitcast.97), channel_id=1, source_target_pairs={{0,16},{16,32},{32,48},{48,64},{64,80},{80,96},{96,112},{112,128},... | collective-permute-start | bytes 24584 | tf_op jit(solution)/shard_map/ppermute | solution.py:23
  215.3 12.4 %collective-permute-start.3 = (bf16[2048,64]{0,1:T(8,128)(2,1)S(1)}, bf16[2048,64]{0,1:T(8,128)(2,1)S(1)}, u32[]{:S(2)}, u32[]{:S(2)}) collective-permute-start(bf16[2048,64]{0,1:T(8,128)(2,1)S(1)} %get-tuple-element.131), channel_id=1, source_target_pairs={{0,16},{16,32},{32,48},{48,64},{64,80},{80,96},{96,112},{112,128},... | collective-permute-start | bytes 786440 | tf_op jit(solution)/shard_map/ppermute | solution.py:23
  220.2 13.1 %collective-permute-start.1 = (bf16[2048,64]{0,1:T(8,128)(2,1)S(1)}, bf16[2048,64]{0,1:T(8,128)(2,1)S(1)}, u32[]{:S(2)}, u32[]{:S(2)}) collective-permute-start(bf16[2048,64]{0,1:T(8,128)(2,1)S(1)} %get-tuple-element.132), channel_id=1, source_target_pairs={{0,16},{16,32},{32,48},{48,64},{64,80},{80,96},{96,112},{112,128},... | collective-permute-start | bytes 786440 | tf_op jit(solution)/shard_map/ppermute | solution.py:23
  233.3 36.9 %copy-start.6 = (s32[128,2]{0,1:T(2,128)S(1)}, s32[128,2]{0,1:T(2,128)}, u32[]{:S(2)}) copy-start(s32[128,2]{0,1:T(2,128)} %param.22) | copy-start | bytes 3076
  248.8 78.4 %copy-start.4 = (bf16[128,1536]{1,0:T(8,128)(2,1)S(1)}, bf16[128,1536]{1,0:T(8,128)(2,1)}, u32[]{:S(2)}) copy-start(bf16[128,1536]{1,0:T(8,128)(2,1)} %param.15) | copy-start | bytes 1179652
  249.9 77.3 %all-to-all-start = ((bf16[16,128,64]{1,2,0:T(8,128)(2,1)}), bf16[16,128,64]{1,2,0:T(8,128)(2,1)S(1)}, u32[]{:S(2)}, u32[]{:S(2)}) async-start(bf16[16,128,64]{1,2,0:T(8,128)(2,1)} %copy.44), calls=%async_computation | async-start | bytes 524288 | tf_op jit(solution)/shard_map/all_to_all | solution.py:118
  271.8 58.9 %copy-start.5 = (f32[1536]{0:T(1024)S(1)}, f32[1536]{0:T(1024)}, u32[]{:S(2)}) copy-start(f32[1536]{0:T(1024)} %param.17) | copy-start | bytes 18436
  329.8 0.9 copy-start.2
  332.9 6.5 %copy-start.9 = (s32[1,128]{1,0:T(1,128)S(1)}, s32[1,128]{1,0:T(1,128)}, u32[]{:S(2)}) copy-start(s32[1,128]{1,0:T(1,128)} %param.27) | copy-start | bytes 1540
  332.9 121.7 %all-to-all-start.1 = ((bf16[16,48,1536]{2,1,0:T(8,128)(2,1)}), bf16[16,48,1536]{2,1,0:T(8,128)(2,1)S(1)}, u32[]{:S(2)}, u32[]{:S(2)}) async-start(bf16[16,48,1536]{2,1,0:T(8,128)(2,1)} %bitcast.17), calls=%async_computation.1 | async-start | bytes 4718592 | tf_op jit(solution)/shard_map/all_to_all | solution.py:150
  454.6 103.5 %all-to-all-start.3 = ((bf16[16,2,4096]{2,1,0:T(2,128)(2,1)}), bf16[16,2,4096]{2,1,0:T(2,128)(2,1)S(1)}, u32[]{:S(2)}, u32[]{:S(2)}) async-start(bf16[16,2,4096]{2,1,0:T(2,128)(2,1)} %reshape.219), calls=%async_computation.3 | async-start | bytes 524288 | tf_op jit(solution)/shard_map/all_to_all | solution.py:101
  558.1 4.7 copy-start.7
  558.1 44.0 %all-to-all-start.2 = ((bf16[16,48,1536]{2,1,0:T(8,128)(2,1)}), bf16[16,48,1536]{2,1,0:T(8,128)(2,1)S(1)}, u32[]{:S(2)}, u32[]{:S(2)}) async-start(bf16[16,48,1536]{2,1,0:T(8,128)(2,1)} %bitcast.93), calls=%async_computation.2 | async-start | bytes 4718592 | tf_op jit(solution)/shard_map/all_to_all | solution.py:158
  602.2 1.4 copy-start.1
  607.9 4.5 copy-start.3
Sparse Core Ops, SparseCore 0:
  11.9 151.0 all-gather.3
  215.3 111.8 all-gather.5
where the time goes:
time: 621 us; the launch traced here: 620 us
  waiting for transfers between devices  450 us (72%)
  starting transfers between devices  49.5 us (8%)
  blocking collectives  43.4 us (7%)
  local copies, waits for them, and re-layouts  24.9 us (4%)
  matrix products  23.5 us (4%)
  between operations  14.4 us (2%)
  other arithmetic  11.5 us (2%)
    all_gather x1, waiting for transfers between devices, body(): lax.all_gather(normed_in, 'tp', axis=0, tiled=True)  153 us
    all_to_all x1, waiting for transfers between devices, body(): lax.all_to_all(send_buf, 'tp', split_axis=0, concat_axis=0, tiled=True)  109 us
    all_to_all x1, waiting for transfers between devices, body(): lax.all_to_all(ordered_pages, 'tp', split_axis=0, concat_axis=2, tiled=True)  85 us
    all_gather x1, waiting for transfers between devices, body(): lax.all_gather(w_out, 'tp', axis=0, tiled=True)  55.3 us
    all_gather x1, blocking collectives, body(): seg_all = lax.all_gather(segment_ids, 'tp', axis=0, tiled=True)  43.4 us
    all_to_all x1, waiting for transfers between devices, body(): lax.all_to_all(half_out, 'tp', split_axis=0, concat_axis=0, tiled=True)  33.7 us
    all_to_all x1, starting transfers between devices, body(): lax.all_to_all(attended, 'tp', split_axis=0, concat_axis=1, tiled=True)  20.4 us
    ppermute x3, waiting for transfers between devices, from_behind(): return lax.ppermute(block, axis, route)  14.1 us
  transfers between devices with their start and end apart: 10, of which 8 were waited for; matrix products, arithmetic and copies ran while one was open for 5% of the time, Pallas kernels for 0%

commit v1 on v0

v1 whole, which is shorter than its diff:
```python
import functools

import jax
import jax.numpy as jnp
import numpy as np
from jax import lax
from jax.sharding import Mesh
from jax.sharding import PartitionSpec as P

AXES = ("y", "zl", "zh", "x", "c")
SIZES = (4, 8, 2, 4, 2)
ROW = ("x", "c")
PAGE = 16
CAP = 48


def permute(block, target):
    route = []
    for source in range(int(np.prod(SIZES))):
        place = dict(zip(AXES, (int(v) for v in np.unravel_index(source, SIZES))))
        goal = target(**place)
        if goal is not None:
            route.append((source, int(np.ravel_multi_index(goal, SIZES))))
    return lax.ppermute(block, AXES, route)


def swap_core(block):
    return permute(block, lambda y, zl, zh, x, c: (y, zl, zh, x, 1 - c))


def swap_half(block):
    return permute(block, lambda y, zl, zh, x, c: (y, zl, 1 - zh, x, c))


def swap_near(block):
    return permute(block, lambda y, zl, zh, x, c: (y, zl ^ 1, zh, x, c))


def next_group(block):
    def target(y, zl, zh, x, c):
        g = y * 8 + zl + 1
        return (g // 8, g % 8, zh, x, c) if zh == 0 and g < 32 else None

    return permute(block, target)


def ahead_x(block, step):
    return permute(block, lambda y, zl, zh, x, c: (y, zl, zh, (x - step) % 4, c))


def ahead_y(block, step):
    return permute(block, lambda y, zl, zh, x, c: ((y - step) % 4, zl, zh, x, c))


def from_all(block, ahead):
    one, three, two = [ahead(block, step) for step in (1, 3, 2)]
    return jnp.stack([block, one, two, three])


def in_order(relative, me):
    twice = jnp.concatenate([relative, relative], axis=0)
    return lax.dynamic_slice_in_dim(twice, (4 - me) % 4, 4, 0)


def rms_scale(row_data, gain_vec):
    values = row_data.astype(jnp.float32)
    inverse = lax.rsqrt(jnp.mean(values * values, axis=-1, keepdims=True) + 1e-05)
    return (values * inverse * gain_vec).astype(jnp.bfloat16)


def attend(queries, key_cat, value_cat, first_key, block_rows):
    rows = queries.shape[1]
    span = rows + block_rows
    outs = []
    for block in range(rows // block_rows):
        low = block * block_rows
        query = queries[:, low : low + block_rows]
        keys = key_cat[low : low + span]
        values = value_cat[low : low + span]
        position = low + jnp.arange(span, dtype=jnp.int32)
        own = rows + low + jnp.arange(block_rows, dtype=jnp.int32)
        allowed = (position[None, :] >= first_key[low : low + block_rows, None]) & (
            position[None, :] <= own[:, None]
        )
        scores = jnp.einsum("hqd,kd->hqk", query, keys, preferred_element_type=jnp.float32)
        scores = jnp.where(allowed[None], scores * 0.125, -1e30)
        exponent = jnp.exp(scores - jnp.max(scores, axis=-1, keepdims=True))
        weights = (exponent / jnp.sum(exponent, axis=-1, keepdims=True)).astype(jnp.bfloat16)
        result = jnp.einsum("hqk,kd->qhd", weights, values, preferred_element_type=jnp.float32)
        outs.append(result.astype(jnp.bfloat16).reshape(block_rows, -1))
    return jnp.concatenate(outs, axis=0)


def body(
    tokens,
    attn_gain,
    ffn_gain,
    w_query,
    key_value_weight,
    w_out,
    segment_ids,
    expert_ids,
    route_weights,
    w_gate,
    w_up,
    w_down,
    page_table,
):
    y, zl, zh, x, c = (lax.axis_index(name) for name in AXES)
    width = tokens.shape[1]
    tok = tokens.shape[0]
    rows = 8 * tok

    own_pack = jnp.concatenate([w_query.T, key_value_weight.T, w_out], axis=0)
    part = own_pack.shape[0] // 4
    far_part = swap_half(lax.dynamic_slice_in_dim(own_pack, y * part, part, 0))
    far_pack = in_order(from_all(far_part, ahead_y), y).reshape(-1, width)
    own_cols, far_cols = own_pack[:128], far_pack[:128]
    other_own = swap_core(own_cols)
    other_far = swap_core(far_cols)

    normed_in = rms_scale(tokens, attn_gain)
    near = from_all(normed_in, ahead_x).reshape(4 * tok, width)

    def project(cols):
        return lax.dot_general(
            near, cols, (((1,), (1,)), ((), ())), preferred_element_type=jnp.float32
        ).astype(jnp.bfloat16)

    keep = jnp.concatenate([project(own_cols), project(far_cols)], axis=1)
    give = jnp.concatenate([project(other_own), project(other_far)], axis=1)
    got = swap_core(give)
    both = jnp.where(c == 0, jnp.stack([keep, got]), jnp.stack([got, keep]))
    both = both.reshape(2, 4, tok, 256).transpose(1, 0, 2, 3)
    projected = in_order(both, x).reshape(rows, 256)
    queries = jnp.stack([projected[:, 0:64], projected[:, 128:192]])
    own_kv, far_kv = projected[:, 64:128], projected[:, 192:256]
    key_rows = jnp.where(zh == 0, own_kv, far_kv)
    value_rows = jnp.where(zh == 0, far_kv, own_kv)
    key_value = jnp.concatenate([key_rows, value_rows], axis=1)

    partner = swap_half(key_value)
    shifted = next_group(partner)
    before = jnp.where(zh == 0, shifted, partner)

    seg_near = from_all(segment_ids, ahead_x)
    seg_got = swap_core(seg_near)
    seg = jnp.where(c == 0, jnp.stack([seg_near, seg_got]), jnp.stack([seg_got, seg_near]))
    seg = in_order(seg.transpose(1, 0, 2), x).reshape(rows)
    base = ((y * 8 + zl) * 2 + zh) * rows
    first_key = seg - base + rows

    key_cat = jnp.concatenate([before[:, :64], key_rows], axis=0)
    value_cat = jnp.concatenate([before[:, 64:], value_rows], axis=0)
    attended = attend(queries, key_cat, value_cat, first_key, 512)

    group_kv = jnp.where(
        zh == 0, jnp.stack([key_value, partner]), jnp.stack([partner, key_value])
    )
    page_order = page_table[0]
    page_ids = zh * 64 + jnp.arange(64, dtype=jnp.int32)
    block_ids = jnp.arange(128, dtype=jnp.int32)
    source_block = jnp.sum(
        jnp.where(page_order[None, :] == page_ids[:, None], block_ids[None, :], 0), axis=1
    )
    pages = group_kv.reshape(128, PAGE, 128)[source_block]

    joined = jnp.concatenate(
        [attended.reshape(8, tok, 128), pages.reshape(8, tok, 128)], axis=1
    )
    joined = lax.all_to_all(joined, ROW, split_axis=0, concat_axis=0, tiled=True)
    token_heads = joined[:, :tok].transpose(1, 0, 2).reshape(tok, 1024)
    kv_cache = joined[:, tok:].reshape(8, 8, PAGE, 2, 64).transpose(1, 2, 3, 0, 4)
    kv_cache = kv_cache.reshape(8, PAGE, 1024)

    out_rows = jnp.concatenate([own_pack[128:], far_pack[128:]], axis=0)
    out_all = lax.all_gather(out_rows, ROW, axis=0, tiled=True)
    out_sum = jnp.dot(token_heads, out_all, preferred_element_type=jnp.float32)
    mid_state = (tokens.astype(jnp.float32) + out_sum).astype(jnp.bfloat16)
    normed_mid = rms_scale(mid_state, ffn_gain)

    gate_up = jnp.concatenate([w_gate, w_up], axis=1)
    piece = y * 2 + zl % 2

    def far_weight(own):
        step = own.shape[0] // 8
        eighth = swap_half(lax.dynamic_slice_in_dim(own, piece * step, step, 0))
        beside = swap_near(eighth)
        pair = jnp.where(
            zl % 2 == 0,
            jnp.concatenate([eighth, beside], axis=0),
            jnp.concatenate([beside, eighth], axis=0),
        )
        return lax.all_gather(pair, "y", axis=0, tiled=True)

    def whole(own):
        far = far_weight(own)
        mine = c == zh
        kept = jnp.where(mine, own, far)
        return kept, swap_core(jnp.where(mine, far, own))

    gate_up_a, gate_up_b = whole(gate_up)
    down_a, down_b = whole(w_down)

    flat = expert_ids.reshape(-1)
    onehot = (flat[:, None] == jnp.arange(8, dtype=jnp.int32)[None, :]).astype(jnp.int32)
    earlier = jnp.cumsum(onehot, axis=0) - onehot
    slot = jnp.sum(earlier * onehot, axis=-1)
    holder = (flat % 4) * 2 + flat // 4
    target_slot = (holder * CAP + slot).reshape(tok, 2)
    slots = jnp.arange(8 * CAP, dtype=jnp.int32)
    pick = [
        (target_slot[:, k : k + 1] == slots[None, :]).astype(jnp.bfloat16) for k in range(2)
    ]
    send = lax.dot_general(
        pick[0] + pick[1],
        normed_mid,
        (((0,), (0,)), ((), ())),
        preferred_element_type=jnp.float32,
    ).astype(jnp.bfloat16)
    arrived = lax.all_to_all(
        send.reshape(8, CAP, width), ROW, split_axis=0, concat_axis=0, tiled=True
    ).reshape(8 * CAP, width)

    def half(gate_up_half, down_half):
        both_act = jnp.dot(arrived, gate_up_half, preferred_element_type=jnp.float32)
        gate_act, up_act = both_act[:, :256], both_act[:, 256:]
        activated = (jax.nn.silu(gate_act) * up_act).astype(jnp.bfloat16)
        return jnp.dot(activated, down_half, preferred_element_type=jnp.float32)

    expert_out = (half(gate_up_a, down_a) + half(gate_up_b, down_b)).astype(jnp.bfloat16)
    returned = lax.all_to_all(
        expert_out.reshape(8, CAP, width), ROW, split_axis=0, concat_axis=0, tiled=True
    ).reshape(8 * CAP, width)
    total = mid_state.astype(jnp.float32)
    for k in range(2):
        chosen = jnp.dot(pick[k], returned, preferred_element_type=jnp.float32)
        total = total + chosen * route_weights[:, k : k + 1]
    return (total.astype(jnp.bfloat16), kv_cache)


def solution(mesh):
    fine = Mesh(mesh.devices.reshape(SIZES), AXES)
    grp, tp = ("y", "zl"), ("zh", "x", "c")
    in_specs = (
        P(AXES, None),
        P(),
        P(),
        P(None, tp),
        P(None, tp),
        P(tp, None),
        P(AXES),
        P(AXES, None),
        P(AXES, None),
        P(None, tp),
        P(None, tp),
        P(tp, None),
        P(grp, None),
    )
    out_specs = (P(AXES, None), P(AXES, None, None))
    return jax.shard_map(body, mesh=fine, in_specs=in_specs, out_specs=out_specs, check_vma=False)
```

time: 621 us -> 279 us (0.45)
  the two profiles are of different devices: /device:TPU:103 before, /device:TPU:24 now
where the time goes in v1:
time: 279 us; the launch traced here: 276 us
  starting transfers between devices  110 us (39%)
  waiting for transfers between devices  65.5 us (23%)
  matrix products  32.5 us (12%)
  other arithmetic  21.8 us (8%)
  local copies, waits for them, and re-layouts  17 us (6%)
  between operations  15.1 us (5%)
  blocking collectives  14.5 us (5%)
    ppermute x22, starting transfers between devices, permute(): return lax.ppermute(block, AXES, route)  96.1 us
    ppermute x22, waiting for transfers between devices, permute(): return lax.ppermute(block, AXES, route)  44.8 us
    all_to_all x1, waiting for transfers between devices, body(): lax.all_to_all(expert_out.reshape(8, CAP, width), ROW, split_axis=0, conc...  15.4 us
    all_gather x1, blocking collectives, far_weight(): return lax.all_gather(pair, 'y', axis=0, tiled=True)  14.5 us
    dot_general x2, matrix products, attend(): jnp.einsum('hqk,kd->qhd', weights, values, preferred_element_type=jnp.flo...  8.46 us
    sub x2, matrix products, attend(): exponent = jnp.exp(scores - jnp.max(scores, axis=-1, keepdims=True))  6.67 us
    unnamed x55, local copies, waits for them, and re-layouts  5.58 us
  transfers between devices with their start and end apart: 27, of which 9 were waited for; matrix products, arithmetic and copies ran while one was open for 23% of the time, Pallas kernels for 0%

profile of v1, /device:TPU:24, one launch (start us, length us, event | category | flops | bytes accessed | tf_op | source)
XLA Modules:
  0.0 276.3 jit_solution(10554161021707727774)
XLA Ops:
  7.2 1.2 fusion.28
  8.5 2.0 fusion.30
  10.4 4.7 %collective-permute-start = (bf16[128,1536]{1,0:T(8,128)(2,1)}, bf16[128,1536]{1,0:T(8,128)(2,1)}, u32[]{:S(2)}, u32[]{:S(2)}) collective-permute-start(bf16[128,1536]{1,0:T(8,128)(2,1)} %fusion.30), channel_id=1, source_target_pairs={{0,6},{1,7},{2,0},{3,1},{4,2},{5,3},{6,4},{7,5},{8,14},{9,15},{10,... | collective-permute-start | bytes 1179656 | tf_op jit(solution)/shard_map/ppermute | solution.py:24
  15.1 2.7 collective-permute-start.1
  17.8 3.1 %collective-permute-start.12 = (s32[128]{0:T(128)}, s32[128]{0:T(128)S(1)}, u32[]{:S(2)}, u32[]{:S(2)}) collective-permute-start(s32[128]{0:T(128)} %param.19), channel_id=1, source_target_pairs={{0,6},{1,7},{2,0},{3,1},{4,2},{5,3},{6,4},{7,5},{8,14},{9,15},{10,... | collective-permute-start | bytes 1544 | tf_op jit(solution)/shard_map/ppermute | solution.py:24
  20.9 3.7 %collective-permute-start.13 = (s32[128]{0:T(128)}, s32[128]{0:T(128)S(1)}, u32[]{:S(2)}, u32[]{:S(2)}) collective-permute-start(s32[128]{0:T(128)} %param.19), channel_id=1, source_target_pairs={{0,4},{1,5},{2,6},{3,7},{4,0},{5,1},{6,2},{7,3},{8,12},{9,13},{10,... | collective-permute-start | bytes 1544 | tf_op jit(solution)/shard_map/ppermute | solution.py:24
  24.6 3.1 %collective-permute-start.14 = (s32[128]{0:T(128)}, s32[128]{0:T(128)S(1)}, u32[]{:S(2)}, u32[]{:S(2)}) collective-permute-start(s32[128]{0:T(128)} %param.19), channel_id=1, source_target_pairs={{0,2},{1,3},{2,4},{3,5},{4,6},{5,7},{6,0},{7,1},{8,10},{9,11},{10,... | collective-permute-start | bytes 1544 | tf_op jit(solution)/shard_map/ppermute | solution.py:24
  27.8 1.2 fusion.146
  31.6 1.2 constant_dynamic-update-slice_fusion
  32.8 1.5 constant_dynamic-slice_fusion
  34.4 2.4 collective-permute-start.2
  36.8 15.7 %collective-permute-start.3 = (bf16[48,1536]{1,0:T(8,128)(2,1)S(1)}, bf16[48,1536]{1,0:T(8,128)(2,1)S(1)}, u32[]{:S(2)}, u32[]{:S(2)}) collective-permute-start(bf16[48,1536]{1,0:T(8,128)(2,1)S(1)} %fusion.56), channel_id=1, source_target_pairs={{0,8},{1,9},{2,10},{3,11},{4,12},{5,13},{6,14},{7,15},{8,0},{9,1},... | collective-permute-start | bytes 442376 | tf_op jit(solution)/shard_map/ppermute | solution.py:24
  52.5 1.9 collective-permute-start.15
  54.7 0.9 collective-permute-done.15
  55.6 1.9 collective-permute-start.16
  57.6 2.7 collective-permute-start.4
  60.9 6.4 %collective-permute-done.4 = bf16[48,1536]{1,0:T(8,128)(2,1)S(1)} collective-permute-done((bf16[48,1536]{1,0:T(8,128)(2,1)S(1)}, bf16[48,1536]{1,0:T(8,128)(2,1)S(1)}, u32[]{:S(2)}, u32[]{:S(2)}) %collective-permute-start.4) | collective-permute-done | bytes 147488 | tf_op jit(solution)/shard_map/ppermute | solution.py:24
  67.3 2.9 %collective-permute-start.5 = (bf16[48,1536]{1,0:T(8,128)(2,1)S(1)}, bf16[48,1536]{1,0:T(8,128)(2,1)S(1)}, u32[]{:S(2)}, u32[]{:S(2)}) collective-permute-start(bf16[48,1536]{1,0:T(8,128)(2,1)S(1)} %collective-permute-done.3), channel_id=1, source_target_pairs={{0,256},{1,257},{2,258},{3,259},{4,260},{5,261},{6,262},{7,263},{8... | collective-permute-start | bytes 442376 | tf_op jit(solution)/shard_map/ppermute | solution.py:24
  70.9 11.9 %collective-permute-done.16 = bf16[192,512]{1,0:T(8,128)(2,1)S(1)} collective-permute-done((bf16[192,512]{1,0:T(8,128)(2,1)S(1)}, bf16[192,512]{1,0:T(8,128)(2,1)S(1)}, u32[]{:S(2)}, u32[]{:S(2)}) %collective-permute-start.16) | collective-permute-done | bytes 196640 | tf_op jit(solution)/shard_map/ppermute | solution.py:24
  82.8 2.0 collective-permute-start.6
  84.8 6.8 %collective-permute-start.17 = (bf16[192,512]{1,0:T(8,128)(2,1)S(1)}, bf16[192,512]{1,0:T(8,128)(2,1)S(1)}, u32[]{:S(2)}, u32[]{:S(2)}) collective-permute-start(bf16[192,512]{1,0:T(8,128)(2,1)S(1)} %collective-permute-done.16), channel_id=1, source_target_pairs={{0,16},{1,17},{2,18},{3,19},{4,20},{5,21},{6,22},{7,23},{8,24},{9,... | collective-permute-start | bytes 589832 | tf_op jit(solution)/shard_map/ppermute | solution.py:24
  92.2 4.1 %collective-permute-done.17 = bf16[192,512]{1,0:T(8,128)(2,1)S(1)} collective-permute-done((bf16[192,512]{1,0:T(8,128)(2,1)S(1)}, bf16[192,512]{1,0:T(8,128)(2,1)S(1)}, u32[]{:S(2)}, u32[]{:S(2)}) %collective-permute-start.17) | collective-permute-done | bytes 196640 | tf_op jit(solution)/shard_map/ppermute | solution.py:24
  96.3 1.9 collective-permute-start.7
  98.2 0.9 maximum_select_fusion.2
  99.2 11.8 %collective-permute-start.18 = (bf16[32,1536]{1,0:T(8,128)(2,1)}, bf16[32,1536]{1,0:T(8,128)(2,1)}, u32[]{:S(2)}, u32[]{:S(2)}) collective-permute-start(bf16[32,1536]{1,0:T(8,128)(2,1)} %constant_dynamic-slice_fusion), channel_id=1, source_target_pairs={{0,8},{1,9},{2,10},{3,11},{4,12},{5,13},{6,14},{7,15},{8,0},{9,1},... | collective-permute-start | bytes 294920 | tf_op jit(solution)/shard_map/ppermute | solution.py:24
  114.3 1.1 constant_dynamic-slice_fusion.2
  116.2 0.8 pad_maximum_fusion.3
  117.1 2.1 collective-permute-start.8
  119.3 1.4 pad_maximum_fusion
  121.3 1.6 convolution_convert_fusion.2
  123.7 2.2 collective-permute-start.9
  127.6 1.0 fusion.34
  128.5 0.8 copy.47
  131.2 2.8 collective-permute-start.10
  133.9 1.6 compare_and_fusion
  135.5 18.2 %collective-permute-done.10 = bf16[1024,128]{0,1:T(8,128)(2,1)S(1)} collective-permute-done((bf16[1024,128]{0,1:T(8,128)(2,1)S(1)}, bf16[1024,128]{0,1:T(8,128)(2,1)S(1)}, u32[]{:S(2)}, u32[]{:S(2)}) %collective-permute-start.10) | collective-permute-done | bytes 262176 | tf_op jit(solution)/shard_map/ppermute | solution.py:24
  153.7 13.3 %collective-permute-start.11 = (bf16[1024,128]{0,1:T(8,128)(2,1)S(1)}, bf16[1024,128]{0,1:T(8,128)(2,1)}, u32[]{:S(2)}, u32[]{:S(2)}) collective-permute-start(bf16[1024,128]{0,1:T(8,128)(2,1)S(1)} %collective-permute-done.10), channel_id=1, source_target_pairs={{0,16},{1,17},{2,18},{3,19},{4,20},{5,21},{6,22},{7,23},{16,32},{1... | collective-permute-start | bytes 786440 | tf_op jit(solution)/shard_map/ppermute | solution.py:24
  167.0 1.8 fusion.8
  169.9 2.7 collective-permute-done.11
  172.6 1.0 broadcast_select_fusion.2
  174.3 3.3 %fusion.126 = f32[2,512]{1,0:T(2,128)S(1)} fusion(pred[512,1536]{1,0:T(8,128)(4,1)S(1)} %copy-done.6, bf16[1024,64]{0,1:T(8,128)(2,1)S(1)} %get-tuple-element.11, bf16[1024,64]{0,1:T(8,128)(2,1)} %copy-done.10, bf16[1,1024,64]{1,2,0:T(8,128)(2,1)} %get-tuple-element.6, bf16[1,1024,64]{1,2,0:T(8,128)(2,1)} %get-tuple-element.7), kind=kOutput, calls=%fused_computation.196 | convolution fusion | flops 208078336 | bytes 1314816 | tf_op jit(solution)/shard_map/sub | solution.py:87
  177.6 4.7 %fusion.23 = bf16[64,2,512]{2,0,1:T(8,128)(2,1)} fusion(f32[2,512]{1,0:T(2,128)S(1)} %fusion.126, pred[512,1536]{1,0:T(8,128)(4,1)S(1)} %copy-done.6, bf16[1024,64]{0,1:T(8,128)(2,1)} %get-tuple-element.10, bf16[1024,64]{0,1:T(8,128)(2,1)} %copy-done.12, bf16[1024,64]{0,1:T(8,128)(2,1)} %copy-done.15, bf16[1024,64]{0,1:T(8,128)(2,1)} %copy-done.10, ...), kind=kOutput, calls=%fused_computation.42 | convolution fusion | flops 411437568 | bytes 1708032 | tf_op jit(solution)/shard_map/hqk,kd->qhd/dot_general | solution.py:89
  182.3 3.4 %fusion.123 = f32[2,512]{1,0:T(2,128)S(1)} fusion(pred[512,1536]{1,0:T(8,128)(4,1)S(1)} %copy-done.5, bf16[1024,64]{0,1:T(8,128)(2,1)} %copy-done.10, bf16[1024,64]{0,1:T(8,128)(2,1)} %copy-done.15, bf16[1,1024,64]{1,2,0:T(8,128)(2,1)} %get-tuple-element.7, bf16[1,1024,64]{1,2,0:T(8,128)(2,1)} %get-tuple-element.6), kind=kOutput, calls=%fused_computation.195 | convolution fusion | flops 208274944 | bytes 1314816 | tf_op jit(solution)/shard_map/sub | solution.py:87
  185.7 3.8 %fusion.22 = bf16[64,2,512]{2,0,1:T(8,128)(2,1)S(1)} fusion(f32[2,512]{1,0:T(2,128)S(1)} %fusion.123, pred[512,1536]{1,0:T(8,128)(4,1)S(1)} %copy-done.5, bf16[1024,64]{0,1:T(8,128)(2,1)S(1)} %copy-done.13, bf16[1024,64]{0,1:T(8,128)(2,1)S(1)} %copy-done.14, bf16[1024,64]{0,1:T(8,128)(2,1)S(1)} %copy-done.11, bf16[1024,64]{0,1:T(8,128)(2,1)S(1)} %copy-done.16, ...), kind=kOutput, calls=%fused_computation.41 | convolution fusion | flops 411634176 | bytes 1708032 | tf_op jit(solution)/shard_map/hqk,kd->qhd/dot_general | solution.py:89
  189.7 0.8 pad_maximum_fusion.1
  190.5 4.5 %all-to-all-start = ((bf16[8,256,128]{2,1,0:T(8,128)(2,1)}), bf16[8,256,128]{2,1,0:T(8,128)(2,1)S(1)}, u32[]{:S(2)}, u32[]{:S(2)}) async-start(bf16[8,256,128]{2,1,0:T(8,128)(2,1)} %pad_maximum_fusion.1), calls=%async_computation | async-start | bytes 1048576 | tf_op jit(solution)/shard_map/all_to_all | solution.py:171
  195.5 4.7 %collective-permute-start.19 = (bf16[32,1536]{1,0:T(8,128)(2,1)}, bf16[32,1536]{1,0:T(8,128)(2,1)S(1)}, u32[]{:S(2)}, u32[]{:S(2)}) collective-permute-start(bf16[32,1536]{1,0:T(8,128)(2,1)} %collective-permute-done.18), channel_id=1, source_target_pairs={{0,16},{1,17},{2,18},{3,19},{4,20},{5,21},{6,22},{7,23},{8,24},{9,... | collective-permute-start | bytes 294920 | tf_op jit(solution)/shard_map/ppermute | solution.py:24
  200.2 5.2 %all-to-all-done = bf16[8,256,128]{2,1,0:T(8,128)(2,1)S(1)} async-done(((bf16[8,256,128]{2,1,0:T(8,128)(2,1)}), bf16[8,256,128]{2,1,0:T(8,128)(2,1)S(1)}, u32[]{:S(2)}, u32[]{:S(2)}) %all-to-all-start) | async-done | bytes 524320 | tf_op jit(solution)/shard_map/all_to_all | solution.py:171
  205.7 2.8 %broadcast_select_fusion = bf16[1536,512]{1,0:T(8,128)(2,1)} fusion(bf16[1536,512]{1,0:T(8,128)(2,1)} %all-gather.5.cloned.1.call-done, bf16[1536,512]{1,0:T(8,128)(2,1)S(1)} %constant_dynamic-update-slice_fusion, pred[]{:T(512)S(6)} %eq.119), kind=kLoop, calls=%fused_computation.37 | loop fusion | flops 786432 | bytes 4718593 | tf_op jit(solution)/shard_map/jit(_where)/select_n | solution.py:200
  208.4 1.9 collective-permute-start.20
  210.4 2.6 multiply_reduce_fusion
  213.0 1.6 convolution_convert_fusion
  214.6 4.3 %all-to-all-start.1 = ((bf16[8,48,1536]{2,1,0:T(8,128)(2,1)}), bf16[8,48,1536]{2,1,0:T(8,128)(2,1)}, u32[]{:S(2)}, u32[]{:S(2)}) async-start(bf16[8,48,1536]{2,1,0:T(8,128)(2,1)} %bitcast.44), calls=%async_computation.1 | async-start | bytes 2359296 | tf_op jit(solution)/shard_map/all_to_all | solution.py:221
  218.9 1.1 maximum_select_fusion.3
  219.9 14.5 %all_gather.11 = bf16[256,1536]{1,0:T(8,128)(2,1)S(1)} all-gather(bf16[64,1536]{1,0:T(8,128)(2,1)S(1)} %maximum_select_fusion.3), channel_id=1, replica_groups=mesh['y'=4,'zl'=8,'zh'=2,'x'=4,'c'=2] {'y'}, dimensions={0}, use_global_device_ids=true | all-gather | bytes 983040 | tf_op jit(solution)/shard_map/all_gather | solution.py:194
  234.5 1.0 broadcast_select_fusion.1
  235.5 1.9 collective-permute-start.21
  237.5 2.6 fusion.131
  240.1 2.2 fusion.19
  242.8 2.7 fusion.13
  245.5 4.9 %all-to-all-start.2 = ((bf16[8,48,1536]{2,1,0:T(8,128)(2,1)}), bf16[8,48,1536]{2,1,0:T(8,128)(2,1)S(1)}, u32[]{:S(2)}, u32[]{:S(2)}) async-start(bf16[8,48,1536]{2,1,0:T(8,128)(2,1)} %bitcast.46), calls=%async_computation.2 | async-start | bytes 2359296 | tf_op jit(solution)/shard_map/all_to_all | solution.py:232
  251.4 1.1 reshape.244
  252.4 15.4 %all-to-all-done.2 = bf16[8,48,1536]{2,1,0:T(8,128)(2,1)S(1)} async-done(((bf16[8,48,1536]{2,1,0:T(8,128)(2,1)}), bf16[8,48,1536]{2,1,0:T(8,128)(2,1)S(1)}, u32[]{:S(2)}, u32[]{:S(2)}) %all-to-all-start.2) | async-done | bytes 1179680 | tf_op jit(solution)/shard_map/all_to_all | solution.py:232
  268.3 1.2 fusion.18
  (136 shorter events, 18.0 us)
Async XLA Ops:
  7.2 21.8 %copy-start.19 = (s32[128,2]{0,1:T(2,128)S(1)}, s32[128,2]{0,1:T(2,128)}, u32[]{:S(2)}) copy-start(s32[128,2]{0,1:T(2,128)} %param.20) | copy-start | bytes 3076
  7.2 22.2 %copy-start.22 = (s32[1,128]{1,0:T(1,128)S(1)}, s32[1,128]{1,0:T(1,128)}, u32[]{:S(2)}) copy-start(s32[1,128]{1,0:T(1,128)} %param.25) | copy-start | bytes 1540
  7.2 23.3 %copy-start.4 = (bf16[1536,256]{1,0:T(8,128)(2,1)S(1)}, bf16[1536,256]{1,0:T(8,128)(2,1)}, u32[]{:S(2)}) copy-start(bf16[1536,256]{1,0:T(8,128)(2,1)} %param.22) | copy-start | bytes 2359300
  7.2 198.5 %all-gather.5.cloned.1.call-start = ((), (), s32[]{:S(2)}) async-start(), calls=%async_computation.4 | async-start | bytes 1966080 | tf_op jit(solution)/shard_map/all_gather | solution.py:194
  8.5 22.1 %copy-start.8 = (bf16[1536,64]{0,1:T(8,128)(2,1)S(1)}, bf16[1536,64]{0,1:T(8,128)(2,1)}, u32[]{:S(2)}) copy-start(bf16[1536,64]{0,1:T(8,128)(2,1)} %param.16) | copy-start | bytes 589828
  8.5 22.1 %copy-start.9 = (bf16[1536,64]{0,1:T(8,128)(2,1)S(1)}, bf16[1536,64]{0,1:T(8,128)(2,1)}, u32[]{:S(2)}) copy-start(bf16[1536,64]{0,1:T(8,128)(2,1)} %param.17) | copy-start | bytes 589828
  10.4 106.6 %collective-permute-start = (bf16[128,1536]{1,0:T(8,128)(2,1)}, bf16[128,1536]{1,0:T(8,128)(2,1)}, u32[]{:S(2)}, u32[]{:S(2)}) collective-permute-start(bf16[128,1536]{1,0:T(8,128)(2,1)} %fusion.30), channel_id=1, source_target_pairs={{0,6},{1,7},{2,0},{3,1},{4,2},{5,3},{6,4},{7,5},{8,14},{9,15},{10,... | collective-permute-start | bytes 1179656 | tf_op jit(solution)/shard_map/ppermute | solution.py:24
  15.1 104.1 %collective-permute-start.1 = (bf16[128,1536]{1,0:T(8,128)(2,1)}, bf16[128,1536]{1,0:T(8,128)(2,1)}, u32[]{:S(2)}, u32[]{:S(2)}) collective-permute-start(bf16[128,1536]{1,0:T(8,128)(2,1)} %fusion.30), channel_id=1, source_target_pairs={{0,4},{1,5},{2,6},{3,7},{4,0},{5,1},{6,2},{7,3},{8,12},{9,13},{10,... | collective-permute-start | bytes 1179656 | tf_op jit(solution)/shard_map/ppermute | solution.py:24
  17.8 16.5 %collective-permute-start.12 = (s32[128]{0:T(128)}, s32[128]{0:T(128)S(1)}, u32[]{:S(2)}, u32[]{:S(2)}) collective-permute-start(s32[128]{0:T(128)} %param.19), channel_id=1, source_target_pairs={{0,6},{1,7},{2,0},{3,1},{4,2},{5,3},{6,4},{7,5},{8,14},{9,15},{10,... | collective-permute-start | bytes 1544 | tf_op jit(solution)/shard_map/ppermute | solution.py:24
  20.9 15.9 %collective-permute-start.13 = (s32[128]{0:T(128)}, s32[128]{0:T(128)S(1)}, u32[]{:S(2)}, u32[]{:S(2)}) collective-permute-start(s32[128]{0:T(128)} %param.19), channel_id=1, source_target_pairs={{0,4},{1,5},{2,6},{3,7},{4,0},{5,1},{6,2},{7,3},{8,12},{9,13},{10,... | collective-permute-start | bytes 1544 | tf_op jit(solution)/shard_map/ppermute | solution.py:24
  24.6 27.9 %collective-permute-start.14 = (s32[128]{0:T(128)}, s32[128]{0:T(128)S(1)}, u32[]{:S(2)}, u32[]{:S(2)}) collective-permute-start(s32[128]{0:T(128)} %param.19), channel_id=1, source_target_pairs={{0,2},{1,3},{2,4},{3,5},{4,6},{5,7},{6,0},{7,1},{8,10},{9,11},{10,... | collective-permute-start | bytes 1544 | tf_op jit(solution)/shard_map/ppermute | solution.py:24
  27.7 3.6 %copy-start.7 = (bf16[64,1536]{1,0:T(8,128)(2,1)S(1)}, bf16[64,1536]{1,0:T(8,128)(2,1)}, u32[]{:S(2)}) copy-start(bf16[64,1536]{1,0:T(8,128)(2,1)} %param.18) | copy-start | bytes 589828
  31.4 21.1 %copy-start.21 = (s32[128]{0:T(128)S(1)}, s32[128]{0:T(128)}, u32[]{:S(2)}) copy-start(s32[128]{0:T(128)} %param.19) | copy-start | bytes 1540
  34.4 84.9 %collective-permute-start.2 = (bf16[128,1536]{1,0:T(8,128)(2,1)}, bf16[128,1536]{1,0:T(8,128)(2,1)}, u32[]{:S(2)}, u32[]{:S(2)}) collective-permute-start(bf16[128,1536]{1,0:T(8,128)(2,1)} %fusion.30), channel_id=1, source_target_pairs={{0,2},{1,3},{2,4},{3,5},{4,6},{5,7},{6,0},{7,1},{8,10},{9,11},{10,... | collective-permute-start | bytes 1179656 | tf_op jit(solution)/shard_map/ppermute | solution.py:24
  36.8 20.8 %collective-permute-start.3 = (bf16[48,1536]{1,0:T(8,128)(2,1)S(1)}, bf16[48,1536]{1,0:T(8,128)(2,1)S(1)}, u32[]{:S(2)}, u32[]{:S(2)}) collective-permute-start(bf16[48,1536]{1,0:T(8,128)(2,1)S(1)} %fusion.56), channel_id=1, source_target_pairs={{0,8},{1,9},{2,10},{3,11},{4,12},{5,13},{6,14},{7,15},{8,0},{9,1},... | collective-permute-start | bytes 442376 | tf_op jit(solution)/shard_map/ppermute | solution.py:24
  52.5 3.1 %collective-permute-start.15 = (s32[4,128]{1,0:T(4,128)S(1)}, s32[4,128]{1,0:T(4,128)S(1)}, u32[]{:S(2)}, u32[]{:S(2)}) collective-permute-start(s32[4,128]{1,0:T(4,128)S(1)} %get-tuple-element.17), channel_id=1, source_target_pairs={{0,1},{1,0},{2,3},{3,2},{4,5},{5,4},{6,7},{7,6},{8,9},{9,8},{10,11... | collective-permute-start | bytes 6152 | tf_op jit(solution)/shard_map/ppermute | solution.py:24
  55.6 27.2 %collective-permute-start.16 = (bf16[192,512]{1,0:T(8,128)(2,1)S(1)}, bf16[192,512]{1,0:T(8,128)(2,1)S(1)}, u32[]{:S(2)}, u32[]{:S(2)}) collective-permute-start(bf16[192,512]{1,0:T(8,128)(2,1)S(1)} %constant_dynamic-slice_fusion.1), channel_id=1, source_target_pairs={{0,8},{1,9},{2,10},{3,11},{4,12},{5,13},{6,14},{7,15},{8,0},{9,1},... | collective-permute-start | bytes 589832 | tf_op jit(solution)/shard_map/ppermute | solution.py:24
  57.6 9.7 %collective-permute-start.4 = (bf16[48,1536]{1,0:T(8,128)(2,1)S(1)}, bf16[48,1536]{1,0:T(8,128)(2,1)S(1)}, u32[]{:S(2)}, u32[]{:S(2)}) collective-permute-start(bf16[48,1536]{1,0:T(8,128)(2,1)S(1)} %collective-permute-done.3), channel_id=1, source_target_pairs={{0,384},{1,385},{2,386},{3,387},{4,388},{5,389},{6,390},{7,391},{8... | collective-permute-start | bytes 442376 | tf_op jit(solution)/shard_map/ppermute | solution.py:24
  67.3 17.5 %collective-permute-start.5 = (bf16[48,1536]{1,0:T(8,128)(2,1)S(1)}, bf16[48,1536]{1,0:T(8,128)(2,1)S(1)}, u32[]{:S(2)}, u32[]{:S(2)}) collective-permute-start(bf16[48,1536]{1,0:T(8,128)(2,1)S(1)} %collective-permute-done.3), channel_id=1, source_target_pairs={{0,256},{1,257},{2,258},{3,259},{4,260},{5,261},{6,262},{7,263},{8... | collective-permute-start | bytes 442376 | tf_op jit(solution)/shard_map/ppermute | solution.py:24
  82.8 16.4 %collective-permute-start.6 = (bf16[48,1536]{1,0:T(8,128)(2,1)S(1)}, bf16[48,1536]{1,0:T(8,128)(2,1)S(1)}, u32[]{:S(2)}, u32[]{:S(2)}) collective-permute-start(bf16[48,1536]{1,0:T(8,128)(2,1)S(1)} %collective-permute-done.3), channel_id=1, source_target_pairs={{0,128},{1,129},{2,130},{3,131},{4,132},{5,133},{6,134},{7,135},{8... | collective-permute-start | bytes 442376 | tf_op jit(solution)/shard_map/ppermute | solution.py:24
  84.8 11.5 %collective-permute-start.17 = (bf16[192,512]{1,0:T(8,128)(2,1)S(1)}, bf16[192,512]{1,0:T(8,128)(2,1)S(1)}, u32[]{:S(2)}, u32[]{:S(2)}) collective-permute-start(bf16[192,512]{1,0:T(8,128)(2,1)S(1)} %collective-permute-done.16), channel_id=1, source_target_pairs={{0,16},{1,17},{2,18},{3,19},{4,20},{5,21},{6,22},{7,23},{8,24},{9,... | collective-permute-start | bytes 589832 | tf_op jit(solution)/shard_map/ppermute | solution.py:24
  96.3 25.0 %collective-permute-start.7 = (bf16[128,1536]{1,0:T(8,128)(2,1)}, bf16[128,1536]{1,0:T(8,128)(2,1)}, u32[]{:S(2)}, u32[]{:S(2)}) collective-permute-start(bf16[128,1536]{1,0:T(8,128)(2,1)} %pad_maximum_fusion.2), channel_id=1, source_target_pairs={{0,1},{1,0},{2,3},{3,2},{4,5},{5,4},{6,7},{7,6},{8,9},{9,8},{10,11... | collective-permute-start | bytes 1179656 | tf_op jit(solution)/shard_map/ppermute | solution.py:24
  99.1 111.2 %all-gather.3.cloned.1.call-start = ((), (), s32[]{:S(2)}) async-start(), calls=%async_computation.3 | async-start | bytes 3538944 | tf_op jit(solution)/shard_map/all_gather | solution.py:177
  99.2 96.3 %collective-permute-start.18 = (bf16[32,1536]{1,0:T(8,128)(2,1)}, bf16[32,1536]{1,0:T(8,128)(2,1)}, u32[]{:S(2)}, u32[]{:S(2)}) collective-permute-start(bf16[32,1536]{1,0:T(8,128)(2,1)} %constant_dynamic-slice_fusion), channel_id=1, source_target_pairs={{0,8},{1,9},{2,10},{3,11},{4,12},{5,13},{6,14},{7,15},{8,0},{9,1},... | collective-permute-start | bytes 294920 | tf_op jit(solution)/shard_map/ppermute | solution.py:24
  117.1 5.9 %collective-permute-start.8 = (bf16[128,1536]{1,0:T(8,128)(2,1)}, bf16[128,1536]{1,0:T(8,128)(2,1)S(1)}, u32[]{:S(2)}, u32[]{:S(2)}) collective-permute-start(bf16[128,1536]{1,0:T(8,128)(2,1)} %slice.124), channel_id=1, source_target_pairs={{0,1},{1,0},{2,3},{3,2},{4,5},{5,4},{6,7},{7,6},{8,9},{9,8},{10,11... | collective-permute-start | bytes 1179656 | tf_op jit(solution)/shard_map/ppermute | solution.py:24
  123.7 3.4 %collective-permute-start.9 = (bf16[512,256]{0,1:T(8,128)(2,1)S(1)}, bf16[512,256]{0,1:T(8,128)(2,1)S(1)}, u32[]{:S(2)}, u32[]{:S(2)}) collective-permute-start(bf16[512,256]{0,1:T(8,128)(2,1)S(1)} %pad_maximum_fusion.5), channel_id=1, source_target_pairs={{0,1},{1,0},{2,3},{3,2},{4,5},{5,4},{6,7},{7,6},{8,9},{9,8},{10,11... | collective-permute-start | bytes 786440 | tf_op jit(solution)/shard_map/ppermute | solution.py:24
  130.4 0.6 copy-start.10
  130.4 0.7 copy-start.12
  131.2 22.6 %collective-permute-start.10 = (bf16[1024,128]{0,1:T(8,128)(2,1)S(1)}, bf16[1024,128]{0,1:T(8,128)(2,1)S(1)}, u32[]{:S(2)}, u32[]{:S(2)}) collective-permute-start(bf16[1024,128]{0,1:T(8,128)(2,1)S(1)} %get-tuple-element.13), channel_id=1, source_target_pairs={{0,8},{1,9},{2,10},{3,11},{4,12},{5,13},{6,14},{7,15},{8,0},{9,1},... | collective-permute-start | bytes 786440 | tf_op jit(solution)/shard_map/ppermute | solution.py:24
  153.7 18.9 %collective-permute-start.11 = (bf16[1024,128]{0,1:T(8,128)(2,1)S(1)}, bf16[1024,128]{0,1:T(8,128)(2,1)}, u32[]{:S(2)}, u32[]{:S(2)}) collective-permute-start(bf16[1024,128]{0,1:T(8,128)(2,1)S(1)} %collective-permute-done.10), channel_id=1, source_target_pairs={{0,16},{1,17},{2,18},{3,19},{4,20},{5,21},{6,22},{7,23},{16,32},{1... | collective-permute-start | bytes 786440 | tf_op jit(solution)/shard_map/ppermute | solution.py:24
  169.2 5.0 %copy-start.6 = (pred[512,1536]{1,0:T(8,128)(4,1)S(1)}, pred[512,1536]{1,0:T(8,128)(4,1)}, u32[]{:S(2)}) copy-start(pred[512,1536]{1,0:T(8,128)(4,1)} %fusion.8) | copy-start | bytes 2359300
  174.3 3.3 %copy-start.15 = (bf16[1024,64]{0,1:T(8,128)(2,1)}, bf16[1024,64]{0,1:T(8,128)(2,1)S(1)}, u32[]{:S(2)}) copy-start(bf16[1024,64]{0,1:T(8,128)(2,1)S(1)} %get-tuple-element.11) | copy-start | bytes 393220
  177.6 4.7 %copy-start.5 = (pred[512,1536]{1,0:T(8,128)(4,1)S(1)}, pred[512,1536]{1,0:T(8,128)(4,1)}, u32[]{:S(2)}) copy-start(pred[512,1536]{1,0:T(8,128)(4,1)} %compare_and_fusion) | copy-start | bytes 2359300
  182.3 3.4 %copy-start.11 = (bf16[1024,64]{0,1:T(8,128)(2,1)S(1)}, bf16[1024,64]{0,1:T(8,128)(2,1)}, u32[]{:S(2)}) copy-start(bf16[1024,64]{0,1:T(8,128)(2,1)} %copy-done.10) | copy-start | bytes 393220
  182.3 3.4 %copy-start.13 = (bf16[1024,64]{0,1:T(8,128)(2,1)S(1)}, bf16[1024,64]{0,1:T(8,128)(2,1)}, u32[]{:S(2)}) copy-start(bf16[1024,64]{0,1:T(8,128)(2,1)} %copy-done.12) | copy-start | bytes 393220
  182.3 3.4 %copy-start.14 = (bf16[1024,64]{0,1:T(8,128)(2,1)S(1)}, bf16[1024,64]{0,1:T(8,128)(2,1)}, u32[]{:S(2)}) copy-start(bf16[1024,64]{0,1:T(8,128)(2,1)} %get-tuple-element.10) | copy-start | bytes 393220
  182.3 3.4 %copy-start.16 = (bf16[1024,64]{0,1:T(8,128)(2,1)S(1)}, bf16[1024,64]{0,1:T(8,128)(2,1)}, u32[]{:S(2)}) copy-start(bf16[1024,64]{0,1:T(8,128)(2,1)} %copy-done.15) | copy-start | bytes 393220
  185.7 3.8 %copy-start.17 = (bf16[64,2,512]{2,0,1:T(8,128)(2,1)S(1)}, bf16[64,2,512]{2,0,1:T(8,128)(2,1)}, u32[]{:S(2)}) copy-start(bf16[64,2,512]{2,0,1:T(8,128)(2,1)} %fusion.23) | copy-start | bytes 393220
  190.5 14.9 %all-to-all-start = ((bf16[8,256,128]{2,1,0:T(8,128)(2,1)}), bf16[8,256,128]{2,1,0:T(8,128)(2,1)S(1)}, u32[]{:S(2)}, u32[]{:S(2)}) async-start(bf16[8,256,128]{2,1,0:T(8,128)(2,1)} %pad_maximum_fusion.1), calls=%async_computation | async-start | bytes 1048576 | tf_op jit(solution)/shard_map/all_to_all | solution.py:171
  195.5 23.4 %collective-permute-start.19 = (bf16[32,1536]{1,0:T(8,128)(2,1)}, bf16[32,1536]{1,0:T(8,128)(2,1)S(1)}, u32[]{:S(2)}, u32[]{:S(2)}) collective-permute-start(bf16[32,1536]{1,0:T(8,128)(2,1)} %collective-permute-done.18), channel_id=1, source_target_pairs={{0,16},{1,17},{2,18},{3,19},{4,20},{5,21},{6,22},{7,23},{8,24},{9,... | collective-permute-start | bytes 294920 | tf_op jit(solution)/shard_map/ppermute | solution.py:24
  205.6 4.8 %copy-start = (bf16[128,1536]{1,0:T(8,128)(2,1)S(1)}, bf16[128,1536]{1,0:T(8,128)(2,1)}, u32[]{:S(2)}) copy-start(bf16[128,1536]{1,0:T(8,128)(2,1)} %param.13) | copy-start | bytes 1179652
  208.4 29.0 %collective-permute-start.20 = (bf16[1536,512]{1,0:T(8,128)(2,1)}, bf16[1536,512]{1,0:T(8,128)(2,1)}, u32[]{:S(2)}, u32[]{:S(2)}) collective-permute-start(bf16[1536,512]{1,0:T(8,128)(2,1)} %broadcast_select_fusion), channel_id=1, source_target_pairs={{0,1},{1,0},{2,3},{3,2},{4,5},{5,4},{6,7},{7,6},{8,9},{9,8},{10,11... | collective-permute-start | bytes 4718600 | tf_op jit(solution)/shard_map/ppermute | solution.py:24
  210.4 2.6 copy-start.18
  214.6 22.8 %all-to-all-start.1 = ((bf16[8,48,1536]{2,1,0:T(8,128)(2,1)}), bf16[8,48,1536]{2,1,0:T(8,128)(2,1)}, u32[]{:S(2)}, u32[]{:S(2)}) async-start(bf16[8,48,1536]{2,1,0:T(8,128)(2,1)} %bitcast.44), calls=%async_computation.1 | async-start | bytes 2359296 | tf_op jit(solution)/shard_map/all_to_all | solution.py:221
  218.9 15.6 %copy-start.1 = (bf16[256,1536]{1,0:T(8,128)(2,1)S(1)}, bf16[256,1536]{1,0:T(8,128)(2,1)}, u32[]{:S(2)}) copy-start(bf16[256,1536]{1,0:T(8,128)(2,1)} %param.24) | copy-start | bytes 2359300
  235.5 7.3 %collective-permute-start.21 = (bf16[256,1536]{1,0:T(8,128)(2,1)}, bf16[256,1536]{1,0:T(8,128)(2,1)}, u32[]{:S(2)}, u32[]{:S(2)}) collective-permute-start(bf16[256,1536]{1,0:T(8,128)(2,1)} %broadcast_select_fusion.1), channel_id=1, source_target_pairs={{0,1},{1,0},{2,3},{3,2},{4,5},{5,4},{6,7},{7,6},{8,9},{9,8},{10,11... | collective-permute-start | bytes 2359304 | tf_op jit(solution)/shard_map/ppermute | solution.py:24
  237.4 2.7 copy-start.3
  240.1 2.2 copy-start.2
  245.5 4.9 %copy-start.20 = (f32[128,2]{0,1:T(2,128)S(1)}, f32[128,2]{0,1:T(2,128)}, u32[]{:S(2)}) copy-start(f32[128,2]{0,1:T(2,128)} %param.21) | copy-start | bytes 3076
  245.5 22.3 %all-to-all-start.2 = ((bf16[8,48,1536]{2,1,0:T(8,128)(2,1)}), bf16[8,48,1536]{2,1,0:T(8,128)(2,1)S(1)}, u32[]{:S(2)}, u32[]{:S(2)}) async-start(bf16[8,48,1536]{2,1,0:T(8,128)(2,1)} %bitcast.46), calls=%async_computation.2 | async-start | bytes 2359296 | tf_op jit(solution)/shard_map/all_to_all | solution.py:232
Sparse Core Ops, SparseCore 0:
  99.2 33.9 all-gather.4
  135.4 36.6 all-gather.2

commit v2 on v1

v2 whole, which is shorter than its diff:
```python
import functools

import jax
import jax.numpy as jnp
import numpy as np
from jax import lax
from jax.experimental import pallas as pl
from jax.experimental.pallas import tpu as pltpu
from jax.sharding import Mesh
from jax.sharding import PartitionSpec as P

AXES = ("y", "zl", "zh", "x", "c")
SIZES = (4, 8, 2, 4, 2)
ROW = ("x", "c")
PAGE = 16
CAP = 48
TOK = 128
WIDTH = 1536
ROWS = 8 * TOK
BF16 = jnp.bfloat16
F32 = jnp.float32
I32 = jnp.int32
VMEM = pl.BlockSpec(memory_space=pltpu.VMEM)
SMEM = pl.BlockSpec(memory_space=pltpu.SMEM)
MIB = 1 << 20


def permute(block, target):
    route = []
    for source in range(int(np.prod(SIZES))):
        place = dict(zip(AXES, (int(v) for v in np.unravel_index(source, SIZES))))
        goal = target(**place)
        if goal is not None:
            route.append((source, int(np.ravel_multi_index(goal, SIZES))))
    return lax.ppermute(block, AXES, route)


def swap_core(block):
    return permute(block, lambda y, zl, zh, x, c: (y, zl, zh, x, 1 - c))


def swap_half(block):
    return permute(block, lambda y, zl, zh, x, c: (y, zl, 1 - zh, x, c))


def swap_near(block):
    return permute(block, lambda y, zl, zh, x, c: (y, zl ^ 1, zh, x, c))


def next_group(block):
    def target(y, zl, zh, x, c):
        g = y * 8 + zl + 1
        return (g // 8, g % 8, zh, x, c) if zh == 0 and g < 32 else None

    return permute(block, target)


def ahead_x(block, step):
    return permute(block, lambda y, zl, zh, x, c: (y, zl, zh, (x - step) % 4, c))


def ahead_y(block, step):
    return permute(block, lambda y, zl, zh, x, c: ((y - step) % 4, zl, zh, x, c))


def after(value, *earlier):
    return lax.optimization_barrier((value,) + earlier)[0]


def call(kernel, outs, in_specs, scratch=(), flops=0, nbytes=0, limit=48):
    outs = [jax.ShapeDtypeStruct(shape, kind) for shape, kind in outs]
    return pl.pallas_call(
        kernel,
        out_shape=outs,
        in_specs=in_specs,
        out_specs=[VMEM] * len(outs),
        scratch_shapes=list(scratch),
        compiler_params=pltpu.CompilerParams(vmem_limit_bytes=limit * MIB),
        cost_estimate=pl.CostEstimate(flops=flops, bytes_accessed=nbytes, transcendentals=0),
    )


def dot_nt(left, right):
    return lax.dot_general(left, right, (((1,), (1,)), ((), ())), preferred_element_type=F32)


def dot_tn(left, right):
    return lax.dot_general(left, right, (((0,), (0,)), ((), ())), preferred_element_type=F32)


def column(lane_row):
    return jnp.transpose(jnp.broadcast_to(lane_row, (TOK, TOK)))


def rms(values, gain):
    inverse = lax.rsqrt(jnp.mean(values * values, axis=-1, keepdims=True) + 1e-05)
    return (values * inverse * gain).astype(BF16)


def norm_kernel(meta, tokens, gain, seg, out):
    out[:TOK] = rms(tokens[...].astype(F32), gain[...])
    own = meta[5] * TOK + lax.broadcasted_iota(I32, (1, TOK), 1)
    back = own - seg[...]
    row = lax.broadcasted_iota(I32, (16, TOK), 0)
    pieces = jnp.where(row == 0, back >> 5, jnp.where(row == 1, back & 31, 0))
    out[TOK:, :TOK] = pieces.astype(F32).astype(BF16)
    out[TOK:, TOK:] = jnp.zeros((16, WIDTH - TOK), BF16)


def project_kernel(meta, b0, b1, b2, b3, s0, s1, s2, s3, wq, wkv, wo, f0, f1, f2, f3,
                   q_out, kv_out, start_out, wo_out, far, cols):
    y, zh, x, c = meta[0], meta[2], meta[3], meta[4]
    for k, part in enumerate((f0, f1, f2, f3)):
        low = pl.multiple_of(lax.rem(y + k, 4) * 48, 16)
        far[pl.ds(low, 48), :] = part[...]
    cols[0:64] = wq[...]
    cols[64:128] = far[0:64]
    key_low = pl.multiple_of(128 + zh * 64, 64)
    value_low = pl.multiple_of(192 - zh * 64, 64)
    cols[pl.ds(key_low, 64), :] = wkv[...]
    cols[pl.ds(value_low, 64), :] = far[64:128]
    wo_out[0:64] = wo[...]
    wo_out[64:128] = far[128:192]
    for k in range(4):
        place = lax.rem(x + k, 4) * 2
        for block, core in (((b0, b1, b2, b3)[k], c), ((s0, s1, s2, s3)[k], 1 - c)):
            low = pl.multiple_of((place + core) * TOK, TOK)
            result = dot_nt(block[:TOK], cols[...]).astype(BF16)
            q_out[pl.ds(low, TOK), :] = result[:, :128]
            kv_out[pl.ds(low, TOK), :] = result[:, 128:]
            pieces = block[TOK:, :TOK].astype(F32)
            back = column(pieces[0:1] * 32.0 + pieces[1:2])
            own = (low + lax.broadcasted_iota(I32, (TOK, TOK), 0)).astype(F32)
            start_out[pl.ds(low, TOK), :] = own - back


def split_kv(kv):
    wide = kv[...].astype(F32)
    turned = pltpu.roll(wide, 64, 1)
    low = lax.broadcasted_iota(I32, wide.shape, 1) < 64
    return (
        jnp.where(low, wide, turned).astype(BF16),
        jnp.where(low, turned, wide).astype(BF16),
    )


STEP = 256


def own_kernel(q, kv, start, ids, sum_out, max_out, den_out, slots_out, keys, values):
    keys[...], values[...] = split_kv(kv)
    low_lane = lax.broadcasted_iota(I32, (STEP, 128), 1) < 64
    for block in range(ROWS // STEP):
        low = block * STEP
        span = low + STEP
        query = q[low:span]
        position = lax.broadcasted_iota(I32, (STEP, span), 1).astype(F32)
        own = (low + lax.broadcasted_iota(I32, (STEP, span), 0)).astype(F32)
        allowed = (position <= own) & (position >= start[low:span, 0:1])
        parts = []
        for head in range(2):
            kept = jnp.where(low_lane if head == 0 else ~low_lane, query, jnp.zeros_like(query))
            scores = jnp.where(allowed, dot_nt(kept, keys[:span]) * 0.125, -1e30)
            top = jnp.max(scores, axis=-1, keepdims=True)
            weights = jnp.exp(scores - top)
            den = jnp.sum(weights, axis=-1, keepdims=True)
            part = jnp.dot(weights.astype(BF16), values[:span], preferred_element_type=F32)
            parts.append((part, top, den))
        for out, one, two in zip((sum_out, max_out, den_out), *parts):
            out[low:span] = jnp.where(low_lane, one, two)
    choice = [ids[k : k + 1].astype(F32) for k in range(2)]
    down = [column(v) for v in choice]
    earlier = lax.broadcasted_iota(I32, (TOK, TOK), 0) < lax.broadcasted_iota(I32, (TOK, TOK), 1)
    result = []
    for k in range(2):
        same = sum((down[j] == choice[k]).astype(F32) for j in range(2))
        rank = jnp.sum(jnp.where(earlier, same, 0.0), axis=0, keepdims=True).astype(I32)
        expert = ids[k : k + 1]
        result.append(((expert & 3) * 2 + (expert >> 2)) * CAP + rank)
    row = lax.broadcasted_iota(I32, (8, TOK), 0)
    slots_out[...] = jnp.where(row == 0, result[0], result[1])


def before_kernel(meta, table, q, kv, partner, shifted, start, sums, maxes, dens,
                  out, keys, values, group):
    zh = meta[2]

    @pl.when(zh == 0)
    def _():
        keys[...], values[...] = split_kv(shifted)

    @pl.when(zh != 0)
    def _():
        keys[...], values[...] = split_kv(partner)

    low_lane = lax.broadcasted_iota(I32, (STEP, 128), 1) < 64
    for block in range(ROWS // STEP):
        low = block * STEP
        high = low + STEP
        span = ROWS - low
        query = q[low:high]
        position = (low - ROWS + lax.broadcasted_iota(I32, (STEP, span), 1)).astype(F32)
        allowed = position >= start[low:high, 0:1]
        parts = []
        for head in range(2):
            kept = jnp.where(low_lane if head == 0 else ~low_lane, query, jnp.zeros_like(query))
            scores = jnp.where(allowed, dot_nt(kept, keys[low:]) * 0.125, -1e30)
            first = maxes[low:high, head * 64 : head * 64 + 1]
            top = jnp.maximum(first, jnp.max(scores, axis=-1, keepdims=True))
            weights = jnp.exp(scores - top)
            scale = jnp.exp(first - top)
            den = jnp.sum(weights, axis=-1, keepdims=True)
            part = jnp.dot(weights.astype(BF16), values[low:], preferred_element_type=F32)
            parts.append((part, scale, den))
        part, scale, den = (jnp.where(low_lane, one, two) for one, two in zip(*parts))
        total = sums[low:high] * scale + part
        result = (total / (dens[low:high] * scale + den)).astype(BF16)
        for j in range(STEP // TOK):
            out[low // TOK + j, :TOK, :] = result[j * TOK : (j + 1) * TOK]
    group[pl.ds(pl.multiple_of(zh * ROWS, ROWS), ROWS), :] = kv[...]
    group[pl.ds(pl.multiple_of((1 - zh) * ROWS, ROWS), ROWS), :] = partner[...]

    def place(block, carry):
        page = table[0, block] - zh * 64

        @pl.when((page >= 0) & (page < 64))
        def _():
            low = pl.multiple_of(TOK + lax.rem(page, 8) * PAGE, PAGE)
            out[page // 8, pl.ds(low, PAGE), :] = group[
                pl.ds(pl.multiple_of(block * PAGE, PAGE), PAGE), :
            ]

        return carry

    lax.fori_loop(0, 128, place, 0)


def cache_kernel(joined, out):
    low = lax.broadcasted_iota(I32, (TOK, 128), 1) < 64
    for pair in range(4):
        one = joined[2 * pair, TOK:, :].astype(F32)
        two = joined[2 * pair + 1, TOK:, :].astype(F32)
        lanes = slice(pair * 128, pair * 128 + 128)
        out[:, lanes] = jnp.where(low, one, pltpu.roll(two, 64, 1)).astype(BF16)
        lanes = slice(512 + pair * 128, 640 + pair * 128)
        out[:, lanes] = jnp.where(low, pltpu.roll(one, 64, 1), two).astype(BF16)


def choose(slots, k):
    place = lax.broadcasted_iota(I32, (8 * CAP, TOK), 0)
    return place == slots[k : k + 1]


def mid_kernel(joined, wo_all, tokens, gain, slots, mid_out, send_out):
    heads = jnp.concatenate([joined[j, :TOK, :] for j in range(8)], axis=1)
    total = jnp.dot(heads, wo_all[...], preferred_element_type=F32)
    mid = (tokens[...].astype(F32) + total).astype(BF16)
    mid_out[...] = mid
    normed = rms(mid.astype(F32), gain[...])
    pick = (choose(slots, 0) | choose(slots, 1)).astype(F32).astype(BF16)
    send_out[...] = jnp.dot(pick, normed, preferred_element_type=F32).astype(BF16)


def expert_kernel(arrived, kept, given, out):
    acts = []
    for half in (kept, given):
        both = jnp.dot(arrived[...], half[:WIDTH], preferred_element_type=F32)
        gate, up = both[:, :256], both[:, 256:]
        acts.append((gate / (1.0 + jnp.exp(-gate)) * up).astype(BF16))
    for chunk in range(3):
        rows = slice(WIDTH + chunk * 256, WIDTH + chunk * 256 + 256)
        total = jnp.dot(acts[0], kept[rows], preferred_element_type=F32)
        total += jnp.dot(acts[1], given[rows], preferred_element_type=F32)
        out[:, chunk * 512 : chunk * 512 + 512] = total.astype(BF16)


def combine_kernel(returned, mid, slots, weights, out):
    total = mid[...].astype(F32)
    for k in range(2):
        pick = choose(slots, k).astype(F32).astype(BF16)
        chosen = dot_tn(pick, returned[...])
        total += chosen * column(weights[k : k + 1])[:, 0:1]
    out[...] = total.astype(BF16)


def body(
    tokens,
    attn_gain,
    ffn_gain,
    w_query,
    key_value_weight,
    w_out,
    segment_ids,
    expert_ids,
    route_weights,
    w_gate,
    w_up,
    w_down,
    page_table,
):
    y, zl, zh, x, c = (lax.axis_index(name) for name in AXES)
    place = (((y * 8 + zl) * 2 + zh) * 4 + x) * 2 + c
    meta = jnp.stack([y, zl, zh, x, c, place]).astype(I32)
    wq, wkv = w_query.T, key_value_weight.T

    own_pack = jnp.concatenate([wq, wkv, w_out], axis=0)
    far = [swap_half(lax.dynamic_slice_in_dim(own_pack, y * 48, 48, 0))]
    (block,) = call(
        norm_kernel, [((TOK + 16, WIDTH), BF16)], [SMEM, VMEM, VMEM, VMEM], nbytes=800000
    )(meta, tokens, attn_gain[None, :], segment_ids[None, :])
    near = [block] + [ahead_x(block, step) for step in (1, 3, 2)]
    far += [ahead_y(far[0], step) for step in (1, 3, 2)]
    across = [swap_core(part) for part in near]
    order = (0, 1, 3, 2)
    q, kv, start, out_rows = call(
        project_kernel,
        [((ROWS, 128), BF16), ((ROWS, 128), BF16), ((ROWS, 128), F32), ((128, WIDTH), BF16)],
        [SMEM] + [VMEM] * 15,
        scratch=[pltpu.VMEM((192, WIDTH), BF16), pltpu.VMEM((256, WIDTH), BF16)],
        flops=2 * ROWS * WIDTH * 256,
        nbytes=5000000,
    )(
        meta,
        *[near[i] for i in order],
        *[across[i] for i in order],
        wq,
        wkv,
        w_out,
        *[far[i] for i in order],
    )
    out_all = lax.all_gather(out_rows, ROW, axis=0, tiled=True)

    partner = swap_half(kv)
    shifted = next_group(partner)
    sums, maxes, dens, slots = call(
        own_kernel,
        [((ROWS, 128), F32)] * 3 + [((8, TOK), I32)],
        [VMEM] * 4,
        scratch=[pltpu.VMEM((ROWS, 128), BF16)] * 2,
        flops=1000000000,
        nbytes=3000000,
    )(q, kv, start, expert_ids.T)
    (joined,) = call(
        before_kernel,
        [((8, 2 * TOK, 128), BF16)],
        [SMEM, SMEM] + [VMEM] * 8,
        scratch=[pltpu.VMEM((ROWS, 128), BF16)] * 2 + [pltpu.VMEM((2 * ROWS, 128), BF16)],
        flops=1000000000,
        nbytes=3000000,
    )(meta, page_table, q, kv, partner, shifted, start, sums, maxes, dens)
    joined = lax.all_to_all(joined, ROW, split_axis=0, concat_axis=0, tiled=True)

    mid, send = call(
        mid_kernel,
        [((TOK, WIDTH), BF16), ((8 * CAP, WIDTH), BF16)],
        [VMEM] * 5,
        flops=600000000,
        nbytes=5000000,
    )(joined, out_all, tokens, ffn_gain[None, :], slots)
    arrived = lax.all_to_all(
        send.reshape(8, CAP, WIDTH), ROW, split_axis=0, concat_axis=0, tiled=True
    ).reshape(8 * CAP, WIDTH)
    (cache,) = call(cache_kernel, [((TOK, 1024), BF16)], [VMEM], nbytes=800000)(joined)

    w_gate, w_up, w_down = (after(w, block) for w in (w_gate, w_up, w_down))
    own = jnp.concatenate(
        [jnp.concatenate([w_gate, w_up], axis=1)] + [w_down[:, i : i + 512] for i in (0, 512, 1024)],
        axis=0,
    )
    eighth = lax.dynamic_slice_in_dim(own, (y * 2 + zl % 2) * 288, 288, 0)
    eighth = swap_half(after(eighth, far[0]))
    beside = swap_near(eighth)
    pair = jnp.where(
        zl % 2 == 0,
        jnp.concatenate([eighth, beside], axis=0),
        jnp.concatenate([beside, eighth], axis=0),
    )
    other = lax.all_gather(pair, "y", axis=0, tiled=True)
    mine = c == zh
    kept = jnp.where(mine, own, other)
    given = swap_core(jnp.where(mine, other, own))
    (expert_out,) = call(
        expert_kernel,
        [((8 * CAP, WIDTH), BF16)],
        [VMEM] * 3,
        flops=1800000000,
        nbytes=7000000,
    )(arrived, kept, given)
    returned = lax.all_to_all(
        expert_out.reshape(8, CAP, WIDTH), ROW, split_axis=0, concat_axis=0, tiled=True
    ).reshape(8 * CAP, WIDTH)
    (hidden,) = call(
        combine_kernel, [((TOK, WIDTH), BF16)], [VMEM] * 4, flops=300000000, nbytes=2000000
    )(returned, mid, slots, route_weights.T)
    return (hidden, cache.reshape(8, PAGE, 1024))


def solution(mesh):
    fine = Mesh(mesh.devices.reshape(SIZES), AXES)
    grp, tp = ("y", "zl"), ("zh", "x", "c")
    in_specs = (
        P(AXES, None),
        P(),
        P(),
        P(None, tp),
        P(None, tp),
        P(tp, None),
        P(AXES),
        P(AXES, None),
        P(AXES, None),
        P(None, tp),
        P(None, tp),
        P(tp, None),
        P(grp, None),
    )
    out_specs = (P(AXES, None), P(AXES, None, None))
    return jax.shard_map(body, mesh=fine, in_specs=in_specs, out_specs=out_specs, check_vma=False)
```

time: 279 us -> 284 us (1.018)
  waiting for transfers between devices: 65.5 us -> 137 us
  matrix products: 32.5 us -> 0 us
  starting transfers between devices: 110 us -> 79.2 us
  Pallas kernels: 0 us -> 22.5 us
  blocking collectives: 14.5 us -> 0 us
  other arithmetic: 21.8 us -> 16.6 us
  local copies, waits for them, and re-layouts: 17 us -> 13.1 us
    ppermute x22 -> x16, waiting for transfers between devices: 44.8 us -> 93.4 us  [permute(): return lax.ppermute(block, AXES, route)]
    ppermute x22 -> x16, starting transfers between devices: 96.1 us -> 67.1 us  [permute(): return lax.ppermute(block, AXES, route)]
    dot_general x14 -> x0, matrix products: 25.8 us -> none  [the longest x2 8.46 us: attend(): jnp.einsum('hqk,kd->qhd', weights, values, preferred_element_type=jnp.flo...]
    pallas_call x0 -> x8, Pallas kernels: none -> 22.5 us  [the longest x1 7.42 us: body(): call(before_kernel, [((8, 2 * TOK, 128), BF16)], [SMEM, SMEM] + [VMEM] *...]
    all_to_all x2, waiting for transfers between devices: 15.4 us -> 33.7 us  [the longest x1 17.3 us: body(): lax.all_to_all(send.reshape(8, CAP, WIDTH), ROW, split_axis=0, concat_axi...]
    all_gather x1 -> x0, blocking collectives: 14.5 us -> none  [far_weight(): return lax.all_gather(pair, 'y', axis=0, tiled=True)]
    sub x2 -> x0, matrix products: 6.67 us -> none  [attend(): exponent = jnp.exp(scores - jnp.max(scores, axis=-1, keepdims=True))]
    concatenate x8 -> x2, other arithmetic: 3.55 us -> 9.3 us  [the longest x1 8.22 us: body(): jnp.concatenate([jnp.concatenate([w_gate, w_up], axis=1)] + [w_down[:, i:...]
  transfers between devices with their start and end apart: 27 -> 21, of which waited for: 9 -> 10; matrix products, arithmetic and copies ran while one was open for 23% -> 6% of each run, Pallas kernels for 0% -> 6%
where the time goes in v2:
time: 284 us; the launch traced here: 283 us
  waiting for transfers between devices  137 us (48%)
  starting transfers between devices  79.2 us (28%)
  Pallas kernels  22.5 us (8%)
  other arithmetic  16.6 us (6%)
  between operations  14.5 us (5%)
  local copies, waits for them, and re-layouts  13.1 us (5%)
    ppermute x16, waiting for transfers between devices, permute(): return lax.ppermute(block, AXES, route)  93.4 us
    ppermute x16, starting transfers between devices, permute(): return lax.ppermute(block, AXES, route)  67.1 us
    all_to_all x1, waiting for transfers between devices, body(): lax.all_to_all(send.reshape(8, CAP, WIDTH), ROW, split_axis=0, concat_axi...  17.3 us
    all_to_all x1, waiting for transfers between devices, body(): lax.all_to_all(expert_out.reshape(8, CAP, WIDTH), ROW, split_axis=0, conc...  16.4 us
    all_to_all x1, waiting for transfers between devices, body(): lax.all_to_all(joined, ROW, split_axis=0, concat_axis=0, tiled=True)  10.3 us
    unnamed x56, local copies, waits for them, and re-layouts  10.1 us
    concatenate x1, other arithmetic, body(): jnp.concatenate([jnp.concatenate([w_gate, w_up], axis=1)] + [w_down[:, i:...  8.22 us
    pallas_call x1, Pallas kernels, body(): call(before_kernel, [((8, 2 * TOK, 128), BF16)], [SMEM, SMEM] + [VMEM] *...  7.42 us
  transfers between devices with their start and end apart: 21, of which 10 were waited for; matrix products, arithmetic and copies ran while one was open for 6% of the time, Pallas kernels for 6%

profile of v2, /device:TPU:24, one launch (start us, length us, event | category | flops | bytes accessed | tf_op | source)
XLA Modules:
  0.0 283.4 jit_solution(6022357157547494187)
XLA Ops:
  7.2 0.0 copy-start.22
  7.2 0.0 all-gather.5.cloned.1.call-start
  7.2 1.1 fusion.1
  8.3 15.7 %collective-permute-start.7 = (bf16[48,1536]{1,0:T(8,128)(2,1)S(1)}, bf16[48,1536]{1,0:T(8,128)(2,1)S(1)}, u32[]{:S(2)}, u32[]{:S(2)}) collective-permute-start(bf16[48,1536]{1,0:T(8,128)(2,1)S(1)} %fusion.1), channel_id=1, source_target_pairs={{0,8},{1,9},{2,10},{3,11},{4,12},{5,13},{6,14},{7,15},{8,0},{9,1},... | collective-permute-start | bytes 442376 | tf_op jit(solution)/shard_map/ppermute | solution.py:35
  24.1 0.7 broadcast_in_dim.9.gain
  24.8 0.1 stack.27.meta
  24.8 1.0 copy-done.4
  25.8 0.7 copy-done.14
  26.5 0.7 shard_map.140.b0
  27.2 1.2 fusion.2
  28.4 0.7 copy-done.26
  29.1 8.2 %pad_maximum_fusion = bf16[2304,512]{1,0:T(8,128)(2,1)} fusion(bf16[256,512]{1,0:T(8,128)(2,1)S(1)} %get-tuple-element.33, bf16[256,512]{1,0:T(8,128)(2,1)S(1)} %get-tuple-element.34, bf16[256,512]{1,0:T(8,128)(2,1)S(1)} %get-tuple-element.32, bf16[1536,256]{1,0:T(8,128)(2,1)S(1)} %copy-done.22, bf16[1536,256]{1,0:T(8,128)(2,1)S(1)} %copy-done.23), kind=kLoop, calls=%fused_computation | loop fusion | flops 11796480 | bytes 4718592 | tf_op jit(solution)/shard_map/concatenate | solution.py:366
  37.4 0.0 copy-start.9
  37.4 1.0 constant_dynamic-slice_fusion
  38.5 2.1 collective-permute-start.13
  40.5 32.8 %collective-permute-done.13 = bf16[288,512]{1,0:T(8,128)(2,1)S(1)} collective-permute-done((bf16[288,512]{1,0:T(8,128)(2,1)S(1)}, bf16[288,512]{1,0:T(8,128)(2,1)S(1)}, u32[]{:S(2)}, u32[]{:S(2)}) %collective-permute-start.13) | collective-permute-done | bytes 294944 | tf_op jit(solution)/shard_map/ppermute | solution.py:35
  73.3 6.2 %collective-permute-start.14 = (bf16[288,512]{1,0:T(8,128)(2,1)S(1)}, bf16[288,512]{1,0:T(8,128)(2,1)S(1)}, u32[]{:S(2)}, u32[]{:S(2)}) collective-permute-start(bf16[288,512]{1,0:T(8,128)(2,1)S(1)} %collective-permute-done.13), channel_id=1, source_target_pairs={{0,16},{1,17},{2,18},{3,19},{4,20},{5,21},{6,22},{7,23},{8,24},{9,... | collective-permute-start | bytes 884744 | tf_op jit(solution)/shard_map/ppermute | solution.py:35
  79.6 5.3 %collective-permute-done.14 = bf16[288,512]{1,0:T(8,128)(2,1)S(1)} collective-permute-done((bf16[288,512]{1,0:T(8,128)(2,1)S(1)}, bf16[288,512]{1,0:T(8,128)(2,1)S(1)}, u32[]{:S(2)}, u32[]{:S(2)}) %collective-permute-start.14) | collective-permute-done | bytes 294944 | tf_op jit(solution)/shard_map/ppermute | solution.py:35
  84.9 1.0 maximum_select_fusion
  85.9 0.0 all-gather.5.cloned.1.call-update
  86.0 0.0 all-gather.3.cloned.1.call-start
  86.0 3.4 %collective-permute-start.2 = (bf16[144,1536]{1,0:T(8,128)(2,1)S(1)}, bf16[144,1536]{1,0:T(8,128)(2,1)S(1)}, u32[]{:S(2)}, u32[]{:S(2)}) collective-permute-start(bf16[144,1536]{1,0:T(8,128)(2,1)S(1)} %shard_map.140.b0), channel_id=1, source_target_pairs={{0,2},{1,3},{2,4},{3,5},{4,6},{5,7},{6,0},{7,1},{8,10},{9,11},{10,... | collective-permute-start | bytes 1327112 | tf_op jit(solution)/shard_map/ppermute | solution.py:35
  89.4 4.6 %collective-permute-start.1 = (bf16[144,1536]{1,0:T(8,128)(2,1)S(1)}, bf16[144,1536]{1,0:T(8,128)(2,1)S(1)}, u32[]{:S(2)}, u32[]{:S(2)}) collective-permute-start(bf16[144,1536]{1,0:T(8,128)(2,1)S(1)} %shard_map.140.b0), channel_id=1, source_target_pairs={{0,4},{1,5},{2,6},{3,7},{4,0},{5,1},{6,2},{7,3},{8,12},{9,13},{10,... | collective-permute-start | bytes 1327112 | tf_op jit(solution)/shard_map/ppermute | solution.py:35
  94.1 3.3 %collective-permute-start = (bf16[144,1536]{1,0:T(8,128)(2,1)S(1)}, bf16[144,1536]{1,0:T(8,128)(2,1)S(1)}, u32[]{:S(2)}, u32[]{:S(2)}) collective-permute-start(bf16[144,1536]{1,0:T(8,128)(2,1)S(1)} %shard_map.140.b0), channel_id=1, source_target_pairs={{0,6},{1,7},{2,0},{3,1},{4,2},{5,3},{6,4},{7,5},{8,14},{9,15},{10,... | collective-permute-start | bytes 1327112 | tf_op jit(solution)/shard_map/ppermute | solution.py:35
  97.4 1.9 collective-permute-start.3
  99.3 2.1 collective-permute-start.10
  101.5 0.0 collective-permute-done.2.b3
  101.5 2.2 collective-permute-start.6
  103.7 5.5 %collective-permute-done.1.b2 = bf16[144,1536]{1,0:T(8,128)(2,1)S(1)} collective-permute-done((bf16[144,1536]{1,0:T(8,128)(2,1)S(1)}, bf16[144,1536]{1,0:T(8,128)(2,1)S(1)}, u32[]{:S(2)}, u32[]{:S(2)}) %collective-permute-start.1) | collective-permute-done | bytes 442400 | tf_op jit(solution)/shard_map/ppermute | solution.py:35
  109.2 1.9 collective-permute-start.5
  111.1 2.4 collective-permute-start.4
  113.5 3.1 %collective-permute-start.9 = (bf16[48,1536]{1,0:T(8,128)(2,1)S(1)}, bf16[48,1536]{1,0:T(8,128)(2,1)S(1)}, u32[]{:S(2)}, u32[]{:S(2)}) collective-permute-start(bf16[48,1536]{1,0:T(8,128)(2,1)S(1)} %collective-permute-done.7.f0), channel_id=1, source_target_pairs={{0,256},{1,257},{2,258},{3,259},{4,260},{5,261},{6,262},{7,263},{8... | collective-permute-start | bytes 442376 | tf_op jit(solution)/shard_map/ppermute | solution.py:35
  116.7 8.8 %collective-permute-done.9.f2 = bf16[48,1536]{1,0:T(8,128)(2,1)S(1)} collective-permute-done((bf16[48,1536]{1,0:T(8,128)(2,1)S(1)}, bf16[48,1536]{1,0:T(8,128)(2,1)S(1)}, u32[]{:S(2)}, u32[]{:S(2)}) %collective-permute-start.9) | collective-permute-done | bytes 147488 | tf_op jit(solution)/shard_map/ppermute | solution.py:35
  125.5 3.6 %collective-permute-start.8 = (bf16[48,1536]{1,0:T(8,128)(2,1)S(1)}, bf16[48,1536]{1,0:T(8,128)(2,1)S(1)}, u32[]{:S(2)}, u32[]{:S(2)}) collective-permute-start(bf16[48,1536]{1,0:T(8,128)(2,1)S(1)} %collective-permute-done.7.f0), channel_id=1, source_target_pairs={{0,384},{1,385},{2,386},{3,387},{4,388},{5,389},{6,390},{7,391},{8... | collective-permute-start | bytes 442376 | tf_op jit(solution)/shard_map/ppermute | solution.py:35
  129.1 4.7 %collective-permute-done.8.f1 = bf16[48,1536]{1,0:T(8,128)(2,1)S(1)} collective-permute-done((bf16[48,1536]{1,0:T(8,128)(2,1)S(1)}, bf16[48,1536]{1,0:T(8,128)(2,1)S(1)}, u32[]{:S(2)}, u32[]{:S(2)}) %collective-permute-start.8) | collective-permute-done | bytes 147488 | tf_op jit(solution)/shard_map/ppermute | solution.py:35
  133.8 3.5 %shard_map.141 = (bf16[1024,128]{1,0:T(8,128)(2,1)S(1)}, bf16[1024,128]{1,0:T(8,128)(2,1)S(1)}, f32[1024,128]{1,0:T(8,128)S(1)}, bf16[128,1536]{1,0:T(8,128)(2,1)}) custom-call(s32[6]{0:T(128)S(1)} %stack.27.meta, bf16[144,1536]{1,0:T(8,128)(2,1)S(1)} %shard_map.140.b0, bf16[144,1536]{1,0:T(8,128)(2,1)S(1)} %collective-permute-done.b1, ...), custom_call_target="tpu_custom_call" | custom-call | flops 805306368 | bytes 5000000 | tf_op jit(solution)/shard_map/pallas_call | solution.py:315
  137.3 0.0 all-gather.3.cloned.1.call-update
  137.3 0.0 copy-start.20
  137.3 0.0 all-gather.5.cloned.1.call-done
  137.4 6.3 %broadcast_select_fusion = (bf16[2304,512]{1,0:T(8,128)(2,1)}, bf16[2304,512]{1,0:T(8,128)(2,1)S(1)}) fusion(bf16[2304,512]{1,0:T(8,128)(2,1)} %all-gather.5.cloned.1.call-done, pred[]{:T(512)S(6)} %eq.9, bf16[256,512]{1,0:T(8,128)(2,1)} %copy-done.25, bf16[256,512]{1,0:T(8,128)(2,1)} %copy-done.26, bf16[256,512]{1,0:T(8,128)(2,1)} %copy-done.24, ...), kind=kLoop, calls=%fused_computation.1 | loop fusion | flops 14155776 | bytes 9437185 | tf_op jit(solution)/shard_map/jit(_where)/select_n | solution.py:381
  143.7 2.0 collective-permute-start.15
  145.7 10.3 %collective-permute-start.11 = (bf16[1024,128]{1,0:T(8,128)(2,1)S(1)}, bf16[1024,128]{1,0:T(8,128)(2,1)S(1)}, u32[]{:S(2)}, u32[]{:S(2)}) collective-permute-start(bf16[1024,128]{1,0:T(8,128)(2,1)S(1)} %get-tuple-element.17.kv), channel_id=1, source_target_pairs={{0,8},{1,9},{2,10},{3,11},{4,12},{5,13},{6,14},{7,15},{8,0},{9,1},... | collective-permute-start | bytes 786440 | tf_op jit(solution)/shard_map/ppermute | solution.py:35
  156.0 25.9 %collective-permute-done.11.partner = bf16[1024,128]{1,0:T(8,128)(2,1)S(1)} collective-permute-done((bf16[1024,128]{1,0:T(8,128)(2,1)S(1)}, bf16[1024,128]{1,0:T(8,128)(2,1)S(1)}, u32[]{:S(2)}, u32[]{:S(2)}) %collective-permute-start.11) | collective-permute-done | bytes 262176 | tf_op jit(solution)/shard_map/ppermute | solution.py:35
  182.0 2.1 collective-permute-start.12
  184.1 0.9 copy-done.18
  185.0 3.8 %shard_map.142 = (f32[1024,128]{1,0:T(8,128)S(1)}, f32[1024,128]{1,0:T(8,128)S(1)}, f32[1024,128]{1,0:T(8,128)S(1)}, s32[8,128]{1,0:T(8,128)S(1)}) custom-call(bf16[1024,128]{1,0:T(8,128)(2,1)S(1)} %get-tuple-element.16.q, bf16[1024,128]{1,0:T(8,128)(2,1)S(1)} %copy-done.18, f32[1024,128]{1,0:T(8,128)S(1)} %get-tuple-element.18.start, s32[2,128]{1,0:T(2,128)S(1)} %bitcast.26), custom_call_target="tpu_custom_call" | custom-call | flops 1000000000 | bytes 3000000 | tf_op jit(solution)/shard_map/pallas_call | solution.py:335
  188.8 10.3 %collective-permute-done.12.shifted = bf16[1024,128]{1,0:T(8,128)(2,1)S(1)} collective-permute-done((bf16[1024,128]{1,0:T(8,128)(2,1)S(1)}, bf16[1024,128]{1,0:T(8,128)(2,1)S(1)}, u32[]{:S(2)}, u32[]{:S(2)}) %collective-permute-start.12) | collective-permute-done | bytes 262176 | tf_op jit(solution)/shard_map/ppermute | solution.py:35
  199.1 0.9 copy-done.16
  200.0 7.4 %shard_map.143 = bf16[8,256,128]{2,1,0:T(8,128)(2,1)S(1)} custom-call(s32[6]{0:T(128)S(1)} %stack.27.meta, s32[1,128]{1,0:T(1,128)S(1)} %copy-done.21, bf16[1024,128]{1,0:T(8,128)(2,1)S(1)} %copy-done.16, bf16[1024,128]{1,0:T(8,128)(2,1)S(1)} %copy-done.19, bf16[1024,128]{1,0:T(8,128)(2,1)S(1)} %collective-permute-done.11.partner, ...), custom_call_target="tpu_custom_call" | custom-call | flops 1000000000 | bytes 3000000 | tf_op jit(solution)/shard_map/pallas_call | solution.py:343
  207.5 0.9 copy-done.10
  208.3 4.8 %all-to-all-start = ((bf16[8,256,128]{2,1,0:T(8,128)(2,1)}), bf16[8,256,128]{2,1,0:T(8,128)(2,1)S(1)}, u32[]{:S(2)}, u32[]{:S(2)}) async-start(bf16[8,256,128]{2,1,0:T(8,128)(2,1)} %copy-done.10), calls=%async_computation | async-start | bytes 1048576 | tf_op jit(solution)/shard_map/all_to_all | solution.py:351
  213.2 10.3 %all-to-all-done.joined = bf16[8,256,128]{2,1,0:T(8,128)(2,1)S(1)} async-done(((bf16[8,256,128]{2,1,0:T(8,128)(2,1)}), bf16[8,256,128]{2,1,0:T(8,128)(2,1)S(1)}, u32[]{:S(2)}, u32[]{:S(2)}) %all-to-all-start) | async-done | bytes 524320 | tf_op jit(solution)/shard_map/all_to_all | solution.py:351
  223.5 2.1 copy-done.3
  225.6 1.1 shard_map.144
  226.8 1.0 copy-done.6
  227.8 0.7 copy-done.11
  228.6 3.6 %all-to-all-start.1 = ((bf16[8,48,1536]{2,1,0:T(8,128)(2,1)}), bf16[8,48,1536]{2,1,0:T(8,128)(2,1)S(1)}, u32[]{:S(2)}, u32[]{:S(2)}) async-start(bf16[8,48,1536]{2,1,0:T(8,128)(2,1)} %bitcast.19), calls=%async_computation.1 | async-start | bytes 2359296 | tf_op jit(solution)/shard_map/all_to_all | solution.py:360
  232.1 17.3 %all-to-all-done.1 = bf16[8,48,1536]{2,1,0:T(8,128)(2,1)S(1)} async-done(((bf16[8,48,1536]{2,1,0:T(8,128)(2,1)}), bf16[8,48,1536]{2,1,0:T(8,128)(2,1)S(1)}, u32[]{:S(2)}, u32[]{:S(2)}) %all-to-all-start.1) | async-done | bytes 1179680 | tf_op jit(solution)/shard_map/all_to_all | solution.py:360
  249.4 3.7 %shard_map.145 = bf16[384,1536]{1,0:T(8,128)(2,1)S(1)} custom-call(bf16[384,1536]{1,0:T(8,128)(2,1)S(1)} %bitcast.16, bf16[2304,512]{1,0:T(8,128)(2,1)S(1)} %get-tuple-element.31.kept, bf16[2304,512]{1,0:T(8,128)(2,1)} %collective-permute-done.15.given), custom_call_target="tpu_custom_call" | custom-call | flops 1800000000 | bytes 7000000 | tf_op jit(solution)/shard_map/pallas_call | solution.py:382
  253.2 1.0 copy-done
  254.2 3.7 %all-to-all-start.2 = ((bf16[8,48,1536]{2,1,0:T(8,128)(2,1)}), bf16[8,48,1536]{2,1,0:T(8,128)(2,1)S(1)}, u32[]{:S(2)}, u32[]{:S(2)}) async-start(bf16[8,48,1536]{2,1,0:T(8,128)(2,1)} %bitcast.17), calls=%async_computation.2 | async-start | bytes 2359296 | tf_op jit(solution)/shard_map/all_to_all | solution.py:389
  257.9 0.9 shard_map.147
  258.8 16.4 %all-to-all-done.2 = bf16[8,48,1536]{2,1,0:T(8,128)(2,1)S(1)} async-done(((bf16[8,48,1536]{2,1,0:T(8,128)(2,1)}), bf16[8,48,1536]{2,1,0:T(8,128)(2,1)S(1)}, u32[]{:S(2)}, u32[]{:S(2)}) %all-to-all-start.2) | async-done | bytes 1179680 | tf_op jit(solution)/shard_map/all_to_all | solution.py:389
  275.2 1.4 shard_map.146
  (53 shorter events, 0.1 us)
Async XLA Ops:
  7.2 22.0 %copy-start.22 = (bf16[1536,256]{1,0:T(8,128)(2,1)S(1)}, bf16[1536,256]{1,0:T(8,128)(2,1)}, u32[]{:S(2)}) copy-start(bf16[1536,256]{1,0:T(8,128)(2,1)} %param.23) | copy-start | bytes 2359300
  7.2 130.2 %all-gather.5.cloned.1.call-start = ((), (), s32[]{:S(2)}) async-start(), calls=%async_computation.4 | async-start | bytes 2949120 | tf_op jit(solution)/shard_map/all_gather | solution.py:378
  8.3 30.1 %collective-permute-start.7 = (bf16[48,1536]{1,0:T(8,128)(2,1)S(1)}, bf16[48,1536]{1,0:T(8,128)(2,1)S(1)}, u32[]{:S(2)}, u32[]{:S(2)}) collective-permute-start(bf16[48,1536]{1,0:T(8,128)(2,1)S(1)} %fusion.1), channel_id=1, source_target_pairs={{0,8},{1,9},{2,10},{3,11},{4,12},{5,13},{6,14},{7,15},{8,0},{9,1},... | collective-permute-start | bytes 442376 | tf_op jit(solution)/shard_map/ppermute | solution.py:35
  24.8 1.0 copy-start.4
  25.8 0.7 copy-start.14
  26.5 2.6 copy-start.23
  28.4 0.7 copy-start.26
  28.4 8.9 %copy-start.24 = (bf16[256,512]{1,0:T(8,128)(2,1)}, bf16[256,512]{1,0:T(8,128)(2,1)S(1)}, u32[]{:S(2)}) copy-start(bf16[256,512]{1,0:T(8,128)(2,1)S(1)} %get-tuple-element.32) | copy-start | bytes 786436
  28.4 8.9 %copy-start.25 = (bf16[256,512]{1,0:T(8,128)(2,1)}, bf16[256,512]{1,0:T(8,128)(2,1)S(1)}, u32[]{:S(2)}) copy-start(bf16[256,512]{1,0:T(8,128)(2,1)S(1)} %get-tuple-element.33) | copy-start | bytes 786436
  37.4 96.5 %copy-start.7 = (bf16[1536,64]{0,1:T(8,128)(2,1)S(1)}, bf16[1536,64]{0,1:T(8,128)(2,1)}, u32[]{:S(2)}) copy-start(bf16[1536,64]{0,1:T(8,128)(2,1)} %param.16) | copy-start | bytes 589828
  37.4 96.5 %copy-start.8 = (bf16[1536,64]{0,1:T(8,128)(2,1)S(1)}, bf16[1536,64]{0,1:T(8,128)(2,1)}, u32[]{:S(2)}) copy-start(bf16[1536,64]{0,1:T(8,128)(2,1)} %param.17) | copy-start | bytes 589828
  37.4 96.5 %copy-start.9 = (bf16[64,1536]{1,0:T(8,128)(2,1)S(1)}, bf16[64,1536]{1,0:T(8,128)(2,1)}, u32[]{:S(2)}) copy-start(bf16[64,1536]{1,0:T(8,128)(2,1)} %wo.1) | copy-start | bytes 589828
  38.5 34.8 %collective-permute-start.13 = (bf16[288,512]{1,0:T(8,128)(2,1)S(1)}, bf16[288,512]{1,0:T(8,128)(2,1)S(1)}, u32[]{:S(2)}, u32[]{:S(2)}) collective-permute-start(bf16[288,512]{1,0:T(8,128)(2,1)S(1)} %constant_dynamic-slice_fusion), channel_id=1, source_target_pairs={{0,8},{1,9},{2,10},{3,11},{4,12},{5,13},{6,14},{7,15},{8,0},{9,1},... | collective-permute-start | bytes 884744 | tf_op jit(solution)/shard_map/ppermute | solution.py:35
  73.3 11.6 %collective-permute-start.14 = (bf16[288,512]{1,0:T(8,128)(2,1)S(1)}, bf16[288,512]{1,0:T(8,128)(2,1)S(1)}, u32[]{:S(2)}, u32[]{:S(2)}) collective-permute-start(bf16[288,512]{1,0:T(8,128)(2,1)S(1)} %collective-permute-done.13), channel_id=1, source_target_pairs={{0,16},{1,17},{2,18},{3,19},{4,20},{5,21},{6,22},{7,23},{8,24},{9,... | collective-permute-start | bytes 884744 | tf_op jit(solution)/shard_map/ppermute | solution.py:35
  86.0 137.6 %all-gather.3.cloned.1.call-start = ((), (), s32[]{:S(2)}) async-start(), calls=%async_computation.3 | async-start | bytes 3538944 | tf_op jit(solution)/shard_map/all_gather | solution.py:331
  86.0 15.5 %collective-permute-start.2 = (bf16[144,1536]{1,0:T(8,128)(2,1)S(1)}, bf16[144,1536]{1,0:T(8,128)(2,1)S(1)}, u32[]{:S(2)}, u32[]{:S(2)}) collective-permute-start(bf16[144,1536]{1,0:T(8,128)(2,1)S(1)} %shard_map.140.b0), channel_id=1, source_target_pairs={{0,2},{1,3},{2,4},{3,5},{4,6},{5,7},{6,0},{7,1},{8,10},{9,11},{10,... | collective-permute-start | bytes 1327112 | tf_op jit(solution)/shard_map/ppermute | solution.py:35
  89.4 19.8 %collective-permute-start.1 = (bf16[144,1536]{1,0:T(8,128)(2,1)S(1)}, bf16[144,1536]{1,0:T(8,128)(2,1)S(1)}, u32[]{:S(2)}, u32[]{:S(2)}) collective-permute-start(bf16[144,1536]{1,0:T(8,128)(2,1)S(1)} %shard_map.140.b0), channel_id=1, source_target_pairs={{0,4},{1,5},{2,6},{3,7},{4,0},{5,1},{6,2},{7,3},{8,12},{9,13},{10,... | collective-permute-start | bytes 1327112 | tf_op jit(solution)/shard_map/ppermute | solution.py:35
  94.1 17.1 %collective-permute-start = (bf16[144,1536]{1,0:T(8,128)(2,1)S(1)}, bf16[144,1536]{1,0:T(8,128)(2,1)S(1)}, u32[]{:S(2)}, u32[]{:S(2)}) collective-permute-start(bf16[144,1536]{1,0:T(8,128)(2,1)S(1)} %shard_map.140.b0), channel_id=1, source_target_pairs={{0,6},{1,7},{2,0},{3,1},{4,2},{5,3},{6,4},{7,5},{8,14},{9,15},{10,... | collective-permute-start | bytes 1327112 | tf_op jit(solution)/shard_map/ppermute | solution.py:35
  97.4 36.4 %collective-permute-start.3 = (bf16[144,1536]{1,0:T(8,128)(2,1)S(1)}, bf16[144,1536]{1,0:T(8,128)(2,1)S(1)}, u32[]{:S(2)}, u32[]{:S(2)}) collective-permute-start(bf16[144,1536]{1,0:T(8,128)(2,1)S(1)} %shard_map.140.b0), channel_id=1, source_target_pairs={{0,1},{1,0},{2,3},{3,2},{4,5},{5,4},{6,7},{7,6},{8,9},{9,8},{10,11... | collective-permute-start | bytes 1327112 | tf_op jit(solution)/shard_map/ppermute | solution.py:35
  99.3 14.2 %collective-permute-start.10 = (bf16[48,1536]{1,0:T(8,128)(2,1)S(1)}, bf16[48,1536]{1,0:T(8,128)(2,1)S(1)}, u32[]{:S(2)}, u32[]{:S(2)}) collective-permute-start(bf16[48,1536]{1,0:T(8,128)(2,1)S(1)} %collective-permute-done.7.f0), channel_id=1, source_target_pairs={{0,128},{1,129},{2,130},{3,131},{4,132},{5,133},{6,134},{7,135},{8... | collective-permute-start | bytes 442376 | tf_op jit(solution)/shard_map/ppermute | solution.py:35
  101.5 32.3 %collective-permute-start.6 = (bf16[144,1536]{1,0:T(8,128)(2,1)S(1)}, bf16[144,1536]{1,0:T(8,128)(2,1)S(1)}, u32[]{:S(2)}, u32[]{:S(2)}) collective-permute-start(bf16[144,1536]{1,0:T(8,128)(2,1)S(1)} %collective-permute-done.2.b3), channel_id=1, source_target_pairs={{0,1},{1,0},{2,3},{3,2},{4,5},{5,4},{6,7},{7,6},{8,9},{9,8},{10,11... | collective-permute-start | bytes 1327112 | tf_op jit(solution)/shard_map/ppermute | solution.py:35
  109.2 24.6 %collective-permute-start.5 = (bf16[144,1536]{1,0:T(8,128)(2,1)S(1)}, bf16[144,1536]{1,0:T(8,128)(2,1)S(1)}, u32[]{:S(2)}, u32[]{:S(2)}) collective-permute-start(bf16[144,1536]{1,0:T(8,128)(2,1)S(1)} %collective-permute-done.1.b2), channel_id=1, source_target_pairs={{0,1},{1,0},{2,3},{3,2},{4,5},{5,4},{6,7},{7,6},{8,9},{9,8},{10,11... | collective-permute-start | bytes 1327112 | tf_op jit(solution)/shard_map/ppermute | solution.py:35
  111.1 22.7 %collective-permute-start.4 = (bf16[144,1536]{1,0:T(8,128)(2,1)S(1)}, bf16[144,1536]{1,0:T(8,128)(2,1)S(1)}, u32[]{:S(2)}, u32[]{:S(2)}) collective-permute-start(bf16[144,1536]{1,0:T(8,128)(2,1)S(1)} %collective-permute-done.b1), channel_id=1, source_target_pairs={{0,1},{1,0},{2,3},{3,2},{4,5},{5,4},{6,7},{7,6},{8,9},{9,8},{10,11... | collective-permute-start | bytes 1327112 | tf_op jit(solution)/shard_map/ppermute | solution.py:35
  113.5 12.0 %collective-permute-start.9 = (bf16[48,1536]{1,0:T(8,128)(2,1)S(1)}, bf16[48,1536]{1,0:T(8,128)(2,1)S(1)}, u32[]{:S(2)}, u32[]{:S(2)}) collective-permute-start(bf16[48,1536]{1,0:T(8,128)(2,1)S(1)} %collective-permute-done.7.f0), channel_id=1, source_target_pairs={{0,256},{1,257},{2,258},{3,259},{4,260},{5,261},{6,262},{7,263},{8... | collective-permute-start | bytes 442376 | tf_op jit(solution)/shard_map/ppermute | solution.py:35
  125.5 8.3 %collective-permute-start.8 = (bf16[48,1536]{1,0:T(8,128)(2,1)S(1)}, bf16[48,1536]{1,0:T(8,128)(2,1)S(1)}, u32[]{:S(2)}, u32[]{:S(2)}) collective-permute-start(bf16[48,1536]{1,0:T(8,128)(2,1)S(1)} %collective-permute-done.7.f0), channel_id=1, source_target_pairs={{0,384},{1,385},{2,386},{3,387},{4,388},{5,389},{6,390},{7,391},{8... | collective-permute-start | bytes 442376 | tf_op jit(solution)/shard_map/ppermute | solution.py:35
  137.3 8.4 %copy-start.17 = (bf16[1024,128]{1,0:T(8,128)(2,1)}, bf16[1024,128]{1,0:T(8,128)(2,1)S(1)}, u32[]{:S(2)}) copy-start(bf16[1024,128]{1,0:T(8,128)(2,1)S(1)} %get-tuple-element.17.kv) | copy-start | bytes 786436
  137.3 46.8 %copy-start.15 = (bf16[1024,128]{1,0:T(8,128)(2,1)}, bf16[1024,128]{1,0:T(8,128)(2,1)S(1)}, u32[]{:S(2)}) copy-start(bf16[1024,128]{1,0:T(8,128)(2,1)S(1)} %get-tuple-element.16.q) | copy-start | bytes 786436
  137.3 46.7 %copy-start.20 = (s32[128,2]{0,1:T(2,128)S(1)}, s32[128,2]{0,1:T(2,128)}, u32[]{:S(2)}) copy-start(s32[128,2]{0,1:T(2,128)} %param.20) | copy-start | bytes 3076
  143.7 55.4 %copy-start.21 = (s32[1,128]{1,0:T(1,128)S(1)}, s32[1,128]{1,0:T(1,128)}, u32[]{:S(2)}) copy-start(s32[1,128]{1,0:T(1,128)} %table.1) | copy-start | bytes 1540
  143.7 88.5 %collective-permute-start.15 = (bf16[2304,512]{1,0:T(8,128)(2,1)}, bf16[2304,512]{1,0:T(8,128)(2,1)}, u32[]{:S(2)}, u32[]{:S(2)}) collective-permute-start(bf16[2304,512]{1,0:T(8,128)(2,1)} %get-tuple-element.30), channel_id=1, source_target_pairs={{0,1},{1,0},{2,3},{3,2},{4,5},{5,4},{6,7},{7,6},{8,9},{9,8},{10,11... | collective-permute-start | bytes 7077896 | tf_op jit(solution)/shard_map/ppermute | solution.py:35
  145.7 36.2 %collective-permute-start.11 = (bf16[1024,128]{1,0:T(8,128)(2,1)S(1)}, bf16[1024,128]{1,0:T(8,128)(2,1)S(1)}, u32[]{:S(2)}, u32[]{:S(2)}) collective-permute-start(bf16[1024,128]{1,0:T(8,128)(2,1)S(1)} %get-tuple-element.17.kv), channel_id=1, source_target_pairs={{0,8},{1,9},{2,10},{3,11},{4,12},{5,13},{6,14},{7,15},{8,0},{9,1},... | collective-permute-start | bytes 786440 | tf_op jit(solution)/shard_map/ppermute | solution.py:35
  182.0 17.1 %collective-permute-start.12 = (bf16[1024,128]{1,0:T(8,128)(2,1)S(1)}, bf16[1024,128]{1,0:T(8,128)(2,1)S(1)}, u32[]{:S(2)}, u32[]{:S(2)}) collective-permute-start(bf16[1024,128]{1,0:T(8,128)(2,1)S(1)} %collective-permute-done.11.partner), channel_id=1, source_target_pairs={{0,16},{1,17},{2,18},{3,19},{4,20},{5,21},{6,22},{7,23},{16,32},{1... | collective-permute-start | bytes 786440 | tf_op jit(solution)/shard_map/ppermute | solution.py:35
  184.1 1.0 copy-start.18
  185.0 14.1 %copy-start.19 = (bf16[1024,128]{1,0:T(8,128)(2,1)S(1)}, bf16[1024,128]{1,0:T(8,128)(2,1)}, u32[]{:S(2)}) copy-start(bf16[1024,128]{1,0:T(8,128)(2,1)} %copy-done.17) | copy-start | bytes 786436
  199.1 1.0 copy-start.16
  200.0 13.1 %copy-start.27 = (f32[1536]{0:T(1024)S(1)}, f32[1536]{0:T(1024)}, u32[]{:S(2)}) copy-start(f32[1536]{0:T(1024)} %param.15) | copy-start | bytes 18436
  200.0 23.5 %copy-start.5 = (bf16[128,1536]{1,0:T(8,128)(2,1)S(1)}, bf16[128,1536]{1,0:T(8,128)(2,1)}, u32[]{:S(2)}) copy-start(bf16[128,1536]{1,0:T(8,128)(2,1)} %tokens.3) | copy-start | bytes 1179652
  207.5 0.9 copy-start.10
  208.3 15.2 %all-to-all-start = ((bf16[8,256,128]{2,1,0:T(8,128)(2,1)}), bf16[8,256,128]{2,1,0:T(8,128)(2,1)S(1)}, u32[]{:S(2)}, u32[]{:S(2)}) async-start(bf16[8,256,128]{2,1,0:T(8,128)(2,1)} %copy-done.10), calls=%async_computation | async-start | bytes 1048576 | tf_op jit(solution)/shard_map/all_to_all | solution.py:351
  223.5 5.0 %copy-start.1 = (bf16[8,256,128]{2,1,0:T(8,128)(2,1)}, bf16[8,256,128]{2,1,0:T(8,128)(2,1)S(1)}, u32[]{:S(2)}) copy-start(bf16[8,256,128]{2,1,0:T(8,128)(2,1)S(1)} %all-to-all-done.joined) | copy-start | bytes 1572868
  223.5 2.1 copy-start.3
  226.8 1.0 copy-start.6
  227.8 0.7 copy-start.11
  228.6 20.9 %all-to-all-start.1 = ((bf16[8,48,1536]{2,1,0:T(8,128)(2,1)}), bf16[8,48,1536]{2,1,0:T(8,128)(2,1)S(1)}, u32[]{:S(2)}, u32[]{:S(2)}) async-start(bf16[8,48,1536]{2,1,0:T(8,128)(2,1)} %bitcast.19), calls=%async_computation.1 | async-start | bytes 2359296 | tf_op jit(solution)/shard_map/all_to_all | solution.py:360
  253.2 1.0 copy-start
  254.2 3.7 %copy-start.2 = (bf16[8,256,128]{2,1,0:T(8,128)(2,1)S(1)}, bf16[8,256,128]{2,1,0:T(8,128)(2,1)}, u32[]{:S(2)}) copy-start(bf16[8,256,128]{2,1,0:T(8,128)(2,1)} %copy-done.1) | copy-start | bytes 1572868
  254.2 21.0 %copy-start.12 = (bf16[128,1536]{1,0:T(8,128)(2,1)S(1)}, bf16[128,1536]{1,0:T(8,128)(2,1)}, u32[]{:S(2)}) copy-start(bf16[128,1536]{1,0:T(8,128)(2,1)} %copy-done.11) | copy-start | bytes 1179652
  254.2 21.0 %copy-start.13 = (f32[128,2]{0,1:T(2,128)S(1)}, f32[128,2]{0,1:T(2,128)}, u32[]{:S(2)}) copy-start(f32[128,2]{0,1:T(2,128)} %param.21) | copy-start | bytes 3076
  254.2 21.0 %all-to-all-start.2 = ((bf16[8,48,1536]{2,1,0:T(8,128)(2,1)}), bf16[8,48,1536]{2,1,0:T(8,128)(2,1)S(1)}, u32[]{:S(2)}, u32[]{:S(2)}) async-start(bf16[8,48,1536]{2,1,0:T(8,128)(2,1)} %bitcast.17), calls=%async_computation.2 | async-start | bytes 2359296 | tf_op jit(solution)/shard_map/all_to_all | solution.py:389
Sparse Core Ops, SparseCore 0:
  86.1 42.0 all-gather.4
  137.4 34.2 all-gather.2

commit v3 on v2

v3 whole, which is shorter than its diff:
```python
import functools

import jax
import jax.numpy as jnp
import numpy as np
from jax import lax
from jax.experimental import pallas as pl
from jax.experimental.pallas import tpu as pltpu
from jax.sharding import Mesh
from jax.sharding import PartitionSpec as P

AXES = ("y", "zq", "zp", "zh", "x", "c")
SIZES = (4, 4, 2, 2, 4, 2)
FLAT = (4, 8, 2, 4, 2)
ROW = ("x", "c")
PAGE = 16
CAP = 48
TOK = 128
WIDTH = 1536
ROWS = 8 * TOK
BF16 = jnp.bfloat16
F32 = jnp.float32
I32 = jnp.int32
VMEM = pl.BlockSpec(memory_space=pltpu.VMEM)
ANY = pl.BlockSpec(memory_space=pl.ANY)
SMEM = pl.BlockSpec(memory_space=pltpu.SMEM)
MIB = 1 << 20


def permute(block, target):
    route = []
    for source in range(int(np.prod(FLAT))):
        goal = target(*(int(v) for v in np.unravel_index(source, FLAT)))
        if goal is not None:
            route.append((source, int(np.ravel_multi_index(goal, FLAT))))
    return lax.ppermute(block, AXES, route)


def swap_core(block):
    return permute(block, lambda y, zl, zh, x, c: (y, zl, zh, x, 1 - c))


def swap_half(block):
    return permute(block, lambda y, zl, zh, x, c: (y, zl, 1 - zh, x, c))


def next_group(block):
    def target(y, zl, zh, x, c):
        if zl < 7:
            return (y, zl + 1, 0, x, c) if zh == 0 else None
        return (y + 1, 0, 0, x, c) if zh == 1 and y < 3 else None

    return permute(block, target)


def give_half(block, near):
    def target(y, zl, zh, x, c):
        return (y, zl, zh, x, 1 - c) if (c == zh) != near else None

    return permute(block, target)


def gather(block, axis):
    wide = jnp.broadcast_to(block[None], (lax.axis_size(axis),) + block.shape)
    return lax.all_to_all(wide, axis, split_axis=0, concat_axis=0, tiled=True)


def after(value, *earlier):
    return lax.optimization_barrier((value,) + earlier)[0]


def call(kernel, outs, in_specs, scratch=(), flops=0, nbytes=0, limit=48):
    outs = [jax.ShapeDtypeStruct(shape, kind) for shape, kind in outs]
    return pl.pallas_call(
        kernel,
        out_shape=outs,
        in_specs=in_specs,
        out_specs=[VMEM] * len(outs),
        scratch_shapes=list(scratch),
        compiler_params=pltpu.CompilerParams(vmem_limit_bytes=limit * MIB),
        cost_estimate=pl.CostEstimate(flops=flops, bytes_accessed=nbytes, transcendentals=0),
    )


def dot_nt(left, right):
    return lax.dot_general(left, right, (((1,), (1,)), ((), ())), preferred_element_type=F32)


def dot_tn(left, right):
    return lax.dot_general(left, right, (((0,), (0,)), ((), ())), preferred_element_type=F32)


def column(lane_row):
    return jnp.transpose(jnp.broadcast_to(lane_row, (TOK, TOK)))


def rms(values, gain):
    inverse = lax.rsqrt(jnp.mean(values * values, axis=-1, keepdims=True) + 1e-05)
    return (values * inverse * gain).astype(BF16)


def pack_kernel(meta, tokens, seg, ids, out):
    own = meta[5] * TOK + lax.broadcasted_iota(I32, (1, TOK), 1)
    back = own - seg[...]
    row = lax.broadcasted_iota(I32, (16, TOK), 0)
    pieces = jnp.where(row == 0, back >> 5, jnp.where(row == 1, back & 31, 0))
    pieces = jnp.where(row == 2, ids[0:1], jnp.where(row == 3, ids[1:2], pieces))
    pieces = pieces.astype(F32).astype(BF16)
    for copy in range(4):
        out[copy, :TOK] = tokens[...]
        out[copy, TOK:, :TOK] = pieces
        out[copy, TOK:, TOK:] = jnp.zeros((16, WIDTH - TOK), BF16)


def eighth_kernel(meta, gate, up, down, out, sems):
    piece = meta[0] * 2 + lax.rem(meta[1], 2)
    wide = pl.ds(pl.multiple_of(piece * 192, 64), 192)
    deep = pl.ds(pl.multiple_of(piece * 32, 32), 32)
    copies = [
        pltpu.make_async_copy(gate.at[wide], out.at[:192, :256], sems.at[0]),
        pltpu.make_async_copy(up.at[wide], out.at[:192, 256:], sems.at[1]),
    ]
    for i in range(3):
        copies.append(
            pltpu.make_async_copy(
                down.at[deep, i * 512 : i * 512 + 512],
                out.at[192 + 32 * i : 224 + 32 * i],
                sems.at[2 + i],
            )
        )
    for copy in copies:
        copy.start()
    for copy in copies:
        copy.wait()


def order_kernel(gate, up, down, out):
    for e in range(8):
        low = e * 288
        out[low : low + 192, :256] = gate[e * 192 : e * 192 + 192]
        out[low : low + 192, 256:] = up[e * 192 : e * 192 + 192]
        for i in range(3):
            out[low + 192 + 32 * i : low + 224 + 32 * i] = down[
                e * 32 : e * 32 + 32, i * 512 : i * 512 + 512
            ]


def project_kernel(meta, near, across, wq, wkv, far, gain, q_out, kv_out, start_out, cols):
    zh, c = meta[2], meta[4]
    cols[0:64] = wq[...]
    cols[64:128] = far[0:64]
    cols[pl.ds(pl.multiple_of(128 + zh * 64, 64), 64), :] = wkv[...]
    cols[pl.ds(pl.multiple_of(192 - zh * 64, 64), 64), :] = far[64:128]
    for k in range(4):
        for block, core in ((near, c), (across, 1 - c)):
            low = pl.multiple_of((2 * k + core) * TOK, TOK)
            normed = rms(block[k, :TOK].astype(F32), gain[...])
            result = dot_nt(normed, cols[...]).astype(BF16)
            q_out[pl.ds(low, TOK), :] = result[:, :128]
            kv_out[pl.ds(low, TOK), :] = result[:, 128:]
            pieces = block[k, TOK:, :TOK].astype(F32)
            back = column(pieces[0:1] * 32.0 + pieces[1:2])
            own = (low + lax.broadcasted_iota(I32, (TOK, TOK), 0)).astype(F32)
            start_out[pl.ds(low, TOK), :] = own - back


def route_kernel(meta, near, across, pick_out, other_out, rows_out):
    x, c = meta[3], meta[4]
    before = lax.broadcasted_iota(I32, (TOK, TOK), 0) < lax.broadcasted_iota(I32, (TOK, TOK), 1)
    before = before.astype(F32).astype(BF16)
    row = lax.broadcasted_iota(I32, (CAP, TOK), 0).astype(F32)
    for expert, out in ((x + 4 * c, pick_out), (x + 4 * (1 - c), other_out)):
        number = expert.astype(F32)
        for k in range(4):
            for block, core in ((near, c), (across, 1 - c)):
                low = pl.multiple_of((2 * k + core) * CAP, 16)
                pieces = block[k, TOK:, :TOK].astype(F32)
                named = (pieces == number).astype(F32)
                named = named[2:3] + named[3:4]
                rank = jnp.dot(
                    jnp.broadcast_to(named, (8, TOK)).astype(BF16),
                    before,
                    preferred_element_type=F32,
                )[0:1]
                pick = jnp.where((row == rank) & (named > 0.0), 1.0, 0.0).astype(BF16)
                out[pl.ds(low, CAP), :] = pick
                if out is pick_out:
                    chosen = jnp.dot(pick, block[k, :TOK], preferred_element_type=F32)
                    rows_out[pl.ds(low, CAP), :] = chosen.astype(BF16)


def split_kv(kv):
    wide = kv[...].astype(F32)
    turned = pltpu.roll(wide, 64, 1)
    low = lax.broadcasted_iota(I32, wide.shape, 1) < 64
    return (
        jnp.where(low, wide, turned).astype(BF16),
        jnp.where(low, turned, wide).astype(BF16),
    )


STEP = 256


def own_kernel(q, kv, start, ids, sum_out, max_out, den_out, slots_out, keys, values):
    keys[...], values[...] = split_kv(kv)
    low_lane = lax.broadcasted_iota(I32, (STEP, 128), 1) < 64
    for block in range(ROWS // STEP):
        low = block * STEP
        span = low + STEP
        query = q[low:span]
        position = lax.broadcasted_iota(I32, (STEP, span), 1).astype(F32)
        own = (low + lax.broadcasted_iota(I32, (STEP, span), 0)).astype(F32)
        allowed = (position <= own) & (position >= start[low:span, 0:1])
        parts = []
        for head in range(2):
            kept = jnp.where(low_lane if head == 0 else ~low_lane, query, jnp.zeros_like(query))
            scores = jnp.where(allowed, dot_nt(kept, keys[:span]) * 0.125, -1e30)
            top = jnp.max(scores, axis=-1, keepdims=True)
            weights = jnp.exp(scores - top)
            den = jnp.sum(weights, axis=-1, keepdims=True)
            part = jnp.dot(weights.astype(BF16), values[:span], preferred_element_type=F32)
            parts.append((part, top, den))
        for out, one, two in zip((sum_out, max_out, den_out), *parts):
            out[low:span] = jnp.where(low_lane, one, two)
    choice = [ids[k : k + 1].astype(F32) for k in range(2)]
    down = [column(v) for v in choice]
    earlier = lax.broadcasted_iota(I32, (TOK, TOK), 0) < lax.broadcasted_iota(I32, (TOK, TOK), 1)
    result = []
    for k in range(2):
        same = sum((down[j] == choice[k]).astype(F32) for j in range(2))
        rank = jnp.sum(jnp.where(earlier, same, 0.0), axis=0, keepdims=True).astype(I32)
        expert = ids[k : k + 1]
        result.append(((expert & 3) * 2 + (expert >> 2)) * CAP + rank)
    row = lax.broadcasted_iota(I32, (8, TOK), 0)
    slots_out[...] = jnp.where(row == 0, result[0], result[1])


def before_kernel(q, kv, start, sums, maxes, dens, out, keys, values):
    keys[...], values[...] = split_kv(kv)
    low_lane = lax.broadcasted_iota(I32, (STEP, 128), 1) < 64
    for block in range(ROWS // STEP):
        low = block * STEP
        high = low + STEP
        span = ROWS - low
        query = q[low:high]
        position = (low - ROWS + lax.broadcasted_iota(I32, (STEP, span), 1)).astype(F32)
        allowed = position >= start[low:high, 0:1]
        parts = []
        for head in range(2):
            kept = jnp.where(low_lane if head == 0 else ~low_lane, query, jnp.zeros_like(query))
            scores = jnp.where(allowed, dot_nt(kept, keys[low:]) * 0.125, -1e30)
            first = maxes[low:high, head * 64 : head * 64 + 1]
            top = jnp.maximum(first, jnp.max(scores, axis=-1, keepdims=True))
            weights = jnp.exp(scores - top)
            scale = jnp.exp(first - top)
            den = jnp.sum(weights, axis=-1, keepdims=True)
            part = jnp.dot(weights.astype(BF16), values[low:], preferred_element_type=F32)
            parts.append((part, scale, den))
        part, scale, den = (jnp.where(low_lane, one, two) for one, two in zip(*parts))
        total = sums[low:high] * scale + part
        result = (total / (dens[low:high] * scale + den)).astype(BF16)
        for copy in range(4):
            out[copy, low:high, :] = result


def page_kernel(meta, table, kv, partner, out, group):
    zh = meta[2]
    group[pl.ds(pl.multiple_of(zh * ROWS, ROWS), ROWS), :] = kv[...]
    group[pl.ds(pl.multiple_of((1 - zh) * ROWS, ROWS), ROWS), :] = partner[...]

    def place(block, carry):
        page = table[0, block] - zh * 64

        @pl.when((page >= 0) & (page < 64))
        def _():
            out[pl.ds(pl.multiple_of(page * PAGE, PAGE), PAGE), :] = group[
                pl.ds(pl.multiple_of(block * PAGE, PAGE), PAGE), :
            ]

        return carry

    lax.fori_loop(0, 128, place, 0)


def cache_kernel(pages, out):
    low = lax.broadcasted_iota(I32, (TOK, 128), 1) < 64
    for pair in range(4):
        one = pages[2 * pair].astype(F32)
        two = pages[2 * pair + 1].astype(F32)
        lanes = slice(pair * 128, pair * 128 + 128)
        out[:, lanes] = jnp.where(low, one, pltpu.roll(two, 64, 1)).astype(BF16)
        lanes = slice(512 + pair * 128, 640 + pair * 128)
        out[:, lanes] = jnp.where(low, pltpu.roll(one, 64, 1), two).astype(BF16)


def choose(slots, k):
    place = lax.broadcasted_iota(I32, (8 * CAP, TOK), 0)
    return place == slots[k : k + 1]


def split_kernel(meta, heads, pick, other, keep_out, give_out):
    x, c = meta[3], meta[4]
    for d in range(8):
        rows = jnp.concatenate([heads[k, d * TOK : d * TOK + TOK] for k in range(4)], axis=1)
        low = slice(d * CAP, d * CAP + CAP)
        keep_out[low] = jnp.dot(pick[low], rows, preferred_element_type=F32).astype(BF16)
        give_out[low] = jnp.dot(other[low], rows, preferred_element_type=F32).astype(BF16)
    for out, core in ((keep_out, c), (give_out, 1 - c)):
        low = pl.multiple_of((2 * x + core) * TOK, TOK)
        for k in range(4):
            out[8 * CAP :, k * 128 : k * 128 + 128] = heads[k, pl.ds(low, TOK), :]


def expert_kernel(meta, keep, got, wo_all, rows, tokens, gain, own, other, given_a, given_b,
                  mid_out, out, raw, wide, deep, sems):
    zh, c = meta[2], meta[4]

    @pl.when(c == zh)
    def _():
        pltpu.make_async_copy(own, raw.at[0], sems.at[0]).start()
        pltpu.make_async_copy(given_a, raw.at[1], sems.at[1]).start()

    @pl.when(c != zh)
    def _():
        pltpu.make_async_copy(other, raw.at[0], sems.at[0]).start()
        pltpu.make_async_copy(given_b, raw.at[1], sems.at[1]).start()

    tiles = []
    for k in range(4):
        one = keep[:, k * 128 : k * 128 + 128]
        two = got[:, k * 128 : k * 128 + 128]
        tiles += [jnp.where(c == 0, one, two), jnp.where(c == 0, two, one)]
    total = jnp.dot(jnp.concatenate(tiles, axis=1), wo_all[...], preferred_element_type=F32)
    mid_out[...] = (tokens[...].astype(F32) + total[8 * CAP :]).astype(BF16)
    mid = (rows[...].astype(F32) + total[: 8 * CAP]).astype(BF16)
    arrived = rms(mid.astype(F32), gain[...])
    acts = []
    for half, source in enumerate((own, given_a)):
        pltpu.make_async_copy(source, raw.at[half], sems.at[half]).wait()
        for e in range(8):
            low = e * 288
            wide[half, e * 192 : e * 192 + 192] = raw[half, low : low + 192]
            for i in range(3):
                deep[half, i * 256 + e * 32 : i * 256 + e * 32 + 32] = raw[
                    half, low + 192 + 32 * i : low + 224 + 32 * i
                ]
        both = jnp.dot(arrived, wide[half], preferred_element_type=F32)
        gate, up = both[:, :256], both[:, 256:]
        acts.append((gate / (1.0 + jnp.exp(-gate)) * up).astype(BF16))
    for i in range(3):
        chunk = slice(i * 256, i * 256 + 256)
        total = jnp.dot(acts[0], deep[0, chunk], preferred_element_type=F32)
        total += jnp.dot(acts[1], deep[1, chunk], preferred_element_type=F32)
        out[:, i * 512 : i * 512 + 512] = total.astype(BF16)


def combine_kernel(returned, mid, slots, weights, out):
    total = mid[...].astype(F32)
    for k in range(2):
        pick = choose(slots, k).astype(F32).astype(BF16)
        chosen = dot_tn(pick, returned[...])
        total += chosen * column(weights[k : k + 1])[:, 0:1]
    out[...] = total.astype(BF16)


def body(
    tokens,
    attn_gain,
    ffn_gain,
    w_query,
    key_value_weight,
    w_out,
    segment_ids,
    expert_ids,
    route_weights,
    w_gate,
    w_up,
    w_down,
    page_table,
):
    y, zq, zp, zh, x, c = (lax.axis_index(name) for name in AXES)
    zl = zq * 2 + zp
    place = (((y * 8 + zl) * 2 + zh) * 4 + x) * 2 + c
    meta = jnp.stack([y, zl, zh, x, c, place]).astype(I32)
    wq, wkv = w_query.T, key_value_weight.T
    ids = expert_ids.T

    parts = jnp.concatenate(
        [lax.dynamic_slice_in_dim(w, y * 16, 16, 0) for w in (wq, wkv, w_out)], axis=0
    )
    parts = swap_half(parts)
    (block,) = call(
        pack_kernel, [((4, TOK + 16, WIDTH), BF16)], [SMEM] + [VMEM] * 3, nbytes=0
    )(meta, tokens, segment_ids[None, :], ids)
    (eighth,) = call(
        eighth_kernel,
        [((288, 512), BF16)],
        [SMEM] + [ANY] * 3,
        scratch=[pltpu.SemaphoreType.DMA((5,))],
        nbytes=0,
    )(meta, w_gate, w_up, w_down)
    near = lax.all_to_all(block, "x", split_axis=0, concat_axis=0, tiled=True)
    eighth = swap_half(eighth)
    near, parts, eighth = lax.optimization_barrier((near, parts, eighth))
    parts = gather(parts, "y").reshape(4, 3, 16, WIDTH)
    far_cols = parts[:, :2].transpose(1, 0, 2, 3).reshape(128, WIDTH)
    across = swap_core(near)
    gain = attn_gain[None, :]
    q, kv, start = call(
        project_kernel,
        [((ROWS, 128), BF16), ((ROWS, 128), BF16), ((ROWS, 128), F32)],
        [SMEM] + [VMEM] * 6,
        scratch=[pltpu.VMEM((256, WIDTH), BF16)],
        flops=0,
        nbytes=0,
    )(meta, near, across, wq, wkv, far_cols, gain)
    out_rows = jnp.concatenate([w_out, parts[:, 2].reshape(64, WIDTH)], axis=0)
    out_all = lax.all_gather(out_rows, ROW, axis=0, tiled=True)

    partner = swap_half(kv)
    sums, maxes, dens, slots = call(
        own_kernel,
        [((ROWS, 128), F32)] * 3 + [((8, TOK), I32)],
        [VMEM] * 4,
        scratch=[pltpu.VMEM((ROWS, 128), BF16)] * 2,
        flops=0,
        nbytes=0,
    )(q, kv, start, ids)
    pick, other_pick, chosen = call(
        route_kernel,
        [((8 * CAP, TOK), BF16)] * 2 + [((8 * CAP, WIDTH), BF16)],
        [SMEM] + [VMEM] * 2,
        flops=0,
        nbytes=0,
    )(meta, after(near, sums), across)

    (own,) = call(order_kernel, [((2304, 512), BF16)], [VMEM] * 3, nbytes=0)(
        *(after(w, sums) for w in (w_gate, w_up, w_down))
    )
    given_a = give_half(own, True)
    other = gather(after(eighth, sums), ("y", "zp")).reshape(2304, 512)

    shifted = next_group(jnp.where(zh == 0, partner, kv))
    (pages,) = call(
        page_kernel,
        [((ROWS, 128), BF16)],
        [SMEM, SMEM] + [VMEM] * 2,
        scratch=[pltpu.VMEM((2 * ROWS, 128), BF16)],
        nbytes=0,
    )(meta, page_table, kv, partner)
    held = lax.all_to_all(
        pages.reshape(8, TOK, 128), ROW, split_axis=0, concat_axis=0, tiled=True
    )
    previous = jnp.where(zh == 0, shifted, partner)
    (heads,) = call(
        before_kernel,
        [((4, ROWS, 128), BF16)],
        [VMEM] * 6,
        scratch=[pltpu.VMEM((ROWS, 128), BF16)] * 2,
        flops=0,
        nbytes=0,
    )(after(q, pages), previous, start, sums, maxes, dens)
    other = after(other, heads)
    given_b = give_half(other, False)
    heads = lax.all_to_all(heads, "x", split_axis=0, concat_axis=0, tiled=True)
    (cache,) = call(cache_kernel, [((TOK, 1024), BF16)], [VMEM], nbytes=0)(held)
    keep, give = call(
        split_kernel,
        [((4 * TOK, 512), BF16)] * 2,
        [SMEM] + [VMEM] * 3,
        flops=0,
        nbytes=0,
    )(meta, heads, pick, other_pick)
    got = swap_core(give)
    mid, expert_out = call(
        expert_kernel,
        [((TOK, WIDTH), BF16), ((8 * CAP, WIDTH), BF16)],
        [SMEM] + [VMEM] * 6 + [ANY] * 4,
        scratch=[
            pltpu.VMEM((2, 2304, 512), BF16),
            pltpu.VMEM((2, WIDTH, 512), BF16),
            pltpu.VMEM((2, 768, 512), BF16),
            pltpu.SemaphoreType.DMA((2,)),
        ],
        flops=0,
        nbytes=0,
    )(meta, keep, got, out_all, chosen, tokens, ffn_gain[None, :], own, other, given_a, given_b)
    returned = lax.all_to_all(
        expert_out.reshape(8, CAP, WIDTH), ROW, split_axis=0, concat_axis=0, tiled=True
    ).reshape(8 * CAP, WIDTH)
    (hidden,) = call(
        combine_kernel, [((TOK, WIDTH), BF16)], [VMEM] * 4, flops=0, nbytes=0
    )(returned, mid, slots, route_weights.T)
    return (hidden, cache.reshape(8, PAGE, 1024))


def solution(mesh):
    fine = Mesh(mesh.devices.reshape(SIZES), AXES)
    grp, tp = ("y", "zq", "zp"), ("zh", "x", "c")
    in_specs = (
        P(AXES, None),
        P(),
        P(),
        P(None, tp),
        P(None, tp),
        P(tp, None),
        P(AXES),
        P(AXES, None),
        P(AXES, None),
        P(None, tp),
        P(None, tp),
        P(tp, None),
        P(grp, None),
    )
    out_specs = (P(AXES, None), P(AXES, None, None))
    return jax.shard_map(body, mesh=fine, in_specs=in_specs, out_specs=out_specs, check_vma=False)
```

time: 284 us -> 262 us (0.923)
  the two profiles are of different devices: /device:TPU:24 before, /device:TPU:32 now
where the time goes in v3:
time: 262 us; the launch traced here: 261 us
  waiting for transfers between devices  110 us (42%)
  starting transfers between devices  72.9 us (28%)
  Pallas kernels  32.7 us (12%)
  local copies, waits for them, and re-layouts  27.9 us (11%)
  between operations  14.5 us (6%)
  other arithmetic  2.73 us (1%)
    ppermute x8, waiting for transfers between devices, permute(): return lax.ppermute(block, AXES, route)  74.3 us
    ppermute x8, starting transfers between devices, permute(): return lax.ppermute(block, AXES, route)  47.1 us
    unnamed x78, local copies, waits for them, and re-layouts  20 us
    all_to_all x1, waiting for transfers between devices, body(): lax.all_to_all(expert_out.reshape(8, CAP, WIDTH), ROW, split_axis=0, conc...  16.5 us
    all_to_all x2, waiting for transfers between devices, gather(): return lax.all_to_all(wide, axis, split_axis=0, concat_axis=0, tiled=True)  10.2 us
    all_to_all x2, starting transfers between devices, gather(): return lax.all_to_all(wide, axis, split_axis=0, concat_axis=0, tiled=True)  8.8 us
    all_to_all x1, waiting for transfers between devices, body(): heads = lax.all_to_all(heads, 'x', split_axis=0, concat_axis=0, tiled=True)  8.76 us
    pallas_call x1, Pallas kernels, body(): call(expert_kernel, [((TOK, WIDTH), BF16), ((8 * CAP, WIDTH), BF16)], [SM...  7.47 us
  transfers between devices with their start and end apart: 15, of which 5 were waited for; matrix products, arithmetic and copies ran while one was open for 3% of the time, Pallas kernels for 9%

profile of v3, /device:TPU:32, one launch (start us, length us, event | category | flops | bytes accessed | tf_op | source)
XLA Modules:
  0.0 260.6 jit_solution(12218587502549853533)
XLA Ops:
  7.2 0.1 stack.27.meta
  7.3 1.0 copy-done.11
  8.3 0.7 copy-done.30
  8.9 0.7 copy-done.33
  9.6 1.9 shard_map.140
  11.5 4.3 %all-to-all-start = ((bf16[4,144,1536]{2,1,0:T(8,128)(2,1)}), bf16[4,144,1536]{2,1,0:T(8,128)(2,1)S(1)}, u32[]{:S(2)}, u32[]{:S(2)}) async-start(bf16[4,144,1536]{2,1,0:T(8,128)(2,1)} %shard_map.140), calls=%async_computation | async-start | bytes 3538944 | tf_op jit(solution)/shard_map/all_to_all | solution.py:403
  15.8 1.1 copy-done.5
  16.9 1.4 shard_map.141
  18.3 14.8 %collective-permute-start.1 = (bf16[288,512]{1,0:T(8,128)(2,1)}, bf16[288,512]{1,0:T(8,128)(2,1)S(1)}, u32[]{:S(2)}, u32[]{:S(2)}) collective-permute-start(bf16[288,512]{1,0:T(8,128)(2,1)} %shard_map.141), channel_id=1, source_target_pairs={{0,8},{1,9},{2,10},{3,11},{4,12},{5,13},{6,14},{7,15},{8,0},{9,1},... | collective-permute-start | bytes 884744 | tf_op jit(solution)/shard_map/ppermute | solution.py:36
  33.1 0.8 constant_dynamic-slice_fusion
  33.9 0.8 dynamic-slice_bitcast_fusion
  34.8 1.9 collective-permute-start
  36.7 35.1 %collective-permute-done = bf16[48,1536]{1,0:T(8,128)(2,1)S(1)} collective-permute-done((bf16[48,1536]{1,0:T(8,128)(2,1)S(1)}, bf16[48,1536]{1,0:T(8,128)(2,1)S(1)}, u32[]{:S(2)}, u32[]{:S(2)}) %collective-permute-start) | collective-permute-done | bytes 147488 | tf_op jit(solution)/shard_map/ppermute | solution.py:36
  71.9 0.7 copy-done.37
  72.5 0.7 copy-done.35
  73.2 1.9 collective-permute-start.2
  75.1 1.8 broadcast_in_dim.22
  76.9 4.5 %all-to-all-start.1 = ((bf16[4,48,1536]{2,1,0:T(8,128)(2,1)}), bf16[4,48,1536]{2,1,0:T(8,128)(2,1)}, u32[]{:S(2)}, u32[]{:S(2)}) async-start(bf16[4,48,1536]{2,1,0:T(8,128)(2,1)} %broadcast_in_dim.22), calls=%async_computation.1 | async-start | bytes 1179648 | tf_op jit(solution)/shard_map/all_to_all | solution.py:65
  81.4 0.7 broadcast_in_dim.23.gain
  82.1 10.2 %all-to-all-done.1 = bf16[4,48,1536]{2,1,0:T(8,128)(2,1)} async-done(((bf16[4,48,1536]{2,1,0:T(8,128)(2,1)}), bf16[4,48,1536]{2,1,0:T(8,128)(2,1)}, u32[]{:S(2)}, u32[]{:S(2)}) %all-to-all-start.1) | async-done | bytes 589856 | tf_op jit(solution)/shard_map/all_to_all | solution.py:65
  92.3 1.0 slice_bitcast_fusion
  93.4 0.9 copy-done.24
  94.3 0.9 copy-done.25
  95.3 2.9 %shard_map.142 = (bf16[1024,128]{1,0:T(8,128)(2,1)S(1)}, bf16[1024,128]{1,0:T(8,128)(2,1)S(1)}, f32[1024,128]{1,0:T(8,128)S(1)}) custom-call(s32[6]{0:T(128)S(1)} %stack.27.meta, bf16[4,144,1536]{2,1,0:T(8,128)(2,1)S(1)} %all-to-all-done.near, bf16[4,144,1536]{2,1,0:T(8,128)(2,1)S(1)} %collective-permute-done.2.across, bf16[64,1536]{1,0:T(8,128)(2,1)S(1)} %bitcast.28, ...), custom_call_target="tpu_custom_call" | custom-call | tf_op jit(solution)/shard_map/pallas_call | solution.py:410
  98.2 3.8 %shard_map.144 = (f32[1024,128]{1,0:T(8,128)S(1)}, f32[1024,128]{1,0:T(8,128)S(1)}, f32[1024,128]{1,0:T(8,128)S(1)}, s32[8,128]{1,0:T(8,128)S(1)}) custom-call(bf16[1024,128]{1,0:T(8,128)(2,1)S(1)} %get-tuple-element.30.q, bf16[1024,128]{1,0:T(8,128)(2,1)S(1)} %get-tuple-element.29.kv, f32[1024,128]{1,0:T(8,128)S(1)} %get-tuple-element.31.start, ...), custom_call_target="tpu_custom_call" | custom-call | tf_op jit(solution)/shard_map/pallas_call | solution.py:422
  102.0 0.7 copy-done.7
  102.7 0.8 copy-done.18
  103.5 0.8 copy-done.20
  104.3 0.8 copy-done.22
  105.2 1.7 broadcast_in_dim.25
  106.9 4.3 %all-to-all-start.3 = ((bf16[8,288,512]{2,1,0:T(8,128)(2,1)}), bf16[8,288,512]{2,1,0:T(8,128)(2,1)}, u32[]{:S(2)}, u32[]{:S(2)}) async-start(bf16[8,288,512]{2,1,0:T(8,128)(2,1)} %broadcast_in_dim.25), calls=%async_computation.3 | async-start | bytes 4718592 | tf_op jit(solution)/shard_map/all_to_all | solution.py:65
  111.2 0.9 slice.9
  112.2 1.7 pad_maximum_fusion
  113.9 12.1 %collective-permute-start.3 = (bf16[1024,128]{1,0:T(8,128)(2,1)}, bf16[1024,128]{1,0:T(8,128)(2,1)}, u32[]{:S(2)}, u32[]{:S(2)}) collective-permute-start(bf16[1024,128]{1,0:T(8,128)(2,1)} %copy-done.7), channel_id=1, source_target_pairs={{0,8},{1,9},{2,10},{3,11},{4,12},{5,13},{6,14},{7,15},{8,0},{9,1},... | collective-permute-start | bytes 786440 | tf_op jit(solution)/shard_map/ppermute | solution.py:36
  126.1 39.2 %collective-permute-done.3.partner = bf16[1024,128]{1,0:T(8,128)(2,1)} collective-permute-done((bf16[1024,128]{1,0:T(8,128)(2,1)}, bf16[1024,128]{1,0:T(8,128)(2,1)}, u32[]{:S(2)}, u32[]{:S(2)}) %collective-permute-start.3) | collective-permute-done | bytes 262176 | tf_op jit(solution)/shard_map/ppermute | solution.py:36
  165.2 1.0 broadcast_select_fusion.1
  166.2 7.2 %collective-permute-start.4 = (bf16[1024,128]{1,0:T(8,128)(2,1)S(1)}, bf16[1024,128]{1,0:T(8,128)(2,1)S(1)}, u32[]{:S(2)}, u32[]{:S(2)}) collective-permute-start(bf16[1024,128]{1,0:T(8,128)(2,1)S(1)} %broadcast_select_fusion.1), channel_id=1, source_target_pairs={{0,16},{1,17},{2,18},{3,19},{4,20},{5,21},{6,22},{7,23},{16,32},{1... | collective-permute-start | bytes 786440 | tf_op jit(solution)/shard_map/ppermute | solution.py:36
  173.4 1.1 copy-done.2
  174.5 1.1 copy-done.4
  175.7 1.1 copy-done.6
  176.8 1.6 shard_map.148.own
  178.5 1.5 collective-permute-start.6
  180.0 2.9 %shard_map.143 = bf16[1024,128]{1,0:T(8,128)(2,1)S(1)} custom-call(s32[6]{0:T(128)S(1)} %stack.27.meta, s32[1,128]{1,0:T(1,128)S(1)} %copy-done.34, bf16[1024,128]{1,0:T(8,128)(2,1)S(1)} %copy-done.8, bf16[1024,128]{1,0:T(8,128)(2,1)} %collective-permute-done.3.partner), custom_call_target="tpu_custom_call" | custom-call | tf_op jit(solution)/shard_map/pallas_call | solution.py:445
  182.9 0.6 copy-done.17
  183.5 4.7 %shard_map.145 = bf16[4,1024,128]{2,1,0:T(8,128)(2,1)S(1)} custom-call(bf16[1024,128]{1,0:T(8,128)(2,1)S(1)} %copy-done.16, bf16[1024,128]{1,0:T(8,128)(2,1)S(1)} %broadcast_select_fusion.kv, f32[1024,128]{1,0:T(8,128)S(1)} %copy-done.10, f32[1024,128]{1,0:T(8,128)S(1)} %copy-done.19, f32[1024,128]{1,0:T(8,128)S(1)} %copy-done.21, f32[1024,128]{1,0:T(8,128)S(1)} %copy-done.23), custom_call_target="tpu_custom_call" | custom-call | tf_op jit(solution)/shard_map/pallas_call | solution.py:456
  188.3 1.0 copy-done
  189.3 5.8 %collective-permute-start.7 = (bf16[2304,512]{1,0:T(8,128)(2,1)}, bf16[2304,512]{1,0:T(8,128)(2,1)}, u32[]{:S(2)}, u32[]{:S(2)}) collective-permute-start(bf16[2304,512]{1,0:T(8,128)(2,1)} %bitcast.16.other), channel_id=1, source_target_pairs={{0,1},{2,3},{4,5},{6,7},{9,8},{11,10},{13,12},{15,14},{16,17},{18,... | collective-permute-start | bytes 7077896 | tf_op jit(solution)/shard_map/ppermute | solution.py:36
  195.0 4.5 %all-to-all-start.2 = ((bf16[4,1024,128]{2,1,0:T(8,128)(2,1)}), bf16[4,1024,128]{2,1,0:T(8,128)(2,1)}, u32[]{:S(2)}, u32[]{:S(2)}) async-start(bf16[4,1024,128]{2,1,0:T(8,128)(2,1)} %copy-done), calls=%async_computation.2 | async-start | bytes 2097152 | tf_op jit(solution)/shard_map/all_to_all | solution.py:466
  199.6 2.2 shard_map.146
  201.8 1.0 copy-done.13
  202.8 0.6 copy-done.26
  203.4 0.6 copy-done.28
  204.1 8.8 %all-to-all-done.2.heads = bf16[4,1024,128]{2,1,0:T(8,128)(2,1)} async-done(((bf16[4,1024,128]{2,1,0:T(8,128)(2,1)}), bf16[4,1024,128]{2,1,0:T(8,128)(2,1)}, u32[]{:S(2)}, u32[]{:S(2)}) %all-to-all-start.2) | async-done | bytes 1048608 | tf_op jit(solution)/shard_map/all_to_all | solution.py:466
  212.8 1.0 copy-done.27
  213.8 0.9 copy-done.29
  214.7 1.6 shard_map.147
  216.4 1.9 collective-permute-start.5
  218.3 3.4 %all-to-all-start.5 = ((bf16[8,128,128]{2,1,0:T(8,128)(2,1)}), bf16[8,128,128]{2,1,0:T(8,128)(2,1)S(1)}, u32[]{:S(2)}, u32[]{:S(2)}) async-start(bf16[8,128,128]{2,1,0:T(8,128)(2,1)} %bitcast.27), calls=%async_computation.5 | async-start | bytes 524288 | tf_op jit(solution)/shard_map/all_to_all | solution.py:452
  221.8 1.0 copy-done.12
  222.8 7.5 %shard_map.149 = (bf16[128,1536]{1,0:T(8,128)(2,1)S(1)}, bf16[384,1536]{1,0:T(8,128)(2,1)}) custom-call(s32[6]{0:T(128)S(1)} %stack.27.meta, bf16[512,512]{1,0:T(8,128)(2,1)S(1)} %get-tuple-element.38.keep, bf16[512,512]{1,0:T(8,128)(2,1)S(1)} %collective-permute-done.5.got, bf16[1024,1536]{1,0:T(8,128)(2,1)} %all-gather.2.cloned.1.call-done.wo_all, ...), custom_call_target="tpu_custom_call" | custom-call | tf_op jit(solution)/shard_map/pallas_call | solution.py:476
  230.3 4.7 %all-to-all-start.4 = ((bf16[8,48,1536]{2,1,0:T(8,128)(2,1)}), bf16[8,48,1536]{2,1,0:T(8,128)(2,1)S(1)}, u32[]{:S(2)}, u32[]{:S(2)}) async-start(bf16[8,48,1536]{2,1,0:T(8,128)(2,1)} %bitcast.17), calls=%async_computation.4 | async-start | bytes 2359296 | tf_op jit(solution)/shard_map/all_to_all | solution.py:489
  235.1 0.9 shard_map.151
  235.9 16.5 %all-to-all-done.4 = bf16[8,48,1536]{2,1,0:T(8,128)(2,1)S(1)} async-done(((bf16[8,48,1536]{2,1,0:T(8,128)(2,1)}), bf16[8,48,1536]{2,1,0:T(8,128)(2,1)S(1)}, u32[]{:S(2)}, u32[]{:S(2)}) %all-to-all-start.4) | async-done | bytes 1179680 | tf_op jit(solution)/shard_map/all_to_all | solution.py:489
  252.4 1.4 shard_map.150
  (71 shorter events, 0.3 us)
Async XLA Ops:
  7.3 1.0 copy-start.11
  8.3 0.7 copy-start.30
  8.9 0.7 copy-start.33
  9.6 6.2 %copy-start.1 = (bf16[1536,256]{1,0:T(8,128)(2,1)S(1)}, bf16[1536,256]{1,0:T(8,128)(2,1)}, u32[]{:S(2)}) copy-start(bf16[1536,256]{1,0:T(8,128)(2,1)} %gate.2) | copy-start | bytes 2359300
  9.6 6.2 %copy-start.3 = (bf16[1536,256]{1,0:T(8,128)(2,1)S(1)}, bf16[1536,256]{1,0:T(8,128)(2,1)}, u32[]{:S(2)}) copy-start(bf16[1536,256]{1,0:T(8,128)(2,1)} %up.2) | copy-start | bytes 2359300
  11.5 61.7 %all-to-all-start = ((bf16[4,144,1536]{2,1,0:T(8,128)(2,1)}), bf16[4,144,1536]{2,1,0:T(8,128)(2,1)S(1)}, u32[]{:S(2)}, u32[]{:S(2)}) async-start(bf16[4,144,1536]{2,1,0:T(8,128)(2,1)} %shard_map.140), calls=%async_computation | async-start | bytes 3538944 | tf_op jit(solution)/shard_map/all_to_all | solution.py:403
  15.8 1.1 copy-start.5
  18.3 53.6 %collective-permute-start.1 = (bf16[288,512]{1,0:T(8,128)(2,1)}, bf16[288,512]{1,0:T(8,128)(2,1)S(1)}, u32[]{:S(2)}, u32[]{:S(2)}) collective-permute-start(bf16[288,512]{1,0:T(8,128)(2,1)} %shard_map.141), channel_id=1, source_target_pairs={{0,8},{1,9},{2,10},{3,11},{4,12},{5,13},{6,14},{7,15},{8,0},{9,1},... | collective-permute-start | bytes 884744 | tf_op jit(solution)/shard_map/ppermute | solution.py:36
  34.8 37.1 %collective-permute-start = (bf16[48,1536]{1,0:T(8,128)(2,1)S(1)}, bf16[48,1536]{1,0:T(8,128)(2,1)S(1)}, u32[]{:S(2)}, u32[]{:S(2)}) collective-permute-start(bf16[48,1536]{1,0:T(8,128)(2,1)S(1)} %pad_maximum_fusion.1), channel_id=1, source_target_pairs={{0,8},{1,9},{2,10},{3,11},{4,12},{5,13},{6,14},{7,15},{8,0},{9,1},... | collective-permute-start | bytes 442376 | tf_op jit(solution)/shard_map/ppermute | solution.py:36
  71.8 0.7 copy-start.37
  72.5 0.7 copy-start.35
  73.2 20.2 %collective-permute-start.2 = (bf16[4,144,1536]{2,1,0:T(8,128)(2,1)S(1)}, bf16[4,144,1536]{2,1,0:T(8,128)(2,1)S(1)}, u32[]{:S(2)}, u32[]{:S(2)}) collective-permute-start(bf16[4,144,1536]{2,1,0:T(8,128)(2,1)S(1)} %all-to-all-done.near), channel_id=1, source_target_pairs={{0,1},{1,0},{2,3},{3,2},{4,5},{5,4},{6,7},{7,6},{8,9},{9,8},{10,11... | collective-permute-start | bytes 5308424 | tf_op jit(solution)/shard_map/ppermute | solution.py:36
  76.9 15.4 %all-to-all-start.1 = ((bf16[4,48,1536]{2,1,0:T(8,128)(2,1)}), bf16[4,48,1536]{2,1,0:T(8,128)(2,1)}, u32[]{:S(2)}, u32[]{:S(2)}) async-start(bf16[4,48,1536]{2,1,0:T(8,128)(2,1)} %broadcast_in_dim.22), calls=%async_computation.1 | async-start | bytes 1179648 | tf_op jit(solution)/shard_map/all_to_all | solution.py:65
  93.4 4.8 %copy-start.31 = (s32[128,2]{0,1:T(2,128)S(1)}, s32[128,2]{0,1:T(2,128)}, u32[]{:S(2)}) copy-start(s32[128,2]{0,1:T(2,128)} %param.20) | copy-start | bytes 3076
  93.4 0.9 copy-start.24
  94.3 0.9 copy-start.25
  95.3 9.9 %copy-start.36 = (bf16[288,512]{1,0:T(8,128)(2,1)S(1)}, bf16[288,512]{1,0:T(8,128)(2,1)}, u32[]{:S(2)}) copy-start(bf16[288,512]{1,0:T(8,128)(2,1)} %copy-done.35) | copy-start | bytes 884740
  98.2 3.8 %copy-start.9 = (f32[1024,128]{1,0:T(8,128)}, f32[1024,128]{1,0:T(8,128)S(1)}, u32[]{:S(2)}) copy-start(f32[1024,128]{1,0:T(8,128)S(1)} %get-tuple-element.31.start) | copy-start | bytes 1572868
  98.2 6.9 %copy-start.15 = (bf16[1024,128]{1,0:T(8,128)(2,1)}, bf16[1024,128]{1,0:T(8,128)(2,1)S(1)}, u32[]{:S(2)}) copy-start(bf16[1024,128]{1,0:T(8,128)(2,1)S(1)} %get-tuple-element.30.q) | copy-start | bytes 786436
  102.0 0.7 copy-start.7
  102.7 0.8 copy-start.18
  103.5 0.8 copy-start.20
  104.3 0.8 copy-start.22
  106.9 82.4 %all-to-all-start.3 = ((bf16[8,288,512]{2,1,0:T(8,128)(2,1)}), bf16[8,288,512]{2,1,0:T(8,128)(2,1)}, u32[]{:S(2)}, u32[]{:S(2)}) async-start(bf16[8,288,512]{2,1,0:T(8,128)(2,1)} %broadcast_in_dim.25), calls=%async_computation.3 | async-start | bytes 4718592 | tf_op jit(solution)/shard_map/all_to_all | solution.py:65
  111.2 110.6 %all-gather.2.cloned.1.call-start = ((), (), s32[]{:S(2)}) async-start(), calls=%async_computation.6 | async-start | bytes 3538944 | tf_op jit(solution)/shard_map/all_gather | solution.py:419
  113.9 51.3 %collective-permute-start.3 = (bf16[1024,128]{1,0:T(8,128)(2,1)}, bf16[1024,128]{1,0:T(8,128)(2,1)}, u32[]{:S(2)}, u32[]{:S(2)}) collective-permute-start(bf16[1024,128]{1,0:T(8,128)(2,1)} %copy-done.7), channel_id=1, source_target_pairs={{0,8},{1,9},{2,10},{3,11},{4,12},{5,13},{6,14},{7,15},{8,0},{9,1},... | collective-permute-start | bytes 786440 | tf_op jit(solution)/shard_map/ppermute | solution.py:36
  166.2 16.6 %collective-permute-start.4 = (bf16[1024,128]{1,0:T(8,128)(2,1)S(1)}, bf16[1024,128]{1,0:T(8,128)(2,1)S(1)}, u32[]{:S(2)}, u32[]{:S(2)}) collective-permute-start(bf16[1024,128]{1,0:T(8,128)(2,1)S(1)} %broadcast_select_fusion.1), channel_id=1, source_target_pairs={{0,16},{1,17},{2,18},{3,19},{4,20},{5,21},{6,22},{7,23},{16,32},{1... | collective-permute-start | bytes 786440 | tf_op jit(solution)/shard_map/ppermute | solution.py:36
  173.4 1.1 copy-start.2
  174.5 1.1 copy-start.4
  175.7 1.1 copy-start.6
  176.8 3.1 %copy-start.8 = (bf16[1024,128]{1,0:T(8,128)(2,1)S(1)}, bf16[1024,128]{1,0:T(8,128)(2,1)}, u32[]{:S(2)}) copy-start(bf16[1024,128]{1,0:T(8,128)(2,1)} %copy-done.7) | copy-start | bytes 786436
  176.8 3.1 %copy-start.34 = (s32[1,128]{1,0:T(1,128)S(1)}, s32[1,128]{1,0:T(1,128)}, u32[]{:S(2)}) copy-start(s32[1,128]{1,0:T(1,128)} %table.1) | copy-start | bytes 1540
  176.8 6.7 %copy-start.10 = (f32[1024,128]{1,0:T(8,128)S(1)}, f32[1024,128]{1,0:T(8,128)}, u32[]{:S(2)}) copy-start(f32[1024,128]{1,0:T(8,128)} %copy-done.9) | copy-start | bytes 1572868
  176.8 6.7 %copy-start.16 = (bf16[1024,128]{1,0:T(8,128)(2,1)S(1)}, bf16[1024,128]{1,0:T(8,128)(2,1)}, u32[]{:S(2)}) copy-start(bf16[1024,128]{1,0:T(8,128)(2,1)} %copy-done.15) | copy-start | bytes 786436
  176.8 6.7 %copy-start.19 = (f32[1024,128]{1,0:T(8,128)S(1)}, f32[1024,128]{1,0:T(8,128)}, u32[]{:S(2)}) copy-start(f32[1024,128]{1,0:T(8,128)} %copy-done.18) | copy-start | bytes 1572868
  176.8 6.7 %copy-start.21 = (f32[1024,128]{1,0:T(8,128)S(1)}, f32[1024,128]{1,0:T(8,128)}, u32[]{:S(2)}) copy-start(f32[1024,128]{1,0:T(8,128)} %copy-done.20) | copy-start | bytes 1572868
  176.8 6.7 %copy-start.23 = (f32[1024,128]{1,0:T(8,128)S(1)}, f32[1024,128]{1,0:T(8,128)}, u32[]{:S(2)}) copy-start(f32[1024,128]{1,0:T(8,128)} %copy-done.22) | copy-start | bytes 1572868
  178.5 43.3 %collective-permute-start.6 = (bf16[2304,512]{1,0:T(8,128)(2,1)}, bf16[2304,512]{1,0:T(8,128)(2,1)}, u32[]{:S(2)}, u32[]{:S(2)}) collective-permute-start(bf16[2304,512]{1,0:T(8,128)(2,1)} %shard_map.148.own), channel_id=1, source_target_pairs={{1,0},{3,2},{5,4},{7,6},{8,9},{10,11},{12,13},{14,15},{17,16},{19,... | collective-permute-start | bytes 7077896 | tf_op jit(solution)/shard_map/ppermute | solution.py:36
  182.8 0.7 copy-start.17
  188.3 1.0 copy-start
  189.3 32.6 %collective-permute-start.7 = (bf16[2304,512]{1,0:T(8,128)(2,1)}, bf16[2304,512]{1,0:T(8,128)(2,1)}, u32[]{:S(2)}, u32[]{:S(2)}) collective-permute-start(bf16[2304,512]{1,0:T(8,128)(2,1)} %bitcast.16.other), channel_id=1, source_target_pairs={{0,1},{2,3},{4,5},{6,7},{9,8},{11,10},{13,12},{15,14},{16,17},{18,... | collective-permute-start | bytes 7077896 | tf_op jit(solution)/shard_map/ppermute | solution.py:36
  195.0 17.8 %all-to-all-start.2 = ((bf16[4,1024,128]{2,1,0:T(8,128)(2,1)}), bf16[4,1024,128]{2,1,0:T(8,128)(2,1)}, u32[]{:S(2)}, u32[]{:S(2)}) async-start(bf16[4,1024,128]{2,1,0:T(8,128)(2,1)} %copy-done), calls=%async_computation.2 | async-start | bytes 2097152 | tf_op jit(solution)/shard_map/all_to_all | solution.py:466
  199.6 22.2 %copy-start.38 = (f32[1536]{0:T(1024)S(1)}, f32[1536]{0:T(1024)}, u32[]{:S(2)}) copy-start(f32[1536]{0:T(1024)} %param.15) | copy-start | bytes 18436
  201.8 1.0 copy-start.13
  202.8 0.6 copy-start.26
  203.4 0.6 copy-start.28
  212.8 9.0 %copy-start.14 = (bf16[384,1536]{1,0:T(8,128)(2,1)S(1)}, bf16[384,1536]{1,0:T(8,128)(2,1)}, u32[]{:S(2)}) copy-start(bf16[384,1536]{1,0:T(8,128)(2,1)} %copy-done.13) | copy-start | bytes 3538948
  212.8 1.0 copy-start.27
  213.8 0.9 copy-start.29
  216.4 5.4 %collective-permute-start.5 = (bf16[512,512]{1,0:T(8,128)(2,1)S(1)}, bf16[512,512]{1,0:T(8,128)(2,1)S(1)}, u32[]{:S(2)}, u32[]{:S(2)}) collective-permute-start(bf16[512,512]{1,0:T(8,128)(2,1)S(1)} %get-tuple-element.39), channel_id=1, source_target_pairs={{0,1},{1,0},{2,3},{3,2},{4,5},{5,4},{6,7},{7,6},{8,9},{9,8},{10,11... | collective-permute-start | bytes 1572872 | tf_op jit(solution)/shard_map/ppermute | solution.py:36
  218.3 12.0 %all-to-all-start.5 = ((bf16[8,128,128]{2,1,0:T(8,128)(2,1)}), bf16[8,128,128]{2,1,0:T(8,128)(2,1)S(1)}, u32[]{:S(2)}, u32[]{:S(2)}) async-start(bf16[8,128,128]{2,1,0:T(8,128)(2,1)} %bitcast.27), calls=%async_computation.5 | async-start | bytes 524288 | tf_op jit(solution)/shard_map/all_to_all | solution.py:452
  221.8 1.0 copy-start.12
  230.3 22.1 %copy-start.32 = (f32[128,2]{0,1:T(2,128)S(1)}, f32[128,2]{0,1:T(2,128)}, u32[]{:S(2)}) copy-start(f32[128,2]{0,1:T(2,128)} %param.21) | copy-start | bytes 3076
  230.3 22.1 %all-to-all-start.4 = ((bf16[8,48,1536]{2,1,0:T(8,128)(2,1)}), bf16[8,48,1536]{2,1,0:T(8,128)(2,1)S(1)}, u32[]{:S(2)}, u32[]{:S(2)}) async-start(bf16[8,48,1536]{2,1,0:T(8,128)(2,1)} %bitcast.17), calls=%async_computation.4 | async-start | bytes 2359296 | tf_op jit(solution)/shard_map/all_to_all | solution.py:489
Sparse Core Ops, SparseCore 0:
  114.7 35.9 all-gather.1

commit v4 on v3

--- a/solution.py
+++ b/solution.py
@@ -9,8 +9,8 @@
 from jax.sharding import Mesh
 from jax.sharding import PartitionSpec as P
 
-AXES = ("y", "zq", "zp", "zh", "x", "c")
-SIZES = (4, 4, 2, 2, 4, 2)
+AXES = ("y", "zq", "zr", "zp", "zh", "x", "c")
+SIZES = (4, 2, 2, 2, 2, 4, 2)
 FLAT = (4, 8, 2, 4, 2)
 ROW = ("x", "c")
 PAGE = 16
@@ -44,6 +44,10 @@
     return permute(block, lambda y, zl, zh, x, c: (y, zl, 1 - zh, x, c))
 
 
+def swap_near(block):
+    return permute(block, lambda y, zl, zh, x, c: (y, zl ^ 1, zh, x, c))
+
+
 def next_group(block):
     def target(y, zl, zh, x, c):
         if zl < 7:
@@ -51,6 +55,10 @@
         return (y + 1, 0, 0, x, c) if zh == 1 and y < 3 else None
 
     return permute(block, target)
+
+
+def ahead_x(block, step):
+    return permute(block, lambda y, zl, zh, x, c: (y, zl, zh, (x - step) % 4, c))
 
 
 def give_half(block, near):
@@ -106,25 +114,24 @@
     pieces = jnp.where(row == 0, back >> 5, jnp.where(row == 1, back & 31, 0))
     pieces = jnp.where(row == 2, ids[0:1], jnp.where(row == 3, ids[1:2], pieces))
     pieces = pieces.astype(F32).astype(BF16)
-    for copy in range(4):
-        out[copy, :TOK] = tokens[...]
-        out[copy, TOK:, :TOK] = pieces
-        out[copy, TOK:, TOK:] = jnp.zeros((16, WIDTH - TOK), BF16)
-
-
-def eighth_kernel(meta, gate, up, down, out, sems):
-    piece = meta[0] * 2 + lax.rem(meta[1], 2)
-    wide = pl.ds(pl.multiple_of(piece * 192, 64), 192)
-    deep = pl.ds(pl.multiple_of(piece * 32, 32), 32)
+    out[:TOK] = tokens[...]
+    out[TOK:, :TOK] = pieces
+    out[TOK:, TOK:] = jnp.zeros((16, WIDTH - TOK), BF16)
+
+
+def piece_kernel(meta, gate, up, down, out, sems):
+    piece = meta[0] * 4 + lax.rem(meta[1], 4)
+    wide = pl.ds(pl.multiple_of(piece * 96, 32), 96)
+    deep = pl.ds(pl.multiple_of(piece * 16, 16), 16)
     copies = [
-        pltpu.make_async_copy(gate.at[wide], out.at[:192, :256], sems.at[0]),
-        pltpu.make_async_copy(up.at[wide], out.at[:192, 256:], sems.at[1]),
+        pltpu.make_async_copy(gate.at[wide], out.at[:96, :256], sems.at[0]),
+        pltpu.make_async_copy(up.at[wide], out.at[:96, 256:], sems.at[1]),
     ]
     for i in range(3):
         copies.append(
             pltpu.make_async_copy(
                 down.at[deep, i * 512 : i * 512 + 512],
-                out.at[192 + 32 * i : 224 + 32 * i],
+                out.at[96 + 16 * i : 112 + 16 * i],
                 sems.at[2 + i],
             )
         )
@@ -135,36 +142,38 @@
 
 
 def order_kernel(gate, up, down, out):
-    for e in range(8):
-        low = e * 288
-        out[low : low + 192, :256] = gate[e * 192 : e * 192 + 192]
-        out[low : low + 192, 256:] = up[e * 192 : e * 192 + 192]
+    for e in range(16):
+        low = e * 144
+        out[low : low + 96, :256] = gate[e * 96 : e * 96 + 96]
+        out[low : low + 96, 256:] = up[e * 96 : e * 96 + 96]
         for i in range(3):
-            out[low + 192 + 32 * i : low + 224 + 32 * i] = down[
-                e * 32 : e * 32 + 32, i * 512 : i * 512 + 512
+            out[low + 96 + 16 * i : low + 112 + 16 * i] = down[
+                e * 16 : e * 16 + 16, i * 512 : i * 512 + 512
             ]
 
 
-def project_kernel(meta, near, across, wq, wkv, far, gain, q_out, kv_out, start_out, cols):
-    zh, c = meta[2], meta[4]
+def project_kernel(meta, b0, b1, b2, b3, s0, s1, s2, s3, wq, wkv, far, gain,
+                   q_out, kv_out, start_out, cols):
+    zh, x, c = meta[2], meta[3], meta[4]
     cols[0:64] = wq[...]
     cols[64:128] = far[0:64]
     cols[pl.ds(pl.multiple_of(128 + zh * 64, 64), 64), :] = wkv[...]
     cols[pl.ds(pl.multiple_of(192 - zh * 64, 64), 64), :] = far[64:128]
     for k in range(4):
-        for block, core in ((near, c), (across, 1 - c)):
-            low = pl.multiple_of((2 * k + core) * TOK, TOK)
-            normed = rms(block[k, :TOK].astype(F32), gain[...])
+        place = lax.rem(x + k, 4) * 2
+        for block, core in (((b0, b1, b2, b3)[k], c), ((s0, s1, s2, s3)[k], 1 - c)):
+            low = pl.multiple_of((place + core) * TOK, TOK)
+            normed = rms(block[:TOK].astype(F32), gain[...])
             result = dot_nt(normed, cols[...]).astype(BF16)
             q_out[pl.ds(low, TOK), :] = result[:, :128]
             kv_out[pl.ds(low, TOK), :] = result[:, 128:]
-            pieces = block[k, TOK:, :TOK].astype(F32)
+            pieces = block[TOK:, :TOK].astype(F32)
             back = column(pieces[0:1] * 32.0 + pieces[1:2])
             own = (low + lax.broadcasted_iota(I32, (TOK, TOK), 0)).astype(F32)
             start_out[pl.ds(low, TOK), :] = own - back
 
 
-def route_kernel(meta, near, across, pick_out, other_out, rows_out):
+def route_kernel(meta, b0, b1, b2, b3, s0, s1, s2, s3, pick_out, other_out, rows_out):
     x, c = meta[3], meta[4]
     before = lax.broadcasted_iota(I32, (TOK, TOK), 0) < lax.broadcasted_iota(I32, (TOK, TOK), 1)
     before = before.astype(F32).astype(BF16)
@@ -172,9 +181,10 @@
     for expert, out in ((x + 4 * c, pick_out), (x + 4 * (1 - c), other_out)):
         number = expert.astype(F32)
         for k in range(4):
-            for block, core in ((near, c), (across, 1 - c)):
-                low = pl.multiple_of((2 * k + core) * CAP, 16)
-                pieces = block[k, TOK:, :TOK].astype(F32)
+            place = lax.rem(x + k, 4) * 2
+            for block, core in (((b0, b1, b2, b3)[k], c), ((s0, s1, s2, s3)[k], 1 - c)):
+                low = pl.multiple_of((place + core) * CAP, 16)
+                pieces = block[TOK:, :TOK].astype(F32)
                 named = (pieces == number).astype(F32)
                 named = named[2:3] + named[3:4]
                 rank = jnp.dot(
@@ -185,7 +195,7 @@
                 pick = jnp.where((row == rank) & (named > 0.0), 1.0, 0.0).astype(BF16)
                 out[pl.ds(low, CAP), :] = pick
                 if out is pick_out:
-                    chosen = jnp.dot(pick, block[k, :TOK], preferred_element_type=F32)
+                    chosen = jnp.dot(pick, block[:TOK], preferred_element_type=F32)
                     rows_out[pl.ds(low, CAP), :] = chosen.astype(BF16)
 
 
@@ -338,12 +348,12 @@
     acts = []
     for half, source in enumerate((own, given_a)):
         pltpu.make_async_copy(source, raw.at[half], sems.at[half]).wait()
-        for e in range(8):
-            low = e * 288
-            wide[half, e * 192 : e * 192 + 192] = raw[half, low : low + 192]
+        for e in range(16):
+            low = e * 144
+            wide[half, e * 96 : e * 96 + 96] = raw[half, low : low + 96]
             for i in range(3):
-                deep[half, i * 256 + e * 32 : i * 256 + e * 32 + 32] = raw[
-                    half, low + 192 + 32 * i : low + 224 + 32 * i
+                deep[half, i * 256 + e * 16 : i * 256 + e * 16 + 16] = raw[
+                    half, low + 96 + 16 * i : low + 112 + 16 * i
                 ]
         both = jnp.dot(arrived, wide[half], preferred_element_type=F32)
         gate, up = both[:, :256], both[:, 256:]
@@ -379,8 +389,8 @@
     w_down,
     page_table,
 ):
-    y, zq, zp, zh, x, c = (lax.axis_index(name) for name in AXES)
-    zl = zq * 2 + zp
+    y, zq, zr, zp, zh, x, c = (lax.axis_index(name) for name in AXES)
+    zl = zq * 4 + zr * 2 + zp
     place = (((y * 8 + zl) * 2 + zh) * 4 + x) * 2 + c
     meta = jnp.stack([y, zl, zh, x, c, place]).astype(I32)
     wq, wkv = w_query.T, key_value_weight.T
@@ -391,30 +401,32 @@
     )
     parts = swap_half(parts)
     (block,) = call(
-        pack_kernel, [((4, TOK + 16, WIDTH), BF16)], [SMEM] + [VMEM] * 3, nbytes=0
+        pack_kernel, [((TOK + 16, WIDTH), BF16)], [SMEM] + [VMEM] * 3, nbytes=0
     )(meta, tokens, segment_ids[None, :], ids)
-    (eighth,) = call(
-        eighth_kernel,
-        [((288, 512), BF16)],
+    (piece,) = call(
+        piece_kernel,
+        [((144, 512), BF16)],
         [SMEM] + [ANY] * 3,
         scratch=[pltpu.SemaphoreType.DMA((5,))],
         nbytes=0,
     )(meta, w_gate, w_up, w_down)
-    near = lax.all_to_all(block, "x", split_axis=0, concat_axis=0, tiled=True)
-    eighth = swap_half(eighth)
-    near, parts, eighth = lax.optimization_barrier((near, parts, eighth))
+    one, three, two = [ahead_x(block, step) for step in (1, 3, 2)]
+    piece = swap_half(piece)
+    one, two, three, parts, piece = lax.optimization_barrier((one, two, three, parts, piece))
     parts = gather(parts, "y").reshape(4, 3, 16, WIDTH)
     far_cols = parts[:, :2].transpose(1, 0, 2, 3).reshape(128, WIDTH)
-    across = swap_core(near)
-    gain = attn_gain[None, :]
+    near = [block, one, two, three]
+    across = [swap_core(b) for b in near]
+    beside = swap_near(piece)
+    gain, beside = lax.optimization_barrier((attn_gain[None, :], beside))
     q, kv, start = call(
         project_kernel,
         [((ROWS, 128), BF16), ((ROWS, 128), BF16), ((ROWS, 128), F32)],
-        [SMEM] + [VMEM] * 6,
+        [SMEM] + [VMEM] * 12,
         scratch=[pltpu.VMEM((256, WIDTH), BF16)],
         flops=0,
         nbytes=0,
-    )(meta, near, across, wq, wkv, far_cols, gain)
+    )(meta, *near, *across, wq, wkv, far_cols, gain)
     out_rows = jnp.concatenate([w_out, parts[:, 2].reshape(64, WIDTH)], axis=0)
     out_all = lax.all_gather(out_rows, ROW, axis=0, tiled=True)
 
@@ -424,24 +436,32 @@
         [((ROWS, 128), F32)] * 3 + [((8, TOK), I32)],
         [VMEM] * 4,
         scratch=[pltpu.VMEM((ROWS, 128), BF16)] * 2,
-        flops=0,
-        nbytes=0,
+        flops=4000000000,
+        nbytes=3000000,
     )(q, kv, start, ids)
     pick, other_pick, chosen = call(
         route_kernel,
         [((8 * CAP, TOK), BF16)] * 2 + [((8 * CAP, WIDTH), BF16)],
-        [SMEM] + [VMEM] * 2,
-        flops=0,
-        nbytes=0,
-    )(meta, after(near, sums), across)
-
-    (own,) = call(order_kernel, [((2304, 512), BF16)], [VMEM] * 3, nbytes=0)(
-        *(after(w, sums) for w in (w_gate, w_up, w_down))
-    )
+        [SMEM] + [VMEM] * 8,
+        flops=2000000000,
+        nbytes=5000000,
+    )(meta, after(block, kv), *near[1:], *across)
+
+    (own,) = call(order_kernel, [((2304, 512), BF16)], [VMEM] * 3, nbytes=5000000)(
+        *(after(w, kv) for w in (w_gate, w_up, w_down))
+    )
+    pair = jnp.where(
+        zp == 0,
+        jnp.concatenate([piece, beside], axis=0),
+        jnp.concatenate([beside, piece], axis=0),
+    )
+    partner, sums, pick, own, out_all, pair = lax.optimization_barrier(
+        (partner, sums, pick, own, out_all, pair)
+    )
+    onward = jnp.where(zh == 0, partner, kv)
+    shifted = next_group(onward)
     given_a = give_half(own, True)
-    other = gather(after(eighth, sums), ("y", "zp")).reshape(2304, 512)
-
-    shifted = next_group(jnp.where(zh == 0, partner, kv))
+    other = gather(pair, ("y", "zr")).reshape(2304, 512)
     (pages,) = call(
         page_kernel,
         [((ROWS, 128), BF16)],
@@ -497,7 +517,7 @@
 
 def solution(mesh):
     fine = Mesh(mesh.devices.reshape(SIZES), AXES)
-    grp, tp = ("y", "zq", "zp"), ("zh", "x", "c")
+    grp, tp = ("y", "zq", "zr", "zp"), ("zh", "x", "c")
     in_specs = (
         P(AXES, None),
         P(),

time: 262 us -> 272 us (1.038)
  the two profiles are of different devices: /device:TPU:32 before, /device:TPU:64 now
where the time goes in v4:
time: 272 us; the launch traced here: 271 us
  starting transfers between devices  95.1 us (35%)
  waiting for transfers between devices  77.9 us (29%)
  Pallas kernels  30 us (11%)
  blocking collectives  29.1 us (11%)
  local copies, waits for them, and re-layouts  22 us (8%)
  between operations  14.8 us (5%)
    ppermute x15, starting transfers between devices, permute(): return lax.ppermute(block, AXES, route)  67.1 us
    ppermute x15, waiting for transfers between devices, permute(): return lax.ppermute(block, AXES, route)  62.3 us
    all_to_all x1, starting transfers between devices, gather(): return lax.all_to_all(wide, axis, split_axis=0, concat_axis=0, tiled=True)  19.3 us
    unnamed x92, local copies, waits for them, and re-layouts  17.2 us
    all_to_all x1, blocking collectives, body(): heads = lax.all_to_all(heads, 'x', split_axis=0, concat_axis=0, tiled=True)  15.8 us
    all_to_all x1, waiting for transfers between devices, body(): lax.all_to_all(expert_out.reshape(8, CAP, WIDTH), ROW, split_axis=0, conc...  15.6 us
    all_to_all x1, blocking collectives, gather(): return lax.all_to_all(wide, axis, split_axis=0, concat_axis=0, tiled=True)  13.3 us
    pallas_call x1, Pallas kernels, body(): call(expert_kernel, [((TOK, WIDTH), BF16), ((8 * CAP, WIDTH), BF16)], [SM...  7.53 us
  transfers between devices with their start and end apart: 19, of which 5 were waited for; matrix products, arithmetic and copies ran while one was open for 1% of the time, Pallas kernels for 10%

profile of v4, /device:TPU:64, one launch (start us, length us, event | category | flops | bytes accessed | tf_op | source)
XLA Modules:
  0.0 270.6 jit_solution(13028168349127559147)
XLA Ops:
  7.3 1.0 copy-done.7
  8.3 0.7 copy-done.39
  9.0 0.7 copy-done.41
  9.7 0.6 shard_map.140.b0
  10.2 3.4 %collective-permute-start.2 = (bf16[144,1536]{1,0:T(8,128)(2,1)S(1)}, bf16[144,1536]{1,0:T(8,128)(2,1)S(1)}, u32[]{:S(2)}, u32[]{:S(2)}) collective-permute-start(bf16[144,1536]{1,0:T(8,128)(2,1)S(1)} %shard_map.140.b0), channel_id=1, source_target_pairs={{0,2},{1,3},{2,4},{3,5},{4,6},{5,7},{6,0},{7,1},{8,10},{9,11},{10,... | collective-permute-start | bytes 1327112 | tf_op jit(solution)/shard_map/ppermute | solution.py:36
  13.6 4.6 %collective-permute-start.1 = (bf16[144,1536]{1,0:T(8,128)(2,1)S(1)}, bf16[144,1536]{1,0:T(8,128)(2,1)S(1)}, u32[]{:S(2)}, u32[]{:S(2)}) collective-permute-start(bf16[144,1536]{1,0:T(8,128)(2,1)S(1)} %shard_map.140.b0), channel_id=1, source_target_pairs={{0,4},{1,5},{2,6},{3,7},{4,0},{5,1},{6,2},{7,3},{8,12},{9,13},{10,... | collective-permute-start | bytes 1327112 | tf_op jit(solution)/shard_map/ppermute | solution.py:36
  18.3 3.3 %collective-permute-start = (bf16[144,1536]{1,0:T(8,128)(2,1)S(1)}, bf16[144,1536]{1,0:T(8,128)(2,1)S(1)}, u32[]{:S(2)}, u32[]{:S(2)}) collective-permute-start(bf16[144,1536]{1,0:T(8,128)(2,1)S(1)} %shard_map.140.b0), channel_id=1, source_target_pairs={{0,6},{1,7},{2,0},{3,1},{4,2},{5,3},{6,4},{7,5},{8,14},{9,15},{10,... | collective-permute-start | bytes 1327112 | tf_op jit(solution)/shard_map/ppermute | solution.py:36
  21.6 1.1 copy-done.1
  22.8 1.1 copy-done.3
  23.9 1.1 copy-done.5
  25.0 0.6 shard_map.141
  25.7 13.9 %collective-permute-start.4 = (bf16[144,512]{1,0:T(8,128)(2,1)S(1)}, bf16[144,512]{1,0:T(8,128)(2,1)S(1)}, u32[]{:S(2)}, u32[]{:S(2)}) collective-permute-start(bf16[144,512]{1,0:T(8,128)(2,1)S(1)} %shard_map.141), channel_id=1, source_target_pairs={{0,8},{1,9},{2,10},{3,11},{4,12},{5,13},{6,14},{7,15},{8,0},{9,1},... | collective-permute-start | bytes 442376 | tf_op jit(solution)/shard_map/ppermute | solution.py:36
  39.7 1.9 collective-permute-start.3
  41.7 9.8 %collective-permute-done.4 = bf16[144,512]{1,0:T(8,128)(2,1)S(1)} collective-permute-done((bf16[144,512]{1,0:T(8,128)(2,1)S(1)}, bf16[144,512]{1,0:T(8,128)(2,1)S(1)}, u32[]{:S(2)}, u32[]{:S(2)}) %collective-permute-start.4) | collective-permute-done | bytes 147488 | tf_op jit(solution)/shard_map/ppermute | solution.py:36
  51.4 4.8 %collective-permute-done.3 = bf16[48,1536]{1,0:T(8,128)(2,1)S(1)} collective-permute-done((bf16[48,1536]{1,0:T(8,128)(2,1)S(1)}, bf16[48,1536]{1,0:T(8,128)(2,1)S(1)}, u32[]{:S(2)}, u32[]{:S(2)}) %collective-permute-start.3) | collective-permute-done | bytes 147488 | tf_op jit(solution)/shard_map/ppermute | solution.py:36
  56.3 13.3 %all_to_all.25 = bf16[4,48,1536]{2,1,0:T(8,128)(2,1)} all-to-all(bf16[4,48,1536]{2,1,0:T(8,128)(2,1)S(1)} %broadcast_in_dim.22), channel_id=1, replica_groups=mesh['y'=4,'zq'=2,'zr'=2,'zp'=2,'zh'=2,'x'=4,'c'=2] {'y'}, dimensions={0} | all-to-all | bytes 1179648 | tf_op jit(solution)/shard_map/all_to_all | solution.py:73
  69.6 0.9 slice.9
  70.6 0.8 pad_maximum_fusion
  71.4 11.5 %collective-permute-start.9 = (bf16[144,512]{1,0:T(8,128)(2,1)S(1)}, bf16[144,512]{1,0:T(8,128)(2,1)S(1)}, u32[]{:S(2)}, u32[]{:S(2)}) collective-permute-start(bf16[144,512]{1,0:T(8,128)(2,1)S(1)} %collective-permute-done.4), channel_id=1, source_target_pairs={{0,16},{1,17},{2,18},{3,19},{4,20},{5,21},{6,22},{7,23},{8,24},{9,... | collective-permute-start | bytes 442376 | tf_op jit(solution)/shard_map/ppermute | solution.py:36
  82.9 1.9 collective-permute-start.5
  84.9 2.4 collective-permute-start.6
  87.3 1.9 collective-permute-start.7
  89.2 2.4 collective-permute-start.8
  91.7 0.8 maximum_select_fusion
  92.5 1.0 slice_bitcast_fusion
  93.6 2.9 %shard_map.142 = (bf16[1024,128]{1,0:T(8,128)(2,1)S(1)}, bf16[1024,128]{1,0:T(8,128)(2,1)S(1)}, f32[1024,128]{1,0:T(8,128)S(1)}) custom-call(s32[6]{0:T(128)S(1)} %stack.27.meta, bf16[144,1536]{1,0:T(8,128)(2,1)S(1)} %shard_map.140.b0, bf16[144,1536]{1,0:T(8,128)(2,1)S(1)} %collective-permute-done.b1, bf16[144,1536]{1,0:T(8,128)(2,1)S(1)} %collective-permute-done.1.b2, ...), custom_call_target="tpu_custom_call" | custom-call | tf_op jit(solution)/shard_map/pallas_call | solution.py:422
  96.6 11.4 %collective-permute-start.10 = (bf16[1024,128]{1,0:T(8,128)(2,1)S(1)}, bf16[1024,128]{1,0:T(8,128)(2,1)S(1)}, u32[]{:S(2)}, u32[]{:S(2)}) collective-permute-start(bf16[1024,128]{1,0:T(8,128)(2,1)S(1)} %get-tuple-element.42.kv), channel_id=1, source_target_pairs={{0,8},{1,9},{2,10},{3,11},{4,12},{5,13},{6,14},{7,15},{8,0},{9,1},... | collective-permute-start | bytes 786440 | tf_op jit(solution)/shard_map/ppermute | solution.py:36
  108.0 3.8 %shard_map.143 = (f32[1024,128]{1,0:T(8,128)S(1)}, f32[1024,128]{1,0:T(8,128)S(1)}, f32[1024,128]{1,0:T(8,128)S(1)}, s32[8,128]{1,0:T(8,128)S(1)}) custom-call(bf16[1024,128]{1,0:T(8,128)(2,1)S(1)} %get-tuple-element.52.q, bf16[1024,128]{1,0:T(8,128)(2,1)S(1)} %get-tuple-element.42.kv, f32[1024,128]{1,0:T(8,128)S(1)} %get-tuple-element.43.start, ...), custom_call_target="tpu_custom_call" | custom-call | flops 4000000000 | bytes 3000000 | tf_op jit(solution)/shard_map/pallas_call | solution.py:434
  111.9 0.8 copy-done.14
  112.7 0.8 copy-done.16
  113.5 0.8 copy-done.18
  114.3 0.7 copy-done.32
  115.0 0.2 shard_map.145.own
  115.2 0.8 copy-done.23
  116.0 0.1 copy-done.25
  116.2 0.1 copy-done.27
  116.3 0.1 copy-done.29
  116.4 2.2 shard_map.144
  118.6 1.0 copy-done.9
  119.6 0.6 copy-done.34
  120.3 0.6 copy-done.36
  120.9 0.9 collective-permute-done.10.partner
  121.8 2.7 broadcast_in_dim.25
  124.5 19.3 %all-to-all-start.2 = ((bf16[8,288,512]{2,1,0:T(8,128)(2,1)}), bf16[8,288,512]{2,1,0:T(8,128)(2,1)}, u32[]{:S(2)}, u32[]{:S(2)}) async-start(bf16[8,288,512]{2,1,0:T(8,128)(2,1)} %broadcast_in_dim.25), calls=%async_computation.2 | async-start | bytes 4718592 | tf_op jit(solution)/shard_map/all_to_all | solution.py:73
  143.8 2.1 collective-permute-start.11
  145.9 2.4 shard_map.146
  148.4 1.5 collective-permute-start.13
  149.9 46.8 %collective-permute-done.11 = bf16[1024,128]{1,0:T(8,128)(2,1)S(1)} collective-permute-done((bf16[1024,128]{1,0:T(8,128)(2,1)S(1)}, bf16[1024,128]{1,0:T(8,128)(2,1)S(1)}, u32[]{:S(2)}, u32[]{:S(2)}) %collective-permute-start.11) | collective-permute-done | bytes 262176 | tf_op jit(solution)/shard_map/ppermute | solution.py:36
  196.7 4.8 %shard_map.147 = bf16[4,1024,128]{2,1,0:T(8,128)(2,1)S(1)} custom-call(bf16[1024,128]{1,0:T(8,128)(2,1)S(1)} %copy-done.33, bf16[1024,128]{1,0:T(8,128)(2,1)S(1)} %broadcast_select_fusion.kv, f32[1024,128]{1,0:T(8,128)S(1)} %copy-done.13, f32[1024,128]{1,0:T(8,128)S(1)} %copy-done.15, f32[1024,128]{1,0:T(8,128)S(1)} %copy-done.17, f32[1024,128]{1,0:T(8,128)S(1)} %copy-done.19), custom_call_target="tpu_custom_call" | custom-call | tf_op jit(solution)/shard_map/pallas_call | solution.py:476
  201.6 2.8 %collective-permute-start.14 = (bf16[2304,512]{1,0:T(8,128)(2,1)}, bf16[2304,512]{1,0:T(8,128)(2,1)}, u32[]{:S(2)}, u32[]{:S(2)}) collective-permute-start(bf16[2304,512]{1,0:T(8,128)(2,1)} %bitcast.16.other), channel_id=1, source_target_pairs={{0,1},{2,3},{4,5},{6,7},{9,8},{11,10},{13,12},{15,14},{16,17},{18,... | collective-permute-start | bytes 7077896 | tf_op jit(solution)/shard_map/ppermute | solution.py:36
  204.4 15.8 %all_to_all.26.heads = bf16[4,1024,128]{2,1,0:T(8,128)(2,1)S(1)} all-to-all(bf16[4,1024,128]{2,1,0:T(8,128)(2,1)S(1)} %shard_map.147), channel_id=1, replica_groups=mesh['y'=4,'zq'=2,'zr'=2,'zp'=2,'zh'=2,'x'=4,'c'=2] {'x'}, dimensions={0} | all-to-all | bytes 2097152 | tf_op jit(solution)/shard_map/all_to_all | solution.py:486
  220.2 1.0 copy-done.35
  221.2 0.9 copy-done.37
  222.1 1.8 shard_map.148
  223.8 0.8 copy-done.20
  224.6 1.9 collective-permute-start.12
  226.6 4.1 %all-to-all-start.4 = ((bf16[8,128,128]{2,1,0:T(8,128)(2,1)}), bf16[8,128,128]{2,1,0:T(8,128)(2,1)}, u32[]{:S(2)}, u32[]{:S(2)}) async-start(bf16[8,128,128]{2,1,0:T(8,128)(2,1)} %bitcast.27), calls=%async_computation.4 | async-start | bytes 524288 | tf_op jit(solution)/shard_map/all_to_all | solution.py:472
  230.7 1.0 copy-done.8
  231.7 1.0 copy-done.21
  232.7 7.5 %shard_map.149 = (bf16[128,1536]{1,0:T(8,128)(2,1)S(1)}, bf16[384,1536]{1,0:T(8,128)(2,1)}) custom-call(s32[6]{0:T(128)S(1)} %stack.27.meta, bf16[512,512]{1,0:T(8,128)(2,1)S(1)} %copy-done.21, bf16[512,512]{1,0:T(8,128)(2,1)} %collective-permute-done.12.got, bf16[1024,1536]{1,0:T(8,128)(2,1)} %all-gather.2.cloned.1.call-done.wo_all, ...), custom_call_target="tpu_custom_call" | custom-call | tf_op jit(solution)/shard_map/pallas_call | solution.py:496
  240.3 4.7 %all-to-all-start.3 = ((bf16[8,48,1536]{2,1,0:T(8,128)(2,1)}), bf16[8,48,1536]{2,1,0:T(8,128)(2,1)S(1)}, u32[]{:S(2)}, u32[]{:S(2)}) async-start(bf16[8,48,1536]{2,1,0:T(8,128)(2,1)} %bitcast.17), calls=%async_computation.3 | async-start | bytes 2359296 | tf_op jit(solution)/shard_map/all_to_all | solution.py:509
  245.0 1.8 shard_map.151
  246.8 15.6 %all-to-all-done.3 = bf16[8,48,1536]{2,1,0:T(8,128)(2,1)S(1)} async-done(((bf16[8,48,1536]{2,1,0:T(8,128)(2,1)}), bf16[8,48,1536]{2,1,0:T(8,128)(2,1)S(1)}, u32[]{:S(2)}, u32[]{:S(2)}) %all-to-all-start.3) | async-done | bytes 1179680 | tf_op jit(solution)/shard_map/all_to_all | solution.py:509
  262.4 1.4 shard_map.150
  (96 shorter events, 0.5 us)
Async XLA Ops:
  7.2 114.6 %all-gather.2.cloned.1.call-start = ((), (), s32[]{:S(2)}) async-start(), calls=%async_computation.5 | async-start | bytes 3538944 | tf_op jit(solution)/shard_map/all_gather | solution.py:431
  7.3 1.0 copy-start.7
  8.3 0.7 copy-start.39
  9.0 0.7 copy-start.41
  9.6 30.0 %copy-start.30 = (bf16[1536,64]{0,1:T(8,128)(2,1)S(1)}, bf16[1536,64]{0,1:T(8,128)(2,1)}, u32[]{:S(2)}) copy-start(bf16[1536,64]{0,1:T(8,128)(2,1)} %param.16) | copy-start | bytes 589828
  9.7 30.0 %copy-start.31 = (bf16[1536,64]{0,1:T(8,128)(2,1)S(1)}, bf16[1536,64]{0,1:T(8,128)(2,1)}, u32[]{:S(2)}) copy-start(bf16[1536,64]{0,1:T(8,128)(2,1)} %param.17) | copy-start | bytes 589828
  9.7 30.0 %copy-start.43 = (bf16[64,1536]{1,0:T(8,128)(2,1)S(1)}, bf16[64,1536]{1,0:T(8,128)(2,1)}, u32[]{:S(2)}) copy-start(bf16[64,1536]{1,0:T(8,128)(2,1)} %param.18) | copy-start | bytes 589828
  10.2 46.0 %collective-permute-start.2 = (bf16[144,1536]{1,0:T(8,128)(2,1)S(1)}, bf16[144,1536]{1,0:T(8,128)(2,1)S(1)}, u32[]{:S(2)}, u32[]{:S(2)}) collective-permute-start(bf16[144,1536]{1,0:T(8,128)(2,1)S(1)} %shard_map.140.b0), channel_id=1, source_target_pairs={{0,2},{1,3},{2,4},{3,5},{4,6},{5,7},{6,0},{7,1},{8,10},{9,11},{10,... | collective-permute-start | bytes 1327112 | tf_op jit(solution)/shard_map/ppermute | solution.py:36
  13.6 42.6 %collective-permute-start.1 = (bf16[144,1536]{1,0:T(8,128)(2,1)S(1)}, bf16[144,1536]{1,0:T(8,128)(2,1)S(1)}, u32[]{:S(2)}, u32[]{:S(2)}) collective-permute-start(bf16[144,1536]{1,0:T(8,128)(2,1)S(1)} %shard_map.140.b0), channel_id=1, source_target_pairs={{0,4},{1,5},{2,6},{3,7},{4,0},{5,1},{6,2},{7,3},{8,12},{9,13},{10,... | collective-permute-start | bytes 1327112 | tf_op jit(solution)/shard_map/ppermute | solution.py:36
  18.3 38.0 %collective-permute-start = (bf16[144,1536]{1,0:T(8,128)(2,1)S(1)}, bf16[144,1536]{1,0:T(8,128)(2,1)S(1)}, u32[]{:S(2)}, u32[]{:S(2)}) collective-permute-start(bf16[144,1536]{1,0:T(8,128)(2,1)S(1)} %shard_map.140.b0), channel_id=1, source_target_pairs={{0,6},{1,7},{2,0},{3,1},{4,2},{5,3},{6,4},{7,5},{8,14},{9,15},{10,... | collective-permute-start | bytes 1327112 | tf_op jit(solution)/shard_map/ppermute | solution.py:36
  21.6 1.1 copy-start.1
  22.8 1.1 copy-start.3
  23.9 1.1 copy-start.5
  25.7 59.2 %copy-start.44 = (f32[1536]{0:T(1024)S(1)}, f32[1536]{0:T(1024)}, u32[]{:S(2)}) copy-start(f32[1536]{0:T(1024)} %param.14) | copy-start | bytes 18436
  25.7 25.7 %collective-permute-start.4 = (bf16[144,512]{1,0:T(8,128)(2,1)S(1)}, bf16[144,512]{1,0:T(8,128)(2,1)S(1)}, u32[]{:S(2)}, u32[]{:S(2)}) collective-permute-start(bf16[144,512]{1,0:T(8,128)(2,1)S(1)} %shard_map.141), channel_id=1, source_target_pairs={{0,8},{1,9},{2,10},{3,11},{4,12},{5,13},{6,14},{7,15},{8,0},{9,1},... | collective-permute-start | bytes 442376 | tf_op jit(solution)/shard_map/ppermute | solution.py:36
  39.7 16.5 %collective-permute-start.3 = (bf16[48,1536]{1,0:T(8,128)(2,1)S(1)}, bf16[48,1536]{1,0:T(8,128)(2,1)S(1)}, u32[]{:S(2)}, u32[]{:S(2)}) collective-permute-start(bf16[48,1536]{1,0:T(8,128)(2,1)S(1)} %pad_maximum_fusion.1), channel_id=1, source_target_pairs={{0,8},{1,9},{2,10},{3,11},{4,12},{5,13},{6,14},{7,15},{8,0},{9,1},... | collective-permute-start | bytes 442376 | tf_op jit(solution)/shard_map/ppermute | solution.py:36
  56.2 37.4 %copy-start.22 = (bf16[144,1536]{1,0:T(8,128)(2,1)}, bf16[144,1536]{1,0:T(8,128)(2,1)S(1)}, u32[]{:S(2)}) copy-start(bf16[144,1536]{1,0:T(8,128)(2,1)S(1)} %collective-permute-done.2.b3) | copy-start | bytes 1327108
  56.2 37.4 %copy-start.24 = (bf16[144,1536]{1,0:T(8,128)(2,1)}, bf16[144,1536]{1,0:T(8,128)(2,1)S(1)}, u32[]{:S(2)}) copy-start(bf16[144,1536]{1,0:T(8,128)(2,1)S(1)} %collective-permute-done.1.b2) | copy-start | bytes 1327108
  56.3 37.4 %copy-start.26 = (bf16[144,1536]{1,0:T(8,128)(2,1)}, bf16[144,1536]{1,0:T(8,128)(2,1)S(1)}, u32[]{:S(2)}) copy-start(bf16[144,1536]{1,0:T(8,128)(2,1)S(1)} %collective-permute-done.b1) | copy-start | bytes 1327108
  71.4 20.3 %collective-permute-start.9 = (bf16[144,512]{1,0:T(8,128)(2,1)S(1)}, bf16[144,512]{1,0:T(8,128)(2,1)S(1)}, u32[]{:S(2)}, u32[]{:S(2)}) collective-permute-start(bf16[144,512]{1,0:T(8,128)(2,1)S(1)} %collective-permute-done.4), channel_id=1, source_target_pairs={{0,16},{1,17},{2,18},{3,19},{4,20},{5,21},{6,22},{7,23},{8,24},{9,... | collective-permute-start | bytes 442376 | tf_op jit(solution)/shard_map/ppermute | solution.py:36
  82.9 10.6 %collective-permute-start.5 = (bf16[144,1536]{1,0:T(8,128)(2,1)S(1)}, bf16[144,1536]{1,0:T(8,128)(2,1)S(1)}, u32[]{:S(2)}, u32[]{:S(2)}) collective-permute-start(bf16[144,1536]{1,0:T(8,128)(2,1)S(1)} %shard_map.140.b0), channel_id=1, source_target_pairs={{0,1},{1,0},{2,3},{3,2},{4,5},{5,4},{6,7},{7,6},{8,9},{9,8},{10,11... | collective-permute-start | bytes 1327112 | tf_op jit(solution)/shard_map/ppermute | solution.py:36
  84.9 8.7 %collective-permute-start.6 = (bf16[144,1536]{1,0:T(8,128)(2,1)S(1)}, bf16[144,1536]{1,0:T(8,128)(2,1)S(1)}, u32[]{:S(2)}, u32[]{:S(2)}) collective-permute-start(bf16[144,1536]{1,0:T(8,128)(2,1)S(1)} %collective-permute-done.b1), channel_id=1, source_target_pairs={{0,1},{1,0},{2,3},{3,2},{4,5},{5,4},{6,7},{7,6},{8,9},{9,8},{10,11... | collective-permute-start | bytes 1327112 | tf_op jit(solution)/shard_map/ppermute | solution.py:36
  87.3 6.3 %collective-permute-start.7 = (bf16[144,1536]{1,0:T(8,128)(2,1)S(1)}, bf16[144,1536]{1,0:T(8,128)(2,1)S(1)}, u32[]{:S(2)}, u32[]{:S(2)}) collective-permute-start(bf16[144,1536]{1,0:T(8,128)(2,1)S(1)} %collective-permute-done.1.b2), channel_id=1, source_target_pairs={{0,1},{1,0},{2,3},{3,2},{4,5},{5,4},{6,7},{7,6},{8,9},{9,8},{10,11... | collective-permute-start | bytes 1327112 | tf_op jit(solution)/shard_map/ppermute | solution.py:36
  89.2 4.4 %collective-permute-start.8 = (bf16[144,1536]{1,0:T(8,128)(2,1)S(1)}, bf16[144,1536]{1,0:T(8,128)(2,1)S(1)}, u32[]{:S(2)}, u32[]{:S(2)}) collective-permute-start(bf16[144,1536]{1,0:T(8,128)(2,1)S(1)} %collective-permute-done.2.b3), channel_id=1, source_target_pairs={{0,1},{1,0},{2,3},{3,2},{4,5},{5,4},{6,7},{7,6},{8,9},{9,8},{10,11... | collective-permute-start | bytes 1327112 | tf_op jit(solution)/shard_map/ppermute | solution.py:36
  93.5 14.5 %copy-start.40 = (s32[128,2]{0,1:T(2,128)S(1)}, s32[128,2]{0,1:T(2,128)}, u32[]{:S(2)}) copy-start(s32[128,2]{0,1:T(2,128)} %param.20) | copy-start | bytes 3076
  93.6 14.4 %copy-start.28 = (bf16[144,1536]{1,0:T(8,128)(2,1)}, bf16[144,1536]{1,0:T(8,128)(2,1)S(1)}, u32[]{:S(2)}) copy-start(bf16[144,1536]{1,0:T(8,128)(2,1)S(1)} %collective-permute-done.5.s0) | copy-start | bytes 1327108
  96.6 15.3 %copy-start.12 = (f32[1024,128]{1,0:T(8,128)}, f32[1024,128]{1,0:T(8,128)S(1)}, u32[]{:S(2)}) copy-start(f32[1024,128]{1,0:T(8,128)S(1)} %get-tuple-element.43.start) | copy-start | bytes 1572868
  96.6 25.2 %collective-permute-start.10 = (bf16[1024,128]{1,0:T(8,128)(2,1)S(1)}, bf16[1024,128]{1,0:T(8,128)(2,1)S(1)}, u32[]{:S(2)}, u32[]{:S(2)}) collective-permute-start(bf16[1024,128]{1,0:T(8,128)(2,1)S(1)} %get-tuple-element.42.kv), channel_id=1, source_target_pairs={{0,8},{1,9},{2,10},{3,11},{4,12},{5,13},{6,14},{7,15},{8,0},{9,1},... | collective-permute-start | bytes 786440 | tf_op jit(solution)/shard_map/ppermute | solution.py:36
  108.0 7.0 %copy-start.2 = (bf16[1536,256]{1,0:T(8,128)(2,1)S(1)}, bf16[1536,256]{1,0:T(8,128)(2,1)}, u32[]{:S(2)}) copy-start(bf16[1536,256]{1,0:T(8,128)(2,1)} %gate.2) | copy-start | bytes 2359300
  108.0 7.0 %copy-start.4 = (bf16[1536,256]{1,0:T(8,128)(2,1)S(1)}, bf16[1536,256]{1,0:T(8,128)(2,1)}, u32[]{:S(2)}) copy-start(bf16[1536,256]{1,0:T(8,128)(2,1)} %up.2) | copy-start | bytes 2359300
  108.0 7.0 %copy-start.6 = (bf16[256,1536]{1,0:T(8,128)(2,1)S(1)}, bf16[256,1536]{1,0:T(8,128)(2,1)}, u32[]{:S(2)}) copy-start(bf16[256,1536]{1,0:T(8,128)(2,1)} %down.2) | copy-start | bytes 2359300
  111.9 0.8 copy-start.14
  112.7 0.8 copy-start.16
  113.5 0.8 copy-start.18
  114.3 0.7 copy-start.32
  115.0 1.0 copy-start.23
  115.0 1.1 copy-start.25
  115.0 1.3 copy-start.27
  115.0 1.4 copy-start.29
  116.4 31.9 %copy-start = (bf16[2304,512]{1,0:T(8,128)(2,1)}, bf16[2304,512]{1,0:T(8,128)(2,1)S(1)}, u32[]{:S(2)}) copy-start(bf16[2304,512]{1,0:T(8,128)(2,1)S(1)} %shard_map.145.own) | copy-start | bytes 7077892
  118.6 1.0 copy-start.9
  119.6 0.6 copy-start.34
  124.5 21.4 %copy-start.42 = (s32[1,128]{1,0:T(1,128)S(1)}, s32[1,128]{1,0:T(1,128)}, u32[]{:S(2)}) copy-start(s32[1,128]{1,0:T(1,128)} %table.1) | copy-start | bytes 1540
  124.5 77.1 %all-to-all-start.2 = ((bf16[8,288,512]{2,1,0:T(8,128)(2,1)}), bf16[8,288,512]{2,1,0:T(8,128)(2,1)}, u32[]{:S(2)}, u32[]{:S(2)}) async-start(bf16[8,288,512]{2,1,0:T(8,128)(2,1)} %broadcast_in_dim.25), calls=%async_computation.2 | async-start | bytes 4718592 | tf_op jit(solution)/shard_map/all_to_all | solution.py:73
  143.8 52.9 %copy-start.13 = (f32[1024,128]{1,0:T(8,128)S(1)}, f32[1024,128]{1,0:T(8,128)}, u32[]{:S(2)}) copy-start(f32[1024,128]{1,0:T(8,128)} %copy-done.12) | copy-start | bytes 1572868
  143.8 52.9 %copy-start.15 = (f32[1024,128]{1,0:T(8,128)S(1)}, f32[1024,128]{1,0:T(8,128)}, u32[]{:S(2)}) copy-start(f32[1024,128]{1,0:T(8,128)} %copy-done.14) | copy-start | bytes 1572868
  143.8 52.9 %copy-start.17 = (f32[1024,128]{1,0:T(8,128)S(1)}, f32[1024,128]{1,0:T(8,128)}, u32[]{:S(2)}) copy-start(f32[1024,128]{1,0:T(8,128)} %copy-done.16) | copy-start | bytes 1572868
  143.8 52.9 %copy-start.19 = (f32[1024,128]{1,0:T(8,128)S(1)}, f32[1024,128]{1,0:T(8,128)}, u32[]{:S(2)}) copy-start(f32[1024,128]{1,0:T(8,128)} %copy-done.18) | copy-start | bytes 1572868
  143.8 52.9 %copy-start.33 = (bf16[1024,128]{1,0:T(8,128)(2,1)S(1)}, bf16[1024,128]{1,0:T(8,128)(2,1)}, u32[]{:S(2)}) copy-start(bf16[1024,128]{1,0:T(8,128)(2,1)} %copy-done.32) | copy-start | bytes 786436
  143.8 52.8 %collective-permute-start.11 = (bf16[1024,128]{1,0:T(8,128)(2,1)S(1)}, bf16[1024,128]{1,0:T(8,128)(2,1)S(1)}, u32[]{:S(2)}, u32[]{:S(2)}) collective-permute-start(bf16[1024,128]{1,0:T(8,128)(2,1)S(1)} %broadcast_select_fusion.1), channel_id=1, source_target_pairs={{0,16},{1,17},{2,18},{3,19},{4,20},{5,21},{6,22},{7,23},{16,32},{1... | collective-permute-start | bytes 786440 | tf_op jit(solution)/shard_map/ppermute | solution.py:36
  148.4 48.3 %copy-start.11 = (bf16[1024,128]{1,0:T(8,128)(2,1)}, bf16[1024,128]{1,0:T(8,128)(2,1)S(1)}, u32[]{:S(2)}) copy-start(bf16[1024,128]{1,0:T(8,128)(2,1)S(1)} %shard_map.146) | copy-start | bytes 786436
  148.4 82.3 %collective-permute-start.13 = (bf16[2304,512]{1,0:T(8,128)(2,1)S(1)}, bf16[2304,512]{1,0:T(8,128)(2,1)}, u32[]{:S(2)}, u32[]{:S(2)}) collective-permute-start(bf16[2304,512]{1,0:T(8,128)(2,1)S(1)} %shard_map.145.own), channel_id=1, source_target_pairs={{1,0},{3,2},{5,4},{7,6},{8,9},{10,11},{12,13},{14,15},{17,16},{19,... | collective-permute-start | bytes 7077896 | tf_op jit(solution)/shard_map/ppermute | solution.py:36
  201.5 29.1 %copy-start.45 = (f32[1536]{0:T(1024)S(1)}, f32[1536]{0:T(1024)}, u32[]{:S(2)}) copy-start(f32[1536]{0:T(1024)} %param.15) | copy-start | bytes 18436
  201.6 29.1 %collective-permute-start.14 = (bf16[2304,512]{1,0:T(8,128)(2,1)}, bf16[2304,512]{1,0:T(8,128)(2,1)}, u32[]{:S(2)}, u32[]{:S(2)}) collective-permute-start(bf16[2304,512]{1,0:T(8,128)(2,1)} %bitcast.16.other), channel_id=1, source_target_pairs={{0,1},{2,3},{4,5},{6,7},{9,8},{11,10},{13,12},{15,14},{16,17},{18,... | collective-permute-start | bytes 7077896 | tf_op jit(solution)/shard_map/ppermute | solution.py:36
  220.2 10.5 %copy-start.10 = (bf16[384,1536]{1,0:T(8,128)(2,1)S(1)}, bf16[384,1536]{1,0:T(8,128)(2,1)}, u32[]{:S(2)}) copy-start(bf16[384,1536]{1,0:T(8,128)(2,1)} %copy-done.9) | copy-start | bytes 3538948
  220.2 1.0 copy-start.35
  221.2 0.9 copy-start.37
  223.8 0.8 copy-start.20
  224.6 6.0 %collective-permute-start.12 = (bf16[512,512]{1,0:T(8,128)(2,1)}, bf16[512,512]{1,0:T(8,128)(2,1)}, u32[]{:S(2)}, u32[]{:S(2)}) collective-permute-start(bf16[512,512]{1,0:T(8,128)(2,1)} %get-tuple-element.59), channel_id=1, source_target_pairs={{0,1},{1,0},{2,3},{3,2},{4,5},{5,4},{6,7},{7,6},{8,9},{9,8},{10,11... | collective-permute-start | bytes 1572872 | tf_op jit(solution)/shard_map/ppermute | solution.py:36
  226.6 13.7 %all-to-all-start.4 = ((bf16[8,128,128]{2,1,0:T(8,128)(2,1)}), bf16[8,128,128]{2,1,0:T(8,128)(2,1)}, u32[]{:S(2)}, u32[]{:S(2)}) async-start(bf16[8,128,128]{2,1,0:T(8,128)(2,1)} %bitcast.27), calls=%async_computation.4 | async-start | bytes 524288 | tf_op jit(solution)/shard_map/all_to_all | solution.py:472
  230.7 1.0 copy-start.8
  231.7 1.0 copy-start.21
  240.3 22.1 %copy-start.38 = (f32[128,2]{0,1:T(2,128)S(1)}, f32[128,2]{0,1:T(2,128)}, u32[]{:S(2)}) copy-start(f32[128,2]{0,1:T(2,128)} %param.21) | copy-start | bytes 3076
  240.3 22.1 %all-to-all-start.3 = ((bf16[8,48,1536]{2,1,0:T(8,128)(2,1)}), bf16[8,48,1536]{2,1,0:T(8,128)(2,1)S(1)}, u32[]{:S(2)}, u32[]{:S(2)}) async-start(bf16[8,48,1536]{2,1,0:T(8,128)(2,1)} %bitcast.17), calls=%async_computation.3 | async-start | bytes 2359296 | tf_op jit(solution)/shard_map/all_to_all | solution.py:509
  (1 other events, 0.6 us)
Sparse Core Ops, SparseCore 0:
  71.5 40.1 all-gather.1

commit v5 on v4

--- a/solution.py
+++ b/solution.py
@@ -22,7 +22,7 @@
 F32 = jnp.float32
 I32 = jnp.int32
 VMEM = pl.BlockSpec(memory_space=pltpu.VMEM)
-ANY = pl.BlockSpec(memory_space=pl.ANY)
+HBM = pl.BlockSpec(memory_space=pltpu.HBM)
 SMEM = pl.BlockSpec(memory_space=pltpu.SMEM)
 MIB = 1 << 20
 
@@ -44,8 +44,13 @@
     return permute(block, lambda y, zl, zh, x, c: (y, zl, 1 - zh, x, c))
 
 
-def swap_near(block):
-    return permute(block, lambda y, zl, zh, x, c: (y, zl ^ 1, zh, x, c))
+def swap_near(block, step):
+    return permute(block, lambda y, zl, zh, x, c: (y, zl ^ step, zh, x, c))
+
+
+def in_pair(mine, theirs, place):
+    first = jnp.where(place == 0, mine, theirs)
+    return jnp.concatenate([first, jnp.where(place == 0, theirs, mine)], axis=0)
 
 
 def next_group(block):
@@ -55,10 +60,6 @@
         return (y + 1, 0, 0, x, c) if zh == 1 and y < 3 else None
 
     return permute(block, target)
-
-
-def ahead_x(block, step):
-    return permute(block, lambda y, zl, zh, x, c: (y, zl, zh, (x - step) % 4, c))
 
 
 def give_half(block, near):
@@ -114,13 +115,15 @@
     pieces = jnp.where(row == 0, back >> 5, jnp.where(row == 1, back & 31, 0))
     pieces = jnp.where(row == 2, ids[0:1], jnp.where(row == 3, ids[1:2], pieces))
     pieces = pieces.astype(F32).astype(BF16)
-    out[:TOK] = tokens[...]
-    out[TOK:, :TOK] = pieces
-    out[TOK:, TOK:] = jnp.zeros((16, WIDTH - TOK), BF16)
+    for copy in range(4):
+        out[copy, :TOK] = tokens[...]
+        out[copy, TOK:, :TOK] = pieces
+        out[copy, TOK:, TOK:] = jnp.zeros((16, WIDTH - TOK), BF16)
 
 
 def piece_kernel(meta, gate, up, down, out, sems):
-    piece = meta[0] * 4 + lax.rem(meta[1], 4)
+    place = lax.rem(meta[1], 4)
+    piece = meta[0] * 4 + lax.rem(place, 2) * 2 + place // 2
     wide = pl.ds(pl.multiple_of(piece * 96, 32), 96)
     deep = pl.ds(pl.multiple_of(piece * 16, 16), 16)
     copies = [
@@ -152,28 +155,27 @@
             ]
 
 
-def project_kernel(meta, b0, b1, b2, b3, s0, s1, s2, s3, wq, wkv, far, gain,
+def project_kernel(meta, near, across, wq, wkv, far, gain,
                    q_out, kv_out, start_out, cols):
-    zh, x, c = meta[2], meta[3], meta[4]
+    zh, c = meta[2], meta[4]
     cols[0:64] = wq[...]
     cols[64:128] = far[0:64]
     cols[pl.ds(pl.multiple_of(128 + zh * 64, 64), 64), :] = wkv[...]
     cols[pl.ds(pl.multiple_of(192 - zh * 64, 64), 64), :] = far[64:128]
     for k in range(4):
-        place = lax.rem(x + k, 4) * 2
-        for block, core in (((b0, b1, b2, b3)[k], c), ((s0, s1, s2, s3)[k], 1 - c)):
-            low = pl.multiple_of((place + core) * TOK, TOK)
-            normed = rms(block[:TOK].astype(F32), gain[...])
+        for block, core in ((near, c), (across, 1 - c)):
+            low = pl.multiple_of((2 * k + core) * TOK, TOK)
+            normed = rms(block[k, :TOK].astype(F32), gain[...])
             result = dot_nt(normed, cols[...]).astype(BF16)
             q_out[pl.ds(low, TOK), :] = result[:, :128]
             kv_out[pl.ds(low, TOK), :] = result[:, 128:]
-            pieces = block[TOK:, :TOK].astype(F32)
+            pieces = block[k, TOK:, :TOK].astype(F32)
             back = column(pieces[0:1] * 32.0 + pieces[1:2])
             own = (low + lax.broadcasted_iota(I32, (TOK, TOK), 0)).astype(F32)
             start_out[pl.ds(low, TOK), :] = own - back
 
 
-def route_kernel(meta, b0, b1, b2, b3, s0, s1, s2, s3, pick_out, other_out, rows_out):
+def route_kernel(meta, near, across, pick_out, other_out, rows_out):
     x, c = meta[3], meta[4]
     before = lax.broadcasted_iota(I32, (TOK, TOK), 0) < lax.broadcasted_iota(I32, (TOK, TOK), 1)
     before = before.astype(F32).astype(BF16)
@@ -181,10 +183,9 @@
     for expert, out in ((x + 4 * c, pick_out), (x + 4 * (1 - c), other_out)):
         number = expert.astype(F32)
         for k in range(4):
-            place = lax.rem(x + k, 4) * 2
-            for block, core in (((b0, b1, b2, b3)[k], c), ((s0, s1, s2, s3)[k], 1 - c)):
-                low = pl.multiple_of((place + core) * CAP, 16)
-                pieces = block[TOK:, :TOK].astype(F32)
+            for block, core in ((near, c), (across, 1 - c)):
+                low = pl.multiple_of((2 * k + core) * CAP, 16)
+                pieces = block[k, TOK:, :TOK].astype(F32)
                 named = (pieces == number).astype(F32)
                 named = named[2:3] + named[3:4]
                 rank = jnp.dot(
@@ -195,7 +196,7 @@
                 pick = jnp.where((row == rank) & (named > 0.0), 1.0, 0.0).astype(BF16)
                 out[pl.ds(low, CAP), :] = pick
                 if out is pick_out:
-                    chosen = jnp.dot(pick, block[:TOK], preferred_element_type=F32)
+                    chosen = jnp.dot(pick, block[k, :TOK], preferred_element_type=F32)
                     rows_out[pl.ds(low, CAP), :] = chosen.astype(BF16)
 
 
@@ -246,7 +247,7 @@
     slots_out[...] = jnp.where(row == 0, result[0], result[1])
 
 
-def before_kernel(q, kv, start, sums, maxes, dens, out, keys, values):
+def before_kernel(q, kv, start, sums, maxes, dens, pages, out, keys, values):
     keys[...], values[...] = split_kv(kv)
     low_lane = lax.broadcasted_iota(I32, (STEP, 128), 1) < 64
     for block in range(ROWS // STEP):
@@ -272,6 +273,8 @@
         result = (total / (dens[low:high] * scale + den)).astype(BF16)
         for copy in range(4):
             out[copy, low:high, :] = result
+    for k in range(4):
+        out[k, ROWS:, :] = pages[k * 256 : k * 256 + 256]
 
 
 def page_kernel(meta, table, kv, partner, out, group):
@@ -293,12 +296,15 @@
     lax.fori_loop(0, 128, place, 0)
 
 
-def cache_kernel(pages, out):
+def cache_kernel(meta, keep, got, out):
+    c = meta[4]
     low = lax.broadcasted_iota(I32, (TOK, 128), 1) < 64
     for pair in range(4):
-        one = pages[2 * pair].astype(F32)
-        two = pages[2 * pair + 1].astype(F32)
         lanes = slice(pair * 128, pair * 128 + 128)
+        mine = keep[4 * TOK :, lanes].astype(F32)
+        theirs = got[4 * TOK :, lanes].astype(F32)
+        one = jnp.where(c == 0, mine, theirs)
+        two = jnp.where(c == 0, theirs, mine)
         out[:, lanes] = jnp.where(low, one, pltpu.roll(two, 64, 1)).astype(BF16)
         lanes = slice(512 + pair * 128, 640 + pair * 128)
         out[:, lanes] = jnp.where(low, pltpu.roll(one, 64, 1), two).astype(BF16)
@@ -318,8 +324,11 @@
         give_out[low] = jnp.dot(other[low], rows, preferred_element_type=F32).astype(BF16)
     for out, core in ((keep_out, c), (give_out, 1 - c)):
         low = pl.multiple_of((2 * x + core) * TOK, TOK)
+        page = pl.multiple_of(ROWS + core * TOK, TOK)
         for k in range(4):
-            out[8 * CAP :, k * 128 : k * 128 + 128] = heads[k, pl.ds(low, TOK), :]
+            lanes = slice(k * 128, k * 128 + 128)
+            out[8 * CAP : 4 * TOK, lanes] = heads[k, pl.ds(low, TOK), :]
+            out[4 * TOK :, lanes] = heads[k, pl.ds(page, TOK), :]
 
 
 def expert_kernel(meta, keep, got, wo_all, rows, tokens, gain, own, other, given_a, given_b,
@@ -338,8 +347,8 @@
 
     tiles = []
     for k in range(4):
-        one = keep[:, k * 128 : k * 128 + 128]
-        two = got[:, k * 128 : k * 128 + 128]
+        one = keep[: 4 * TOK, k * 128 : k * 128 + 128]
+        two = got[: 4 * TOK, k * 128 : k * 128 + 128]
         tiles += [jnp.where(c == 0, one, two), jnp.where(c == 0, two, one)]
     total = jnp.dot(jnp.concatenate(tiles, axis=1), wo_all[...], preferred_element_type=F32)
     mid_out[...] = (tokens[...].astype(F32) + total[8 * CAP :]).astype(BF16)
@@ -401,33 +410,32 @@
     )
     parts = swap_half(parts)
     (block,) = call(
-        pack_kernel, [((TOK + 16, WIDTH), BF16)], [SMEM] + [VMEM] * 3, nbytes=0
+        pack_kernel, [((4, TOK + 16, WIDTH), BF16)], [SMEM] + [VMEM] * 3, nbytes=0
     )(meta, tokens, segment_ids[None, :], ids)
     (piece,) = call(
         piece_kernel,
         [((144, 512), BF16)],
-        [SMEM] + [ANY] * 3,
+        [SMEM] + [HBM] * 3,
         scratch=[pltpu.SemaphoreType.DMA((5,))],
         nbytes=0,
     )(meta, w_gate, w_up, w_down)
-    one, three, two = [ahead_x(block, step) for step in (1, 3, 2)]
+    near = lax.all_to_all(block, "x", split_axis=0, concat_axis=0, tiled=True)
     piece = swap_half(piece)
-    one, two, three, parts, piece = lax.optimization_barrier((one, two, three, parts, piece))
+    near, parts, piece = lax.optimization_barrier((near, parts, piece))
     parts = gather(parts, "y").reshape(4, 3, 16, WIDTH)
     far_cols = parts[:, :2].transpose(1, 0, 2, 3).reshape(128, WIDTH)
-    near = [block, one, two, three]
-    across = [swap_core(b) for b in near]
-    beside = swap_near(piece)
+    across = swap_core(near)
+    beside = swap_near(piece, 2)
     gain, beside = lax.optimization_barrier((attn_gain[None, :], beside))
     q, kv, start = call(
         project_kernel,
         [((ROWS, 128), BF16), ((ROWS, 128), BF16), ((ROWS, 128), F32)],
-        [SMEM] + [VMEM] * 12,
+        [SMEM] + [VMEM] * 6,
         scratch=[pltpu.VMEM((256, WIDTH), BF16)],
         flops=0,
         nbytes=0,
-    )(meta, *near, *across, wq, wkv, far_cols, gain)
-    out_rows = jnp.concatenate([w_out, parts[:, 2].reshape(64, WIDTH)], axis=0)
+    )(meta, near, across, wq, wkv, far_cols, gain)
+    out_rows = jnp.concatenate([w_out, after(parts, across)[:, 2].reshape(64, WIDTH)], axis=0)
     out_all = lax.all_gather(out_rows, ROW, axis=0, tiled=True)
 
     partner = swap_half(kv)
@@ -442,26 +450,23 @@
     pick, other_pick, chosen = call(
         route_kernel,
         [((8 * CAP, TOK), BF16)] * 2 + [((8 * CAP, WIDTH), BF16)],
-        [SMEM] + [VMEM] * 8,
+        [SMEM] + [VMEM] * 2,
         flops=2000000000,
         nbytes=5000000,
-    )(meta, after(block, kv), *near[1:], *across)
+    )(meta, after(near, kv), across)
 
     (own,) = call(order_kernel, [((2304, 512), BF16)], [VMEM] * 3, nbytes=5000000)(
         *(after(w, kv) for w in (w_gate, w_up, w_down))
     )
-    pair = jnp.where(
-        zp == 0,
-        jnp.concatenate([piece, beside], axis=0),
-        jnp.concatenate([beside, piece], axis=0),
-    )
-    partner, sums, pick, own, out_all, pair = lax.optimization_barrier(
-        (partner, sums, pick, own, out_all, pair)
+    pair = in_pair(piece, beside, zr)
+    four = in_pair(pair, swap_near(after(pair, kv), 1), zp)
+    partner, sums, pick, own, four, out_all = lax.optimization_barrier(
+        (partner, sums, pick, own, four, out_all)
     )
     onward = jnp.where(zh == 0, partner, kv)
     shifted = next_group(onward)
     given_a = give_half(own, True)
-    other = gather(pair, ("y", "zr")).reshape(2304, 512)
+    other = lax.all_gather(four, "y", axis=0, tiled=True)
     (pages,) = call(
         page_kernel,
         [((ROWS, 128), BF16)],
@@ -469,34 +474,30 @@
         scratch=[pltpu.VMEM((2 * ROWS, 128), BF16)],
         nbytes=0,
     )(meta, page_table, kv, partner)
-    held = lax.all_to_all(
-        pages.reshape(8, TOK, 128), ROW, split_axis=0, concat_axis=0, tiled=True
-    )
     previous = jnp.where(zh == 0, shifted, partner)
     (heads,) = call(
         before_kernel,
-        [((4, ROWS, 128), BF16)],
-        [VMEM] * 6,
+        [((4, ROWS + 256, 128), BF16)],
+        [VMEM] * 7,
         scratch=[pltpu.VMEM((ROWS, 128), BF16)] * 2,
         flops=0,
         nbytes=0,
-    )(after(q, pages), previous, start, sums, maxes, dens)
-    other = after(other, heads)
-    given_b = give_half(other, False)
+    )(q, previous, start, sums, maxes, dens, pages)
     heads = lax.all_to_all(heads, "x", split_axis=0, concat_axis=0, tiled=True)
-    (cache,) = call(cache_kernel, [((TOK, 1024), BF16)], [VMEM], nbytes=0)(held)
     keep, give = call(
         split_kernel,
-        [((4 * TOK, 512), BF16)] * 2,
+        [((5 * TOK, 512), BF16)] * 2,
         [SMEM] + [VMEM] * 3,
         flops=0,
         nbytes=0,
     )(meta, heads, pick, other_pick)
     got = swap_core(give)
+    other = after(other, give)
+    given_b = give_half(other, False)
     mid, expert_out = call(
         expert_kernel,
         [((TOK, WIDTH), BF16), ((8 * CAP, WIDTH), BF16)],
-        [SMEM] + [VMEM] * 6 + [ANY] * 4,
+        [SMEM] + [VMEM] * 6 + [HBM] * 4,
         scratch=[
             pltpu.VMEM((2, 2304, 512), BF16),
             pltpu.VMEM((2, WIDTH, 512), BF16),
@@ -506,6 +507,9 @@
         flops=0,
         nbytes=0,
     )(meta, keep, got, out_all, chosen, tokens, ffn_gain[None, :], own, other, given_a, given_b)
+    (cache,) = call(cache_kernel, [((TOK, 1024), BF16)], [SMEM] + [VMEM] * 2, nbytes=800000)(
+        meta, after(keep, expert_out), got
+    )
     returned = lax.all_to_all(
         expert_out.reshape(8, CAP, WIDTH), ROW, split_axis=0, concat_axis=0, tiled=True
     ).reshape(8 * CAP, WIDTH)

time: 272 us -> 225 us (0.83)
  the two profiles are of different devices: /device:TPU:64 before, /device:TPU:24 now
where the time goes in v5:
time: 225 us; the launch traced here: 223 us
  waiting for transfers between devices  90.6 us (40%)
  starting transfers between devices  51.5 us (23%)
  Pallas kernels  33.2 us (15%)
  local copies, waits for them, and re-layouts  16.2 us (7%)
  between operations  14.6 us (6%)
  blocking collectives  13.3 us (6%)
  other arithmetic  3.79 us (2%)
    ppermute x10, waiting for transfers between devices, permute(): return lax.ppermute(block, AXES, route)  58.6 us
    ppermute x10, starting transfers between devices, permute(): return lax.ppermute(block, AXES, route)  38.5 us
    all_to_all x1, waiting for transfers between devices, body(): heads = lax.all_to_all(heads, 'x', split_axis=0, concat_axis=0, tiled=True)  16.1 us
    all_to_all x1, waiting for transfers between devices, body(): lax.all_to_all(expert_out.reshape(8, CAP, WIDTH), ROW, split_axis=0, conc...  15.9 us
    unnamed x92, local copies, waits for them, and re-layouts  15.2 us
    all_to_all x1, blocking collectives, gather(): return lax.all_to_all(wide, axis, split_axis=0, concat_axis=0, tiled=True)  13.3 us
    pallas_call x1, Pallas kernels, body(): call(expert_kernel, [((TOK, WIDTH), BF16), ((8 * CAP, WIDTH), BF16)], [SM...  7.71 us
    all_to_all x1, starting transfers between devices, body(): heads = lax.all_to_all(heads, 'x', split_axis=0, concat_axis=0, tiled=True)  4.85 us
  transfers between devices with their start and end apart: 15, of which 8 were waited for; matrix products, arithmetic and copies ran while one was open for 1% of the time, Pallas kernels for 10%

profile of v5, /device:TPU:24, one launch (start us, length us, event | category | flops | bytes accessed | tf_op | source)
XLA Modules:
  0.0 223.2 jit_solution(2479907087026420091)
XLA Ops:
  7.2 0.1 stack.27.meta
  7.3 1.0 copy-done.13
  8.3 0.7 copy-done.36
  9.0 0.7 copy-done.39
  9.6 1.9 shard_map.140
  11.5 4.4 %all-to-all-start = ((bf16[4,144,1536]{2,1,0:T(8,128)(2,1)}), bf16[4,144,1536]{2,1,0:T(8,128)(2,1)S(1)}, u32[]{:S(2)}, u32[]{:S(2)}) async-start(bf16[4,144,1536]{2,1,0:T(8,128)(2,1)} %shard_map.140), calls=%async_computation | async-start | bytes 3538944 | tf_op jit(solution)/shard_map/all_to_all | solution.py:422
  15.9 1.1 copy-done.5
  17.1 1.1 copy-done.7
  18.2 0.7 shard_map.141
  18.9 15.7 %collective-permute-start.1 = (bf16[144,512]{1,0:T(8,128)(2,1)S(1)}, bf16[144,512]{1,0:T(8,128)(2,1)S(1)}, u32[]{:S(2)}, u32[]{:S(2)}) collective-permute-start(bf16[144,512]{1,0:T(8,128)(2,1)S(1)} %shard_map.141), channel_id=1, source_target_pairs={{0,8},{1,9},{2,10},{3,11},{4,12},{5,13},{6,14},{7,15},{8,0},{9,1},... | collective-permute-start | bytes 442376 | tf_op jit(solution)/shard_map/ppermute | solution.py:36
  34.6 0.8 constant_dynamic-slice_fusion
  35.4 0.0 copy-start.44
  35.5 1.9 collective-permute-start
  37.4 1.0 collective-permute-done.1
  38.4 27.4 %collective-permute-done = bf16[48,1536]{1,0:T(8,128)(2,1)S(1)} collective-permute-done((bf16[48,1536]{1,0:T(8,128)(2,1)S(1)}, bf16[48,1536]{1,0:T(8,128)(2,1)S(1)}, u32[]{:S(2)}, u32[]{:S(2)}) %collective-permute-start) | collective-permute-done | bytes 147488 | tf_op jit(solution)/shard_map/ppermute | solution.py:36
  65.9 1.9 collective-permute-start.2
  67.9 13.3 %all_to_all.20 = bf16[4,48,1536]{2,1,0:T(8,128)(2,1)S(1)} all-to-all(bf16[4,48,1536]{2,1,0:T(8,128)(2,1)S(1)} %broadcast_in_dim.16), channel_id=1, replica_groups=mesh['y'=4,'zq'=2,'zr'=2,'zp'=2,'zh'=2,'x'=4,'c'=2] {'y'}, dimensions={0} | all-to-all | bytes 1179648 | tf_op jit(solution)/shard_map/all_to_all | solution.py:74
  81.1 1.2 copy-done.11
  82.3 1.7 pad_maximum_fusion.1
  84.0 0.0 all-gather.3.cloned.1.call-update
  84.1 0.0 all-gather.5.cloned.1.call-start
  84.1 1.9 collective-permute-start.3
  86.1 6.3 %collective-permute-done.3 = bf16[144,512]{1,0:T(8,128)(2,1)} collective-permute-done((bf16[144,512]{1,0:T(8,128)(2,1)}, bf16[144,512]{1,0:T(8,128)(2,1)}, u32[]{:S(2)}, u32[]{:S(2)}) %collective-permute-start.3) | collective-permute-done | bytes 147488 | tf_op jit(solution)/shard_map/ppermute | solution.py:36
  92.4 1.0 broadcast_select_fusion.5
  93.5 0.0 copy-start.6
  93.5 0.0 copy-start.8
  93.5 3.6 %shard_map.142 = (bf16[1024,128]{1,0:T(8,128)(2,1)S(1)}, bf16[1024,128]{1,0:T(8,128)(2,1)}, f32[1024,128]{1,0:T(8,128)S(1)}) custom-call(s32[6]{0:T(128)S(1)} %stack.27.meta, bf16[4,144,1536]{2,1,0:T(8,128)(2,1)S(1)} %all-to-all-done.near, bf16[4,144,1536]{2,1,0:T(8,128)(2,1)S(1)} %copy-done.12, bf16[64,1536]{1,0:T(8,128)(2,1)S(1)} %bitcast.26, ...), custom_call_target="tpu_custom_call" | custom-call | tf_op jit(solution)/shard_map/pallas_call | solution.py:430
  97.2 8.2 %collective-permute-start.4 = (bf16[1024,128]{1,0:T(8,128)(2,1)}, bf16[1024,128]{1,0:T(8,128)(2,1)S(1)}, u32[]{:S(2)}, u32[]{:S(2)}) collective-permute-start(bf16[1024,128]{1,0:T(8,128)(2,1)} %get-tuple-element.40.kv), channel_id=1, source_target_pairs={{0,8},{1,9},{2,10},{3,11},{4,12},{5,13},{6,14},{7,15},{8,0},{9,1},... | collective-permute-start | bytes 786440 | tf_op jit(solution)/shard_map/ppermute | solution.py:36
  105.4 1.9 collective-permute-start.5
  107.4 0.2 shard_map.145.own
  107.5 0.0 copy-start.37
  107.6 2.2 shard_map.144
  109.8 1.0 copy-done.16
  110.8 4.8 %shard_map.143 = (f32[1024,128]{1,0:T(8,128)S(1)}, f32[1024,128]{1,0:T(8,128)S(1)}, f32[1024,128]{1,0:T(8,128)S(1)}, s32[8,128]{1,0:T(8,128)S(1)}) custom-call(bf16[1024,128]{1,0:T(8,128)(2,1)S(1)} %get-tuple-element.39.q, bf16[1024,128]{1,0:T(8,128)(2,1)} %get-tuple-element.40.kv, f32[1024,128]{1,0:T(8,128)S(1)} %get-tuple-element.41.start, ...), custom_call_target="tpu_custom_call" | custom-call | flops 4000000000 | bytes 3000000 | tf_op jit(solution)/shard_map/pallas_call | solution.py:442
  115.7 0.8 copy-done.24
  116.5 13.4 %collective-permute-done.5 = bf16[288,512]{1,0:T(8,128)(2,1)S(1)} collective-permute-done((bf16[288,512]{1,0:T(8,128)(2,1)S(1)}, bf16[288,512]{1,0:T(8,128)(2,1)S(1)}, u32[]{:S(2)}, u32[]{:S(2)}) %collective-permute-start.5) | collective-permute-done | bytes 294944 | tf_op jit(solution)/shard_map/ppermute | solution.py:36
  129.8 0.1 broadcast_select_fusion.1
  130.0 0.9 pad_maximum_fusion
  130.9 0.0 all-gather.3.cloned.1.call-done.wo_all
  130.9 0.0 all-gather.5.cloned.1.call-update
  131.0 2.2 %collective-permute-start.6 = (bf16[1024,128]{1,0:T(8,128)(2,1)S(1)}, bf16[1024,128]{1,0:T(8,128)(2,1)S(1)}, u32[]{:S(2)}, u32[]{:S(2)}) collective-permute-start(bf16[1024,128]{1,0:T(8,128)(2,1)S(1)} %broadcast_select_fusion.3), channel_id=1, source_target_pairs={{0,16},{1,17},{2,18},{3,19},{4,20},{5,21},{6,22},{7,23},{16,32},{1... | collective-permute-start | bytes 786440 | tf_op jit(solution)/shard_map/ppermute | solution.py:36
  133.2 2.9 %shard_map.146.pages = bf16[1024,128]{1,0:T(8,128)(2,1)S(1)} custom-call(s32[6]{0:T(128)S(1)} %stack.27.meta, s32[1,128]{1,0:T(1,128)S(1)} %copy-done.40, bf16[1024,128]{1,0:T(8,128)(2,1)} %get-tuple-element.40.kv, bf16[1024,128]{1,0:T(8,128)(2,1)S(1)} %collective-permute-done.4.partner), custom_call_target="tpu_custom_call" | custom-call | tf_op jit(solution)/shard_map/pallas_call | solution.py:470
  136.1 7.2 %collective-permute-done.6 = bf16[1024,128]{1,0:T(8,128)(2,1)S(1)} collective-permute-done((bf16[1024,128]{1,0:T(8,128)(2,1)S(1)}, bf16[1024,128]{1,0:T(8,128)(2,1)S(1)}, u32[]{:S(2)}, u32[]{:S(2)}) %collective-permute-start.6) | collective-permute-done | bytes 262176 | tf_op jit(solution)/shard_map/ppermute | solution.py:36
  143.4 4.7 %shard_map.147 = bf16[4,1280,128]{2,1,0:T(8,128)(2,1)S(1)} custom-call(bf16[1024,128]{1,0:T(8,128)(2,1)S(1)} %copy-done.31, bf16[1024,128]{1,0:T(8,128)(2,1)S(1)} %broadcast_select_fusion.2.kv, f32[1024,128]{1,0:T(8,128)S(1)} %copy-done.19, f32[1024,128]{1,0:T(8,128)S(1)} %copy-done.21, f32[1024,128]{1,0:T(8,128)S(1)} %copy-done.23, ...), custom_call_target="tpu_custom_call" | custom-call | tf_op jit(solution)/shard_map/pallas_call | solution.py:478
  148.2 1.1 copy-done.3
  149.3 4.8 %all-to-all-start.2 = ((bf16[4,1280,128]{2,1,0:T(8,128)(2,1)}), bf16[4,1280,128]{2,1,0:T(8,128)(2,1)}, u32[]{:S(2)}, u32[]{:S(2)}) async-start(bf16[4,1280,128]{2,1,0:T(8,128)(2,1)} %copy-done.3), calls=%async_computation.2 | async-start | bytes 2621440 | tf_op jit(solution)/shard_map/all_to_all | solution.py:486
  154.2 1.3 collective-permute-start.8
  155.4 16.1 %all-to-all-done.2.heads = bf16[4,1280,128]{2,1,0:T(8,128)(2,1)} async-done(((bf16[4,1280,128]{2,1,0:T(8,128)(2,1)}), bf16[4,1280,128]{2,1,0:T(8,128)(2,1)}, u32[]{:S(2)}, u32[]{:S(2)}) %all-to-all-start.2) | async-done | bytes 1310752 | tf_op jit(solution)/shard_map/all_to_all | solution.py:486
  171.5 0.9 copy-done.35
  172.4 1.8 shard_map.148
  174.2 0.8 copy-done.41
  175.0 1.4 collective-permute-start.9
  176.4 1.9 collective-permute-start.7
  178.4 3.2 %collective-permute-done.7.got = bf16[640,512]{1,0:T(8,128)(2,1)S(1)} collective-permute-done((bf16[640,512]{1,0:T(8,128)(2,1)}, bf16[640,512]{1,0:T(8,128)(2,1)S(1)}, u32[]{:S(2)}, u32[]{:S(2)}) %collective-permute-start.7) | collective-permute-done | bytes 655392 | tf_op jit(solution)/shard_map/ppermute | solution.py:36
  181.6 0.0 collective-permute-done.9.given_b
  181.6 1.6 copy-done.42
  183.2 1.3 copy-done.17
  184.4 7.7 %shard_map.149 = (bf16[128,1536]{1,0:T(8,128)(2,1)S(1)}, bf16[384,1536]{1,0:T(8,128)(2,1)S(1)}) custom-call(s32[6]{0:T(128)S(1)} %stack.27.meta, bf16[640,512]{1,0:T(8,128)(2,1)S(1)} %get-tuple-element.67.keep, bf16[640,512]{1,0:T(8,128)(2,1)S(1)} %collective-permute-done.7.got, bf16[1024,1536]{1,0:T(8,128)(2,1)} %all-gather.3.cloned.1.call-done.wo_all, ...), custom_call_target="tpu_custom_call" | custom-call | tf_op jit(solution)/shard_map/pallas_call | solution.py:497
  192.2 1.0 copy-done.15
  193.2 0.7 copy-done.26
  194.0 3.7 %all-to-all-start.3 = ((bf16[8,48,1536]{2,1,0:T(8,128)(2,1)}), bf16[8,48,1536]{2,1,0:T(8,128)(2,1)S(1)}, u32[]{:S(2)}, u32[]{:S(2)}) async-start(bf16[8,48,1536]{2,1,0:T(8,128)(2,1)} %bitcast.25), calls=%async_computation.3 | async-start | bytes 2359296 | tf_op jit(solution)/shard_map/all_to_all | solution.py:513
  197.7 1.4 shard_map.151
  199.1 15.9 %all-to-all-done.3 = bf16[8,48,1536]{2,1,0:T(8,128)(2,1)S(1)} async-done(((bf16[8,48,1536]{2,1,0:T(8,128)(2,1)}), bf16[8,48,1536]{2,1,0:T(8,128)(2,1)S(1)}, u32[]{:S(2)}, u32[]{:S(2)}) %all-to-all-start.3) | async-done | bytes 1179680 | tf_op jit(solution)/shard_map/all_to_all | solution.py:513
  214.9 1.4 shard_map.150
  (90 shorter events, 0.4 us)
Async XLA Ops:
  7.3 1.0 copy-start.13
  8.3 0.7 copy-start.36
  8.9 0.7 copy-start.39
  11.5 4.4 %copy-start.4 = (bf16[1536,256]{1,0:T(8,128)(2,1)S(1)}, bf16[1536,256]{1,0:T(8,128)(2,1)}, u32[]{:S(2)}) copy-start(bf16[1536,256]{1,0:T(8,128)(2,1)} %gate.2) | copy-start | bytes 2359300
  11.5 54.4 %all-to-all-start = ((bf16[4,144,1536]{2,1,0:T(8,128)(2,1)}), bf16[4,144,1536]{2,1,0:T(8,128)(2,1)S(1)}, u32[]{:S(2)}, u32[]{:S(2)}) async-start(bf16[4,144,1536]{2,1,0:T(8,128)(2,1)} %shard_map.140), calls=%async_computation | async-start | bytes 3538944 | tf_op jit(solution)/shard_map/all_to_all | solution.py:422
  15.9 115.0 %all-gather.3.cloned.1.call-start = ((), (), s32[]{:S(2)}) async-start(), calls=%async_computation.4 | async-start | bytes 3538944 | tf_op jit(solution)/shard_map/all_gather | solution.py:439
  15.9 1.1 copy-start.5
  17.1 1.1 copy-start.7
  18.2 17.2 %copy-start.28 = (bf16[1536,64]{0,1:T(8,128)(2,1)S(1)}, bf16[1536,64]{0,1:T(8,128)(2,1)}, u32[]{:S(2)}) copy-start(bf16[1536,64]{0,1:T(8,128)(2,1)} %param.16) | copy-start | bytes 589828
  18.2 17.2 %copy-start.29 = (bf16[1536,64]{0,1:T(8,128)(2,1)S(1)}, bf16[1536,64]{0,1:T(8,128)(2,1)}, u32[]{:S(2)}) copy-start(bf16[1536,64]{0,1:T(8,128)(2,1)} %param.17) | copy-start | bytes 589828
  18.9 19.6 %collective-permute-start.1 = (bf16[144,512]{1,0:T(8,128)(2,1)S(1)}, bf16[144,512]{1,0:T(8,128)(2,1)S(1)}, u32[]{:S(2)}, u32[]{:S(2)}) collective-permute-start(bf16[144,512]{1,0:T(8,128)(2,1)S(1)} %shard_map.141), channel_id=1, source_target_pairs={{0,8},{1,9},{2,10},{3,11},{4,12},{5,13},{6,14},{7,15},{8,0},{9,1},... | collective-permute-start | bytes 442376 | tf_op jit(solution)/shard_map/ppermute | solution.py:36
  35.4 50.6 %copy-start.44 = (f32[1536]{0:T(1024)S(1)}, f32[1536]{0:T(1024)}, u32[]{:S(2)}) copy-start(f32[1536]{0:T(1024)} %param.14) | copy-start | bytes 18436
  35.5 30.4 %collective-permute-start = (bf16[48,1536]{1,0:T(8,128)(2,1)S(1)}, bf16[48,1536]{1,0:T(8,128)(2,1)S(1)}, u32[]{:S(2)}, u32[]{:S(2)}) collective-permute-start(bf16[48,1536]{1,0:T(8,128)(2,1)S(1)} %pad_maximum_fusion.3), channel_id=1, source_target_pairs={{0,8},{1,9},{2,10},{3,11},{4,12},{5,13},{6,14},{7,15},{8,0},{9,1},... | collective-permute-start | bytes 442376 | tf_op jit(solution)/shard_map/ppermute | solution.py:36
  38.4 29.4 %copy-start.43 = (bf16[144,512]{1,0:T(8,128)(2,1)}, bf16[144,512]{1,0:T(8,128)(2,1)S(1)}, u32[]{:S(2)}) copy-start(bf16[144,512]{1,0:T(8,128)(2,1)S(1)} %collective-permute-done.1) | copy-start | bytes 442372
  65.9 27.6 %copy-start.1 = (bf16[4,144,1536]{2,1,0:T(8,128)(2,1)}, bf16[4,144,1536]{2,1,0:T(8,128)(2,1)S(1)}, u32[]{:S(2)}) copy-start(bf16[4,144,1536]{2,1,0:T(8,128)(2,1)S(1)} %all-to-all-done.near) | copy-start | bytes 5308420
  65.9 15.2 %collective-permute-start.2 = (bf16[4,144,1536]{2,1,0:T(8,128)(2,1)S(1)}, bf16[4,144,1536]{2,1,0:T(8,128)(2,1)S(1)}, u32[]{:S(2)}, u32[]{:S(2)}) collective-permute-start(bf16[4,144,1536]{2,1,0:T(8,128)(2,1)S(1)} %all-to-all-done.near), channel_id=1, source_target_pairs={{0,1},{1,0},{2,3},{3,2},{4,5},{5,4},{6,7},{7,6},{8,9},{9,8},{10,11... | collective-permute-start | bytes 5308424 | tf_op jit(solution)/shard_map/ppermute | solution.py:36
  81.1 1.2 copy-start.11
  84.1 90.9 %all-gather.5.cloned.1.call-start = ((), (), s32[]{:S(2)}) async-start(), calls=%async_computation.5 | async-start | bytes 2949120 | tf_op jit(solution)/shard_map/all_gather | solution.py:469
  84.1 8.3 %collective-permute-start.3 = (bf16[144,512]{1,0:T(8,128)(2,1)}, bf16[144,512]{1,0:T(8,128)(2,1)}, u32[]{:S(2)}, u32[]{:S(2)}) collective-permute-start(bf16[144,512]{1,0:T(8,128)(2,1)} %copy-done.43), channel_id=1, source_target_pairs={{0,32},{1,33},{2,34},{3,35},{4,36},{5,37},{6,38},{7,39},{8,40},{9,... | collective-permute-start | bytes 442376 | tf_op jit(solution)/shard_map/ppermute | solution.py:36
  86.1 7.4 %copy-start.12 = (bf16[4,144,1536]{2,1,0:T(8,128)(2,1)S(1)}, bf16[4,144,1536]{2,1,0:T(8,128)(2,1)}, u32[]{:S(2)}) copy-start(bf16[4,144,1536]{2,1,0:T(8,128)(2,1)} %copy-done.11) | copy-start | bytes 5308420
  93.5 13.8 %copy-start.6 = (bf16[1536,256]{1,0:T(8,128)(2,1)S(1)}, bf16[1536,256]{1,0:T(8,128)(2,1)}, u32[]{:S(2)}) copy-start(bf16[1536,256]{1,0:T(8,128)(2,1)} %up.2) | copy-start | bytes 2359300
  93.5 13.8 %copy-start.8 = (bf16[256,1536]{1,0:T(8,128)(2,1)S(1)}, bf16[256,1536]{1,0:T(8,128)(2,1)}, u32[]{:S(2)}) copy-start(bf16[256,1536]{1,0:T(8,128)(2,1)} %down.2) | copy-start | bytes 2359300
  97.2 13.6 %copy-start.18 = (f32[1024,128]{1,0:T(8,128)}, f32[1024,128]{1,0:T(8,128)S(1)}, u32[]{:S(2)}) copy-start(f32[1024,128]{1,0:T(8,128)S(1)} %get-tuple-element.41.start) | copy-start | bytes 1572868
  97.2 13.6 %copy-start.30 = (bf16[1024,128]{1,0:T(8,128)(2,1)}, bf16[1024,128]{1,0:T(8,128)(2,1)S(1)}, u32[]{:S(2)}) copy-start(bf16[1024,128]{1,0:T(8,128)(2,1)S(1)} %get-tuple-element.39.q) | copy-start | bytes 786436
  97.2 10.4 %copy-start.2 = (bf16[4,144,1536]{2,1,0:T(8,128)(2,1)S(1)}, bf16[4,144,1536]{2,1,0:T(8,128)(2,1)}, u32[]{:S(2)}) copy-start(bf16[4,144,1536]{2,1,0:T(8,128)(2,1)} %copy-done.1) | copy-start | bytes 5308420
  97.2 33.7 %collective-permute-start.4 = (bf16[1024,128]{1,0:T(8,128)(2,1)}, bf16[1024,128]{1,0:T(8,128)(2,1)S(1)}, u32[]{:S(2)}, u32[]{:S(2)}) collective-permute-start(bf16[1024,128]{1,0:T(8,128)(2,1)} %get-tuple-element.40.kv), channel_id=1, source_target_pairs={{0,8},{1,9},{2,10},{3,11},{4,12},{5,13},{6,14},{7,15},{8,0},{9,1},... | collective-permute-start | bytes 786440 | tf_op jit(solution)/shard_map/ppermute | solution.py:36
  105.4 24.4 %collective-permute-start.5 = (bf16[288,512]{1,0:T(8,128)(2,1)S(1)}, bf16[288,512]{1,0:T(8,128)(2,1)S(1)}, u32[]{:S(2)}, u32[]{:S(2)}) collective-permute-start(bf16[288,512]{1,0:T(8,128)(2,1)S(1)} %pad_maximum_fusion.2), channel_id=1, source_target_pairs={{0,16},{1,17},{2,18},{3,19},{4,20},{5,21},{6,22},{7,23},{8,24},{9,... | collective-permute-start | bytes 884744 | tf_op jit(solution)/shard_map/ppermute | solution.py:36
  107.5 46.6 %copy-start = (bf16[2304,512]{1,0:T(8,128)(2,1)}, bf16[2304,512]{1,0:T(8,128)(2,1)S(1)}, u32[]{:S(2)}) copy-start(bf16[2304,512]{1,0:T(8,128)(2,1)S(1)} %shard_map.145.own) | copy-start | bytes 7077892
  107.5 3.3 %copy-start.37 = (s32[128,2]{0,1:T(2,128)S(1)}, s32[128,2]{0,1:T(2,128)}, u32[]{:S(2)}) copy-start(s32[128,2]{0,1:T(2,128)} %param.20) | copy-start | bytes 3076
  109.8 1.0 copy-start.16
  110.8 4.8 %copy-start.32 = (bf16[384,128]{1,0:T(8,128)(2,1)}, bf16[384,128]{1,0:T(8,128)(2,1)S(1)}, u32[]{:S(2)}) copy-start(bf16[384,128]{1,0:T(8,128)(2,1)S(1)} %get-tuple-element.55.pick) | copy-start | bytes 294916
  110.8 4.8 %copy-start.34 = (bf16[384,128]{1,0:T(8,128)(2,1)}, bf16[384,128]{1,0:T(8,128)(2,1)S(1)}, u32[]{:S(2)}) copy-start(bf16[384,128]{1,0:T(8,128)(2,1)S(1)} %get-tuple-element.56.other) | copy-start | bytes 294916
  115.6 0.8 copy-start.24
  116.5 13.5 %copy-start.20 = (f32[1024,128]{1,0:T(8,128)}, f32[1024,128]{1,0:T(8,128)S(1)}, u32[]{:S(2)}) copy-start(f32[1024,128]{1,0:T(8,128)S(1)} %get-tuple-element.52.sums) | copy-start | bytes 1572868
  116.5 13.5 %copy-start.22 = (f32[1024,128]{1,0:T(8,128)}, f32[1024,128]{1,0:T(8,128)S(1)}, u32[]{:S(2)}) copy-start(f32[1024,128]{1,0:T(8,128)S(1)} %get-tuple-element.53.maxes) | copy-start | bytes 1572868
  116.5 16.8 %copy-start.40 = (s32[1,128]{1,0:T(1,128)S(1)}, s32[1,128]{1,0:T(1,128)}, u32[]{:S(2)}) copy-start(s32[1,128]{1,0:T(1,128)} %table.1) | copy-start | bytes 1540
  130.9 12.5 %copy-start.19 = (f32[1024,128]{1,0:T(8,128)S(1)}, f32[1024,128]{1,0:T(8,128)}, u32[]{:S(2)}) copy-start(f32[1024,128]{1,0:T(8,128)} %copy-done.18) | copy-start | bytes 1572868
  130.9 12.5 %copy-start.31 = (bf16[1024,128]{1,0:T(8,128)(2,1)S(1)}, bf16[1024,128]{1,0:T(8,128)(2,1)}, u32[]{:S(2)}) copy-start(bf16[1024,128]{1,0:T(8,128)(2,1)} %copy-done.30) | copy-start | bytes 786436
  130.9 12.5 %copy-start.21 = (f32[1024,128]{1,0:T(8,128)S(1)}, f32[1024,128]{1,0:T(8,128)}, u32[]{:S(2)}) copy-start(f32[1024,128]{1,0:T(8,128)} %copy-done.20) | copy-start | bytes 1572868
  130.9 12.5 %copy-start.23 = (f32[1024,128]{1,0:T(8,128)S(1)}, f32[1024,128]{1,0:T(8,128)}, u32[]{:S(2)}) copy-start(f32[1024,128]{1,0:T(8,128)} %copy-done.22) | copy-start | bytes 1572868
  130.9 12.5 %copy-start.25 = (f32[1024,128]{1,0:T(8,128)S(1)}, f32[1024,128]{1,0:T(8,128)}, u32[]{:S(2)}) copy-start(f32[1024,128]{1,0:T(8,128)} %copy-done.24) | copy-start | bytes 1572868
  131.0 12.4 %collective-permute-start.6 = (bf16[1024,128]{1,0:T(8,128)(2,1)S(1)}, bf16[1024,128]{1,0:T(8,128)(2,1)S(1)}, u32[]{:S(2)}, u32[]{:S(2)}) collective-permute-start(bf16[1024,128]{1,0:T(8,128)(2,1)S(1)} %broadcast_select_fusion.3), channel_id=1, source_target_pairs={{0,16},{1,17},{2,18},{3,19},{4,20},{5,21},{6,22},{7,23},{16,32},{1... | collective-permute-start | bytes 786440 | tf_op jit(solution)/shard_map/ppermute | solution.py:36
  148.2 1.1 copy-start.3
  149.3 22.2 %copy-start.33 = (bf16[384,128]{1,0:T(8,128)(2,1)S(1)}, bf16[384,128]{1,0:T(8,128)(2,1)}, u32[]{:S(2)}) copy-start(bf16[384,128]{1,0:T(8,128)(2,1)} %copy-done.32) | copy-start | bytes 294916
  149.3 29.1 %copy-start.45 = (f32[1536]{0:T(1024)S(1)}, f32[1536]{0:T(1024)}, u32[]{:S(2)}) copy-start(f32[1536]{0:T(1024)} %param.15) | copy-start | bytes 18436
  149.3 33.9 %copy-start.14 = (bf16[128,1536]{1,0:T(8,128)(2,1)S(1)}, bf16[128,1536]{1,0:T(8,128)(2,1)}, u32[]{:S(2)}) copy-start(bf16[128,1536]{1,0:T(8,128)(2,1)} %tokens.3) | copy-start | bytes 1179652
  149.3 22.2 %all-to-all-start.2 = ((bf16[4,1280,128]{2,1,0:T(8,128)(2,1)}), bf16[4,1280,128]{2,1,0:T(8,128)(2,1)}, u32[]{:S(2)}, u32[]{:S(2)}) async-start(bf16[4,1280,128]{2,1,0:T(8,128)(2,1)} %copy-done.3), calls=%async_computation.2 | async-start | bytes 2621440 | tf_op jit(solution)/shard_map/all_to_all | solution.py:486
  154.2 27.4 %collective-permute-start.8 = (bf16[2304,512]{1,0:T(8,128)(2,1)S(1)}, bf16[2304,512]{1,0:T(8,128)(2,1)}, u32[]{:S(2)}, u32[]{:S(2)}) collective-permute-start(bf16[2304,512]{1,0:T(8,128)(2,1)S(1)} %shard_map.145.own), channel_id=1, source_target_pairs={{1,0},{3,2},{5,4},{7,6},{8,9},{10,11},{12,13},{14,15},{17,16},{19,... | collective-permute-start | bytes 7077896 | tf_op jit(solution)/shard_map/ppermute | solution.py:36
  171.5 0.9 copy-start.35
  174.2 0.8 copy-start.41
  175.0 6.6 %collective-permute-start.9 = (bf16[2304,512]{1,0:T(8,128)(2,1)}, bf16[2304,512]{1,0:T(8,128)(2,1)S(1)}, u32[]{:S(2)}, u32[]{:S(2)}) collective-permute-start(bf16[2304,512]{1,0:T(8,128)(2,1)} %all-gather.5.cloned.1.call-done.other), channel_id=1, source_target_pairs={{0,1},{2,3},{4,5},{6,7},{9,8},{11,10},{13,12},{15,14},{16,17},{18,... | collective-permute-start | bytes 7077896 | tf_op jit(solution)/shard_map/ppermute | solution.py:36
  176.4 5.1 %collective-permute-start.7 = (bf16[640,512]{1,0:T(8,128)(2,1)}, bf16[640,512]{1,0:T(8,128)(2,1)S(1)}, u32[]{:S(2)}, u32[]{:S(2)}) collective-permute-start(bf16[640,512]{1,0:T(8,128)(2,1)} %copy-done.41), channel_id=1, source_target_pairs={{0,1},{1,0},{2,3},{3,2},{4,5},{5,4},{6,7},{7,6},{8,9},{9,8},{10,11... | collective-permute-start | bytes 1966088 | tf_op jit(solution)/shard_map/ppermute | solution.py:36
  181.6 10.6 %copy-start.9 = (bf16[640,512]{1,0:T(8,128)(2,1)}, bf16[640,512]{1,0:T(8,128)(2,1)S(1)}, u32[]{:S(2)}) copy-start(bf16[640,512]{1,0:T(8,128)(2,1)S(1)} %collective-permute-done.7.got) | copy-start | bytes 1966084
  181.6 1.6 copy-start.42
  183.2 1.3 copy-start.17
  192.2 1.0 copy-start.15
  193.2 0.7 copy-start.26
  193.9 3.7 %copy-start.10 = (bf16[640,512]{1,0:T(8,128)(2,1)S(1)}, bf16[640,512]{1,0:T(8,128)(2,1)}, u32[]{:S(2)}) copy-start(bf16[640,512]{1,0:T(8,128)(2,1)} %copy-done.9) | copy-start | bytes 1966084
  193.9 21.0 %copy-start.27 = (bf16[128,1536]{1,0:T(8,128)(2,1)S(1)}, bf16[128,1536]{1,0:T(8,128)(2,1)}, u32[]{:S(2)}) copy-start(bf16[128,1536]{1,0:T(8,128)(2,1)} %copy-done.26) | copy-start | bytes 1179652
  193.9 21.0 %copy-start.38 = (f32[128,2]{0,1:T(2,128)S(1)}, f32[128,2]{0,1:T(2,128)}, u32[]{:S(2)}) copy-start(f32[128,2]{0,1:T(2,128)} %param.21) | copy-start | bytes 3076
  194.0 21.0 %all-to-all-start.3 = ((bf16[8,48,1536]{2,1,0:T(8,128)(2,1)}), bf16[8,48,1536]{2,1,0:T(8,128)(2,1)S(1)}, u32[]{:S(2)}, u32[]{:S(2)}) async-start(bf16[8,48,1536]{2,1,0:T(8,128)(2,1)} %bitcast.25), calls=%async_computation.3 | async-start | bytes 2359296 | tf_op jit(solution)/shard_map/all_to_all | solution.py:513
Sparse Core Ops, SparseCore 0:
  84.2 29.0 all-gather.2
  131.0 36.9 all-gather.4

commit v6 on v5

--- a/solution.py
+++ b/solution.py
@@ -121,23 +121,25 @@
         out[copy, TOK:, TOK:] = jnp.zeros((16, WIDTH - TOK), BF16)
 
 
-def piece_kernel(meta, gate, up, down, out, sems):
+def piece_kernel(meta, wq, wkv, wo, gate, up, down, out, sems):
+    y = meta[0]
     place = lax.rem(meta[1], 4)
-    piece = meta[0] * 4 + lax.rem(place, 2) * 2 + place // 2
-    wide = pl.ds(pl.multiple_of(piece * 96, 32), 96)
+    piece = y * 4 + lax.rem(place, 2) * 2 + place // 2
+    small = pl.ds(pl.multiple_of(y * 16, 16), 16)
     deep = pl.ds(pl.multiple_of(piece * 16, 16), 16)
-    copies = [
-        pltpu.make_async_copy(gate.at[wide], out.at[:96, :256], sems.at[0]),
-        pltpu.make_async_copy(up.at[wide], out.at[:96, 256:], sems.at[1]),
+    pairs = [
+        (wq.at[small], out.at[0:16]),
+        (wkv.at[small], out.at[16:32]),
+        (wo.at[small], out.at[32:48]),
     ]
+    for i in range(2):
+        wide = pl.ds(pl.multiple_of(piece * 96 + 48 * i, 16), 48)
+        pairs.append((gate.at[wide], out.at[48:96, 512 * i : 512 * i + 256]))
+        pairs.append((up.at[wide], out.at[48:96, 512 * i + 256 : 512 * i + 512]))
     for i in range(3):
-        copies.append(
-            pltpu.make_async_copy(
-                down.at[deep, i * 512 : i * 512 + 512],
-                out.at[96 + 16 * i : 112 + 16 * i],
-                sems.at[2 + i],
-            )
-        )
+        chunk = slice(512 * i, 512 * i + 512)
+        pairs.append((down.at[deep, chunk], out.at[48 + 16 * i : 64 + 16 * i, 1024:]))
+    copies = [pltpu.make_async_copy(a, b, sems.at[n]) for n, (a, b) in enumerate(pairs)]
     for copy in copies:
         copy.start()
     for copy in copies:
@@ -146,22 +148,26 @@
 
 def order_kernel(gate, up, down, out):
     for e in range(16):
-        low = e * 144
-        out[low : low + 96, :256] = gate[e * 96 : e * 96 + 96]
-        out[low : low + 96, 256:] = up[e * 96 : e * 96 + 96]
+        rows = slice(48 * e, 48 * e + 48)
+        for i in range(2):
+            low = 96 * e + 48 * i
+            out[rows, 512 * i : 512 * i + 256] = gate[low : low + 48]
+            out[rows, 512 * i + 256 : 512 * i + 512] = up[low : low + 48]
         for i in range(3):
-            out[low + 96 + 16 * i : low + 112 + 16 * i] = down[
-                e * 16 : e * 16 + 16, i * 512 : i * 512 + 512
-            ]
-
-
-def project_kernel(meta, near, across, wq, wkv, far, gain,
-                   q_out, kv_out, start_out, cols):
+            low = 48 * e + 16 * i
+            out[low : low + 16, 1024:] = down[16 * e : 16 * e + 16, 512 * i : 512 * i + 512]
+
+
+def project_kernel(meta, near, across, wq, wkv, wo, parts, gain,
+                   q_out, kv_out, start_out, wo_out, cols):
     zh, c = meta[2], meta[4]
     cols[0:64] = wq[...]
-    cols[64:128] = far[0:64]
     cols[pl.ds(pl.multiple_of(128 + zh * 64, 64), 64), :] = wkv[...]
-    cols[pl.ds(pl.multiple_of(192 - zh * 64, 64), 64), :] = far[64:128]
+    wo_out[0:64] = wo[...]
+    for i in range(4):
+        cols[64 + 16 * i : 80 + 16 * i] = parts[i, 0:16]
+        cols[pl.ds(pl.multiple_of(192 - zh * 64 + 16 * i, 16), 16), :] = parts[i, 16:32]
+        wo_out[64 + 16 * i : 80 + 16 * i] = parts[i, 32:48]
     for k in range(4):
         for block, core in ((near, c), (across, 1 - c)):
             low = pl.multiple_of((2 * k + core) * TOK, TOK)
@@ -358,11 +364,15 @@
     for half, source in enumerate((own, given_a)):
         pltpu.make_async_copy(source, raw.at[half], sems.at[half]).wait()
         for e in range(16):
-            low = e * 144
-            wide[half, e * 96 : e * 96 + 96] = raw[half, low : low + 96]
+            for i in range(2):
+                low = 96 * e + 48 * i
+                wide[half, low : low + 48] = raw[
+                    half, 48 * e : 48 * e + 48, 512 * i : 512 * i + 512
+                ]
             for i in range(3):
+                low = 48 * e + 16 * i
                 deep[half, i * 256 + e * 16 : i * 256 + e * 16 + 16] = raw[
-                    half, low + 96 + 16 * i : low + 112 + 16 * i
+                    half, low : low + 16, 1024:
                 ]
         both = jnp.dot(arrived, wide[half], preferred_element_type=F32)
         gate, up = both[:, :256], both[:, 256:]
@@ -405,37 +415,25 @@
     wq, wkv = w_query.T, key_value_weight.T
     ids = expert_ids.T
 
-    parts = jnp.concatenate(
-        [lax.dynamic_slice_in_dim(w, y * 16, 16, 0) for w in (wq, wkv, w_out)], axis=0
-    )
-    parts = swap_half(parts)
     (block,) = call(
         pack_kernel, [((4, TOK + 16, WIDTH), BF16)], [SMEM] + [VMEM] * 3, nbytes=0
     )(meta, tokens, segment_ids[None, :], ids)
     (piece,) = call(
         piece_kernel,
-        [((144, 512), BF16)],
-        [SMEM] + [HBM] * 3,
-        scratch=[pltpu.SemaphoreType.DMA((5,))],
-        nbytes=0,
-    )(meta, w_gate, w_up, w_down)
+        [((96, WIDTH), BF16)],
+        [SMEM] + [HBM] * 6,
+        scratch=[pltpu.SemaphoreType.DMA((10,))],
+    )(meta, wq, wkv, w_out, w_gate, w_up, w_down)
     near = lax.all_to_all(block, "x", split_axis=0, concat_axis=0, tiled=True)
-    piece = swap_half(piece)
-    near, parts, piece = lax.optimization_barrier((near, parts, piece))
-    parts = gather(parts, "y").reshape(4, 3, 16, WIDTH)
-    far_cols = parts[:, :2].transpose(1, 0, 2, 3).reshape(128, WIDTH)
+    near, piece = lax.optimization_barrier((near, swap_half(piece)))
+    parts = gather(piece[:48], "y")
     across = swap_core(near)
-    beside = swap_near(piece, 2)
-    gain, beside = lax.optimization_barrier((attn_gain[None, :], beside))
-    q, kv, start = call(
+    q, kv, start, out_rows = call(
         project_kernel,
-        [((ROWS, 128), BF16), ((ROWS, 128), BF16), ((ROWS, 128), F32)],
-        [SMEM] + [VMEM] * 6,
+        [((ROWS, 128), BF16), ((ROWS, 128), BF16), ((ROWS, 128), F32), ((128, WIDTH), BF16)],
+        [SMEM] + [VMEM] * 7,
         scratch=[pltpu.VMEM((256, WIDTH), BF16)],
-        flops=0,
-        nbytes=0,
-    )(meta, near, across, wq, wkv, far_cols, gain)
-    out_rows = jnp.concatenate([w_out, after(parts, across)[:, 2].reshape(64, WIDTH)], axis=0)
+    )(meta, near, across, wq, wkv, w_out, parts, attn_gain[None, :])
     out_all = lax.all_gather(out_rows, ROW, axis=0, tiled=True)
 
     partner = swap_half(kv)
@@ -455,11 +453,12 @@
         nbytes=5000000,
     )(meta, after(near, kv), across)
 
-    (own,) = call(order_kernel, [((2304, 512), BF16)], [VMEM] * 3, nbytes=5000000)(
+    (own,) = call(order_kernel, [((768, WIDTH), BF16)], [VMEM] * 3, nbytes=5000000)(
         *(after(w, kv) for w in (w_gate, w_up, w_down))
     )
-    pair = in_pair(piece, beside, zr)
-    four = in_pair(pair, swap_near(after(pair, kv), 1), zp)
+    piece = after(piece[48:], kv)
+    pair = in_pair(piece, swap_near(piece, 2), zr)
+    four = in_pair(pair, swap_near(pair, 1), zp)
     partner, sums, pick, own, four, out_all = lax.optimization_barrier(
         (partner, sums, pick, own, four, out_all)
     )
@@ -499,7 +498,7 @@
         [((TOK, WIDTH), BF16), ((8 * CAP, WIDTH), BF16)],
         [SMEM] + [VMEM] * 6 + [HBM] * 4,
         scratch=[
-            pltpu.VMEM((2, 2304, 512), BF16),
+            pltpu.VMEM((2, 768, WIDTH), BF16),
             pltpu.VMEM((2, WIDTH, 512), BF16),
             pltpu.VMEM((2, 768, 512), BF16),
             pltpu.SemaphoreType.DMA((2,)),

time: 225 us -> 232 us (1.031)
  starting transfers between devices: 51.5 us -> 73.7 us
  blocking collectives: 13.3 us -> 0 us
  waiting for transfers between devices: 90.6 us -> 78.2 us
  local copies, waits for them, and re-layouts: 16.2 us -> 28 us
  other arithmetic: 3.79 us -> 1.06 us
    ppermute x10 -> x9, waiting for transfers between devices: 58.6 us -> 39.1 us  [permute(): return lax.ppermute(block, AXES, route)]
    ppermute x10 -> x9, starting transfers between devices: 38.5 us -> 56.2 us  [permute(): return lax.ppermute(block, AXES, route)]
    all_to_all x1 -> x0, blocking collectives: 13.3 us -> none  [gather(): return lax.all_to_all(wide, axis, split_axis=0, concat_axis=0, tiled=True)]
    unnamed x92 -> x94, local copies, waits for them, and re-layouts: 15.2 us -> 25.7 us
    all_to_all x0 -> x1, waiting for transfers between devices: none -> 8.07 us  [gather(): return lax.all_to_all(wide, axis, split_axis=0, concat_axis=0, tiled=True)]
    all_to_all x0 -> x1, starting transfers between devices: none -> 4.68 us  [gather(): return lax.all_to_all(wide, axis, split_axis=0, concat_axis=0, tiled=True)]
  transfers between devices with their start and end apart: 15 -> 15, of which waited for: 8 -> 8; matrix products, arithmetic and copies ran while one was open for 1% -> 1% of each run, Pallas kernels for 10% -> 8%
where the time goes in v6:
time: 232 us; the launch traced here: 230 us
  waiting for transfers between devices  78.2 us (34%)
  starting transfers between devices  73.7 us (32%)
  Pallas kernels  34.1 us (15%)
  local copies, waits for them, and re-layouts  28 us (12%)
  between operations  14.5 us (6%)
    ppermute x9, starting transfers between devices, permute(): return lax.ppermute(block, AXES, route)  56.2 us
    ppermute x9, waiting for transfers between devices, permute(): return lax.ppermute(block, AXES, route)  39.1 us
    unnamed x94, local copies, waits for them, and re-layouts  25.7 us
    all_to_all x1, waiting for transfers between devices, body(): lax.all_to_all(expert_out.reshape(8, CAP, WIDTH), ROW, split_axis=0, conc...  15.9 us
    all_to_all x1, waiting for transfers between devices, body(): heads = lax.all_to_all(heads, 'x', split_axis=0, concat_axis=0, tiled=True)  15.1 us
    all_to_all x1, waiting for transfers between devices, gather(): return lax.all_to_all(wide, axis, split_axis=0, concat_axis=0, tiled=True)  8.07 us
    pallas_call x1, Pallas kernels, body(): call(expert_kernel, [((TOK, WIDTH), BF16), ((8 * CAP, WIDTH), BF16)], [SM...  7.7 us
    pallas_call x1, Pallas kernels, body(): call(before_kernel, [((4, ROWS + 256, 128), BF16)], [VMEM] * 7, scratch=[...  4.73 us
  transfers between devices with their start and end apart: 15, of which 8 were waited for; matrix products, arithmetic and copies ran while one was open for 1% of the time, Pallas kernels for 8%

profile of v6, /device:TPU:24, one launch (start us, length us, event | category | flops | bytes accessed | tf_op | source)
XLA Modules:
  0.0 229.6 jit_solution(12612005729815084768)
XLA Ops:
  7.3 1.0 copy-done.11
  8.3 0.7 copy-done.38
  8.9 0.7 copy-done.41
  9.6 1.9 shard_map.140
  11.5 4.4 %all-to-all-start = ((bf16[4,144,1536]{2,1,0:T(8,128)(2,1)}), bf16[4,144,1536]{2,1,0:T(8,128)(2,1)S(1)}, u32[]{:S(2)}, u32[]{:S(2)}) async-start(bf16[4,144,1536]{2,1,0:T(8,128)(2,1)} %shard_map.140), calls=%async_computation | async-start | bytes 3538944 | tf_op jit(solution)/shard_map/all_to_all | solution.py:427
  16.0 1.1 copy-done.5
  17.1 1.1 copy-done.7
  18.2 0.9 shard_map.141
  19.2 15.7 %collective-permute-start = (bf16[96,1536]{1,0:T(8,128)(2,1)S(1)}, bf16[96,1536]{1,0:T(8,128)(2,1)S(1)}, u32[]{:S(2)}, u32[]{:S(2)}) collective-permute-start(bf16[96,1536]{1,0:T(8,128)(2,1)S(1)} %shard_map.141), channel_id=1, source_target_pairs={{0,8},{1,9},{2,10},{3,11},{4,12},{5,13},{6,14},{7,15},{8,0},{9,1},... | collective-permute-start | bytes 884744 | tf_op jit(solution)/shard_map/ppermute | solution.py:36
  34.9 11.3 %collective-permute-done = bf16[96,1536]{1,0:T(8,128)(2,1)S(1)} collective-permute-done((bf16[96,1536]{1,0:T(8,128)(2,1)S(1)}, bf16[96,1536]{1,0:T(8,128)(2,1)S(1)}, u32[]{:S(2)}, u32[]{:S(2)}) %collective-permute-start) | collective-permute-done | bytes 294944 | tf_op jit(solution)/shard_map/ppermute | solution.py:36
  46.1 1.9 collective-permute-start.1
  48.1 0.7 fusion
  48.7 0.9 broadcast_in_dim.16
  49.6 4.7 %all-to-all-start.1 = ((bf16[4,48,1536]{2,1,0:T(8,128)(2,1)}), bf16[4,48,1536]{2,1,0:T(8,128)(2,1)S(1)}, u32[]{:S(2)}, u32[]{:S(2)}) async-start(bf16[4,48,1536]{2,1,0:T(8,128)(2,1)} %broadcast_in_dim.16), calls=%async_computation.1 | async-start | bytes 1179648 | tf_op jit(solution)/shard_map/all_to_all | solution.py:74
  54.3 0.7 broadcast_in_dim.17.gain
  55.0 8.1 %all-to-all-done.1.parts = bf16[4,48,1536]{2,1,0:T(8,128)(2,1)S(1)} async-done(((bf16[4,48,1536]{2,1,0:T(8,128)(2,1)}), bf16[4,48,1536]{2,1,0:T(8,128)(2,1)S(1)}, u32[]{:S(2)}, u32[]{:S(2)}) %all-to-all-start.1) | async-done | bytes 589856 | tf_op jit(solution)/shard_map/all_to_all | solution.py:74
  63.1 0.9 copy-done.22
  64.0 3.9 %shard_map.142 = (bf16[1024,128]{1,0:T(8,128)(2,1)S(1)}, bf16[1024,128]{1,0:T(8,128)(2,1)S(1)}, f32[1024,128]{1,0:T(8,128)S(1)}, bf16[128,1536]{1,0:T(8,128)(2,1)S(1)}) custom-call(s32[6]{0:T(128)S(1)} %stack.27.meta, bf16[4,144,1536]{2,1,0:T(8,128)(2,1)S(1)} %all-to-all-done.near, bf16[4,144,1536]{2,1,0:T(8,128)(2,1)} %collective-permute-done.1.across, ...), custom_call_target="tpu_custom_call" | custom-call | tf_op jit(solution)/shard_map/pallas_call | solution.py:431
  67.9 0.7 copy-done.16
  68.6 0.8 copy-done.23
  69.5 0.7 copy-done.32
  70.2 0.7 copy-done.33
  71.0 12.5 %collective-permute-start.2 = (bf16[1024,128]{1,0:T(8,128)(2,1)}, bf16[1024,128]{1,0:T(8,128)(2,1)S(1)}, u32[]{:S(2)}, u32[]{:S(2)}) collective-permute-start(bf16[1024,128]{1,0:T(8,128)(2,1)} %copy-done.16), channel_id=1, source_target_pairs={{0,8},{1,9},{2,10},{3,11},{4,12},{5,13},{6,14},{7,15},{8,0},{9,1},... | collective-permute-start | bytes 786440 | tf_op jit(solution)/shard_map/ppermute | solution.py:36
  83.5 17.1 %collective-permute-start.3 = (bf16[48,1536]{1,0:T(8,128)(2,1)}, bf16[48,1536]{1,0:T(8,128)(2,1)S(1)}, u32[]{:S(2)}, u32[]{:S(2)}) collective-permute-start(bf16[48,1536]{1,0:T(8,128)(2,1)} %get-tuple-element.43), channel_id=1, source_target_pairs={{0,32},{1,33},{2,34},{3,35},{4,36},{5,37},{6,38},{7,39},{8,40},{9,... | collective-permute-start | bytes 442376 | tf_op jit(solution)/shard_map/ppermute | solution.py:36
  100.6 1.1 copy-done.6
  101.8 1.2 copy-done.8
  103.0 0.2 shard_map.145.own
  103.2 4.1 %shard_map.144 = (bf16[384,128]{1,0:T(8,128)(2,1)S(1)}, bf16[384,128]{1,0:T(8,128)(2,1)S(1)}, bf16[384,1536]{1,0:T(8,128)(2,1)S(1)}) custom-call(s32[6]{0:T(128)S(1)} %stack.27.meta, bf16[4,144,1536]{2,1,0:T(8,128)(2,1)S(1)} %copy-done.2, bf16[4,144,1536]{2,1,0:T(8,128)(2,1)} %collective-permute-done.1.across), custom_call_target="tpu_custom_call" | custom-call | flops 2000000000 | bytes 5000000 | tf_op jit(solution)/shard_map/pallas_call | solution.py:448
  107.3 0.6 copy-done.36
  107.9 15.3 %collective-permute-done.3 = bf16[48,1536]{1,0:T(8,128)(2,1)S(1)} collective-permute-done((bf16[48,1536]{1,0:T(8,128)(2,1)}, bf16[48,1536]{1,0:T(8,128)(2,1)S(1)}, u32[]{:S(2)}, u32[]{:S(2)}) %collective-permute-start.3) | collective-permute-done | bytes 147488 | tf_op jit(solution)/shard_map/ppermute | solution.py:36
  123.3 1.9 collective-permute-start.4
  125.3 3.8 %shard_map.143 = (f32[1024,128]{1,0:T(8,128)S(1)}, f32[1024,128]{1,0:T(8,128)S(1)}, f32[1024,128]{1,0:T(8,128)S(1)}, s32[8,128]{1,0:T(8,128)S(1)}) custom-call(bf16[1024,128]{1,0:T(8,128)(2,1)S(1)} %copy-done.34, bf16[1024,128]{1,0:T(8,128)(2,1)S(1)} %copy-done.17, f32[1024,128]{1,0:T(8,128)S(1)} %copy-done.24, s32[2,128]{1,0:T(2,128)S(1)} %bitcast.21), custom_call_target="tpu_custom_call" | custom-call | flops 4000000000 | bytes 3000000 | tf_op jit(solution)/shard_map/pallas_call | solution.py:440
  129.1 0.8 copy-done.26
  129.9 0.8 copy-done.28
  130.7 0.8 copy-done.30
  131.5 2.6 %collective-permute-done.4 = bf16[96,1536]{1,0:T(8,128)(2,1)S(1)} collective-permute-done((bf16[96,1536]{1,0:T(8,128)(2,1)S(1)}, bf16[96,1536]{1,0:T(8,128)(2,1)S(1)}, u32[]{:S(2)}, u32[]{:S(2)}) %collective-permute-start.4) | collective-permute-done | bytes 294944 | tf_op jit(solution)/shard_map/ppermute | solution.py:36
  134.2 0.9 pad_maximum_fusion
  135.2 2.4 %collective-permute-start.5 = (bf16[1024,128]{1,0:T(8,128)(2,1)S(1)}, bf16[1024,128]{1,0:T(8,128)(2,1)S(1)}, u32[]{:S(2)}, u32[]{:S(2)}) collective-permute-start(bf16[1024,128]{1,0:T(8,128)(2,1)S(1)} %broadcast_select_fusion.3), channel_id=1, source_target_pairs={{0,16},{1,17},{2,18},{3,19},{4,20},{5,21},{6,22},{7,23},{16,32},{1... | collective-permute-start | bytes 786440 | tf_op jit(solution)/shard_map/ppermute | solution.py:36
  137.6 2.4 %shard_map.146.pages = bf16[1024,128]{1,0:T(8,128)(2,1)S(1)} custom-call(s32[6]{0:T(128)S(1)} %stack.27.meta, s32[1,128]{1,0:T(1,128)S(1)} %copy-done.42, bf16[1024,128]{1,0:T(8,128)(2,1)S(1)} %copy-done.18, bf16[1024,128]{1,0:T(8,128)(2,1)S(1)} %collective-permute-done.2.partner), custom_call_target="tpu_custom_call" | custom-call | tf_op jit(solution)/shard_map/pallas_call | solution.py:469
  140.0 6.6 %collective-permute-done.5 = bf16[1024,128]{1,0:T(8,128)(2,1)S(1)} collective-permute-done((bf16[1024,128]{1,0:T(8,128)(2,1)S(1)}, bf16[1024,128]{1,0:T(8,128)(2,1)S(1)}, u32[]{:S(2)}, u32[]{:S(2)}) %collective-permute-start.5) | collective-permute-done | bytes 262176 | tf_op jit(solution)/shard_map/ppermute | solution.py:36
  146.7 1.0 copy-done.25
  147.7 1.0 copy-done.27
  148.8 1.0 copy-done.29
  149.8 1.0 copy-done.31
  150.9 1.0 copy-done.35
  151.8 4.7 %shard_map.147 = bf16[4,1280,128]{2,1,0:T(8,128)(2,1)S(1)} custom-call(bf16[1024,128]{1,0:T(8,128)(2,1)S(1)} %copy-done.35, bf16[1024,128]{1,0:T(8,128)(2,1)S(1)} %broadcast_select_fusion.2.kv, f32[1024,128]{1,0:T(8,128)S(1)} %copy-done.25, f32[1024,128]{1,0:T(8,128)S(1)} %copy-done.27, f32[1024,128]{1,0:T(8,128)S(1)} %copy-done.29, ...), custom_call_target="tpu_custom_call" | custom-call | tf_op jit(solution)/shard_map/pallas_call | solution.py:477
  156.6 1.1 copy-done.3
  157.7 4.7 %all-to-all-start.2 = ((bf16[4,1280,128]{2,1,0:T(8,128)(2,1)}), bf16[4,1280,128]{2,1,0:T(8,128)(2,1)}, u32[]{:S(2)}, u32[]{:S(2)}) async-start(bf16[4,1280,128]{2,1,0:T(8,128)(2,1)} %copy-done.3), calls=%async_computation.2 | async-start | bytes 2621440 | tf_op jit(solution)/shard_map/all_to_all | solution.py:485
  162.4 1.3 collective-permute-start.7
  163.6 15.1 %all-to-all-done.2.heads = bf16[4,1280,128]{2,1,0:T(8,128)(2,1)} async-done(((bf16[4,1280,128]{2,1,0:T(8,128)(2,1)}), bf16[4,1280,128]{2,1,0:T(8,128)(2,1)}, u32[]{:S(2)}, u32[]{:S(2)}) %all-to-all-start.2) | async-done | bytes 1310752 | tf_op jit(solution)/shard_map/all_to_all | solution.py:485
  178.7 0.9 copy-done.37
  179.6 1.8 shard_map.148
  181.4 0.8 copy-done.43
  182.2 1.4 collective-permute-start.8
  183.6 1.9 collective-permute-start.6
  185.6 3.2 %collective-permute-done.6.got = bf16[640,512]{1,0:T(8,128)(2,1)S(1)} collective-permute-done((bf16[640,512]{1,0:T(8,128)(2,1)}, bf16[640,512]{1,0:T(8,128)(2,1)S(1)}, u32[]{:S(2)}, u32[]{:S(2)}) %collective-permute-start.6) | collective-permute-done | bytes 655392 | tf_op jit(solution)/shard_map/ppermute | solution.py:36
  188.8 1.5 copy-done.44
  190.4 1.3 copy-done.15
  191.6 7.7 %shard_map.149 = (bf16[128,1536]{1,0:T(8,128)(2,1)S(1)}, bf16[384,1536]{1,0:T(8,128)(2,1)S(1)}) custom-call(s32[6]{0:T(128)S(1)} %stack.27.meta, bf16[640,512]{1,0:T(8,128)(2,1)S(1)} %get-tuple-element.61.keep, bf16[640,512]{1,0:T(8,128)(2,1)S(1)} %collective-permute-done.6.got, bf16[1024,1536]{1,0:T(8,128)(2,1)} %all-gather.3.cloned.1.call-done.wo_all, ...), custom_call_target="tpu_custom_call" | custom-call | tf_op jit(solution)/shard_map/pallas_call | solution.py:496
  199.4 1.0 copy-done.13
  200.4 3.7 %all-to-all-start.3 = ((bf16[8,48,1536]{2,1,0:T(8,128)(2,1)}), bf16[8,48,1536]{2,1,0:T(8,128)(2,1)S(1)}, u32[]{:S(2)}, u32[]{:S(2)}) async-start(bf16[8,48,1536]{2,1,0:T(8,128)(2,1)} %bitcast.15), calls=%async_computation.3 | async-start | bytes 2359296 | tf_op jit(solution)/shard_map/all_to_all | solution.py:512
  204.1 1.4 shard_map.151
  205.5 15.9 %all-to-all-done.3 = bf16[8,48,1536]{2,1,0:T(8,128)(2,1)S(1)} async-done(((bf16[8,48,1536]{2,1,0:T(8,128)(2,1)}), bf16[8,48,1536]{2,1,0:T(8,128)(2,1)S(1)}, u32[]{:S(2)}, u32[]{:S(2)}) %all-to-all-start.3) | async-done | bytes 1179680 | tf_op jit(solution)/shard_map/all_to_all | solution.py:512
  221.4 1.4 shard_map.150
  (85 shorter events, 0.5 us)
Async XLA Ops:
  7.3 1.0 copy-start.11
  8.3 0.7 copy-start.38
  8.9 0.7 copy-start.41
  11.5 4.5 %copy-start.4 = (bf16[1536,256]{1,0:T(8,128)(2,1)S(1)}, bf16[1536,256]{1,0:T(8,128)(2,1)}, u32[]{:S(2)}) copy-start(bf16[1536,256]{1,0:T(8,128)(2,1)} %gate.2) | copy-start | bytes 2359300
  11.5 4.5 %copy-start.19 = (bf16[1536,64]{0,1:T(8,128)(2,1)S(1)}, bf16[1536,64]{0,1:T(8,128)(2,1)}, u32[]{:S(2)}) copy-start(bf16[1536,64]{0,1:T(8,128)(2,1)} %param.16) | copy-start | bytes 589828
  11.5 4.5 %copy-start.20 = (bf16[1536,64]{0,1:T(8,128)(2,1)S(1)}, bf16[1536,64]{0,1:T(8,128)(2,1)}, u32[]{:S(2)}) copy-start(bf16[1536,64]{0,1:T(8,128)(2,1)} %param.17) | copy-start | bytes 589828
  11.5 4.5 %copy-start.21 = (bf16[64,1536]{1,0:T(8,128)(2,1)S(1)}, bf16[64,1536]{1,0:T(8,128)(2,1)}, u32[]{:S(2)}) copy-start(bf16[64,1536]{1,0:T(8,128)(2,1)} %wo.3) | copy-start | bytes 589828
  11.5 34.6 %all-to-all-start = ((bf16[4,144,1536]{2,1,0:T(8,128)(2,1)}), bf16[4,144,1536]{2,1,0:T(8,128)(2,1)S(1)}, u32[]{:S(2)}, u32[]{:S(2)}) async-start(bf16[4,144,1536]{2,1,0:T(8,128)(2,1)} %shard_map.140), calls=%async_computation | async-start | bytes 3538944 | tf_op jit(solution)/shard_map/all_to_all | solution.py:427
  16.0 1.1 copy-start.5
  17.1 1.1 copy-start.7
  19.2 27.0 %collective-permute-start = (bf16[96,1536]{1,0:T(8,128)(2,1)S(1)}, bf16[96,1536]{1,0:T(8,128)(2,1)S(1)}, u32[]{:S(2)}, u32[]{:S(2)}) collective-permute-start(bf16[96,1536]{1,0:T(8,128)(2,1)S(1)} %shard_map.141), channel_id=1, source_target_pairs={{0,8},{1,9},{2,10},{3,11},{4,12},{5,13},{6,14},{7,15},{8,0},{9,1},... | collective-permute-start | bytes 884744 | tf_op jit(solution)/shard_map/ppermute | solution.py:36
  46.1 21.8 %copy-start.1 = (bf16[4,144,1536]{2,1,0:T(8,128)(2,1)}, bf16[4,144,1536]{2,1,0:T(8,128)(2,1)S(1)}, u32[]{:S(2)}) copy-start(bf16[4,144,1536]{2,1,0:T(8,128)(2,1)S(1)} %all-to-all-done.near) | copy-start | bytes 5308420
  46.1 16.9 %collective-permute-start.1 = (bf16[4,144,1536]{2,1,0:T(8,128)(2,1)S(1)}, bf16[4,144,1536]{2,1,0:T(8,128)(2,1)}, u32[]{:S(2)}, u32[]{:S(2)}) collective-permute-start(bf16[4,144,1536]{2,1,0:T(8,128)(2,1)S(1)} %all-to-all-done.near), channel_id=1, source_target_pairs={{0,1},{1,0},{2,3},{3,2},{4,5},{5,4},{6,7},{7,6},{8,9},{9,8},{10,11... | collective-permute-start | bytes 5308424 | tf_op jit(solution)/shard_map/ppermute | solution.py:36
  49.6 13.5 %all-to-all-start.1 = ((bf16[4,48,1536]{2,1,0:T(8,128)(2,1)}), bf16[4,48,1536]{2,1,0:T(8,128)(2,1)S(1)}, u32[]{:S(2)}, u32[]{:S(2)}) async-start(bf16[4,48,1536]{2,1,0:T(8,128)(2,1)} %broadcast_in_dim.16), calls=%async_computation.1 | async-start | bytes 1179648 | tf_op jit(solution)/shard_map/all_to_all | solution.py:74
  54.3 80.8 %all-gather.3.cloned.1.call-start = ((), (), s32[]{:S(2)}) async-start(), calls=%async_computation.4 | async-start | bytes 3538944 | tf_op jit(solution)/shard_map/all_gather | solution.py:437
  63.1 0.9 copy-start.22
  67.9 0.7 copy-start.16
  68.6 0.8 copy-start.23
  69.5 0.7 copy-start.32
  70.2 0.7 copy-start.33
  70.9 111.3 %all-gather.5.cloned.1.call-start = ((), (), s32[]{:S(2)}) async-start(), calls=%async_computation.5 | async-start | bytes 2949120 | tf_op jit(solution)/shard_map/all_gather | solution.py:468
  71.0 64.1 %collective-permute-start.2 = (bf16[1024,128]{1,0:T(8,128)(2,1)}, bf16[1024,128]{1,0:T(8,128)(2,1)S(1)}, u32[]{:S(2)}, u32[]{:S(2)}) collective-permute-start(bf16[1024,128]{1,0:T(8,128)(2,1)} %copy-done.16), channel_id=1, source_target_pairs={{0,8},{1,9},{2,10},{3,11},{4,12},{5,13},{6,14},{7,15},{8,0},{9,1},... | collective-permute-start | bytes 786440 | tf_op jit(solution)/shard_map/ppermute | solution.py:36
  83.5 19.6 %copy-start.2 = (bf16[4,144,1536]{2,1,0:T(8,128)(2,1)S(1)}, bf16[4,144,1536]{2,1,0:T(8,128)(2,1)}, u32[]{:S(2)}) copy-start(bf16[4,144,1536]{2,1,0:T(8,128)(2,1)} %copy-done.1) | copy-start | bytes 5308420
  83.5 39.7 %collective-permute-start.3 = (bf16[48,1536]{1,0:T(8,128)(2,1)}, bf16[48,1536]{1,0:T(8,128)(2,1)S(1)}, u32[]{:S(2)}, u32[]{:S(2)}) collective-permute-start(bf16[48,1536]{1,0:T(8,128)(2,1)} %get-tuple-element.43), channel_id=1, source_target_pairs={{0,32},{1,33},{2,34},{3,35},{4,36},{5,37},{6,38},{7,39},{8,40},{9,... | collective-permute-start | bytes 442376 | tf_op jit(solution)/shard_map/ppermute | solution.py:36
  100.6 1.1 copy-start.6
  101.8 1.2 copy-start.8
  103.1 59.2 %copy-start = (bf16[768,1536]{1,0:T(8,128)(2,1)}, bf16[768,1536]{1,0:T(8,128)(2,1)S(1)}, u32[]{:S(2)}) copy-start(bf16[768,1536]{1,0:T(8,128)(2,1)S(1)} %shard_map.145.own) | copy-start | bytes 7077892
  103.1 20.1 %copy-start.45 = (bf16[48,1536]{1,0:T(8,128)(2,1)S(1)}, bf16[48,1536]{1,0:T(8,128)(2,1)}, u32[]{:S(2)}) copy-start(bf16[48,1536]{1,0:T(8,128)(2,1)} %get-tuple-element.43) | copy-start | bytes 442372
  103.1 22.1 %copy-start.17 = (bf16[1024,128]{1,0:T(8,128)(2,1)S(1)}, bf16[1024,128]{1,0:T(8,128)(2,1)}, u32[]{:S(2)}) copy-start(bf16[1024,128]{1,0:T(8,128)(2,1)} %copy-done.16) | copy-start | bytes 786436
  103.1 22.1 %copy-start.24 = (f32[1024,128]{1,0:T(8,128)S(1)}, f32[1024,128]{1,0:T(8,128)}, u32[]{:S(2)}) copy-start(f32[1024,128]{1,0:T(8,128)} %copy-done.23) | copy-start | bytes 1572868
  103.2 22.1 %copy-start.34 = (bf16[1024,128]{1,0:T(8,128)(2,1)S(1)}, bf16[1024,128]{1,0:T(8,128)(2,1)}, u32[]{:S(2)}) copy-start(bf16[1024,128]{1,0:T(8,128)(2,1)} %copy-done.33) | copy-start | bytes 786436
  103.2 22.1 %copy-start.39 = (s32[128,2]{0,1:T(2,128)S(1)}, s32[128,2]{0,1:T(2,128)}, u32[]{:S(2)}) copy-start(s32[128,2]{0,1:T(2,128)} %param.20) | copy-start | bytes 3076
  107.3 0.6 copy-start.36
  107.9 21.2 %copy-start.14 = (bf16[384,1536]{1,0:T(8,128)(2,1)}, bf16[384,1536]{1,0:T(8,128)(2,1)S(1)}, u32[]{:S(2)}) copy-start(bf16[384,1536]{1,0:T(8,128)(2,1)S(1)} %get-tuple-element.54.rows) | copy-start | bytes 3538948
  123.3 10.8 %collective-permute-start.4 = (bf16[96,1536]{1,0:T(8,128)(2,1)S(1)}, bf16[96,1536]{1,0:T(8,128)(2,1)S(1)}, u32[]{:S(2)}, u32[]{:S(2)}) collective-permute-start(bf16[96,1536]{1,0:T(8,128)(2,1)S(1)} %pad_maximum_fusion.1), channel_id=1, source_target_pairs={{0,16},{1,17},{2,18},{3,19},{4,20},{5,21},{6,22},{7,23},{8,24},{9,... | collective-permute-start | bytes 884744 | tf_op jit(solution)/shard_map/ppermute | solution.py:36
  129.1 0.8 copy-start.26
  129.9 0.8 copy-start.28
  130.7 0.8 copy-start.30
  131.5 3.6 %copy-start.18 = (bf16[1024,128]{1,0:T(8,128)(2,1)S(1)}, bf16[1024,128]{1,0:T(8,128)(2,1)}, u32[]{:S(2)}) copy-start(bf16[1024,128]{1,0:T(8,128)(2,1)} %copy-done.16) | copy-start | bytes 786436
  131.5 6.1 %copy-start.42 = (s32[1,128]{1,0:T(1,128)S(1)}, s32[1,128]{1,0:T(1,128)}, u32[]{:S(2)}) copy-start(s32[1,128]{1,0:T(1,128)} %table.1) | copy-start | bytes 1540
  135.2 11.5 %collective-permute-start.5 = (bf16[1024,128]{1,0:T(8,128)(2,1)S(1)}, bf16[1024,128]{1,0:T(8,128)(2,1)S(1)}, u32[]{:S(2)}, u32[]{:S(2)}) collective-permute-start(bf16[1024,128]{1,0:T(8,128)(2,1)S(1)} %broadcast_select_fusion.3), channel_id=1, source_target_pairs={{0,16},{1,17},{2,18},{3,19},{4,20},{5,21},{6,22},{7,23},{16,32},{1... | collective-permute-start | bytes 786440 | tf_op jit(solution)/shard_map/ppermute | solution.py:36
  146.7 1.0 copy-start.25
  147.7 1.0 copy-start.27
  148.8 1.0 copy-start.29
  149.8 1.0 copy-start.31
  150.9 1.0 copy-start.35
  156.6 1.1 copy-start.3
  157.7 27.9 %copy-start.46 = (f32[1536]{0:T(1024)S(1)}, f32[1536]{0:T(1024)}, u32[]{:S(2)}) copy-start(f32[1536]{0:T(1024)} %param.15) | copy-start | bytes 18436
  157.7 32.7 %copy-start.12 = (bf16[128,1536]{1,0:T(8,128)(2,1)S(1)}, bf16[128,1536]{1,0:T(8,128)(2,1)}, u32[]{:S(2)}) copy-start(bf16[128,1536]{1,0:T(8,128)(2,1)} %tokens.3) | copy-start | bytes 1179652
  157.7 21.0 %all-to-all-start.2 = ((bf16[4,1280,128]{2,1,0:T(8,128)(2,1)}), bf16[4,1280,128]{2,1,0:T(8,128)(2,1)}, u32[]{:S(2)}, u32[]{:S(2)}) async-start(bf16[4,1280,128]{2,1,0:T(8,128)(2,1)} %copy-done.3), calls=%async_computation.2 | async-start | bytes 2621440 | tf_op jit(solution)/shard_map/all_to_all | solution.py:485
  162.4 26.4 %collective-permute-start.7 = (bf16[768,1536]{1,0:T(8,128)(2,1)S(1)}, bf16[768,1536]{1,0:T(8,128)(2,1)}, u32[]{:S(2)}, u32[]{:S(2)}) collective-permute-start(bf16[768,1536]{1,0:T(8,128)(2,1)S(1)} %shard_map.145.own), channel_id=1, source_target_pairs={{1,0},{3,2},{5,4},{7,6},{8,9},{10,11},{12,13},{14,15},{17,16},{19,... | collective-permute-start | bytes 7077896 | tf_op jit(solution)/shard_map/ppermute | solution.py:36
  178.7 0.9 copy-start.37
  181.4 0.8 copy-start.43
  182.2 6.6 %collective-permute-start.8 = (bf16[768,1536]{1,0:T(8,128)(2,1)}, bf16[768,1536]{1,0:T(8,128)(2,1)S(1)}, u32[]{:S(2)}, u32[]{:S(2)}) collective-permute-start(bf16[768,1536]{1,0:T(8,128)(2,1)} %all-gather.5.cloned.1.call-done.other), channel_id=1, source_target_pairs={{0,1},{2,3},{4,5},{6,7},{9,8},{11,10},{13,12},{15,14},{16,17},{18,... | collective-permute-start | bytes 7077896 | tf_op jit(solution)/shard_map/ppermute | solution.py:36
  183.6 5.1 %collective-permute-start.6 = (bf16[640,512]{1,0:T(8,128)(2,1)}, bf16[640,512]{1,0:T(8,128)(2,1)S(1)}, u32[]{:S(2)}, u32[]{:S(2)}) collective-permute-start(bf16[640,512]{1,0:T(8,128)(2,1)} %copy-done.43), channel_id=1, source_target_pairs={{0,1},{1,0},{2,3},{3,2},{4,5},{5,4},{6,7},{7,6},{8,9},{9,8},{10,11... | collective-permute-start | bytes 1966088 | tf_op jit(solution)/shard_map/ppermute | solution.py:36
  188.8 10.5 %copy-start.9 = (bf16[640,512]{1,0:T(8,128)(2,1)}, bf16[640,512]{1,0:T(8,128)(2,1)S(1)}, u32[]{:S(2)}) copy-start(bf16[640,512]{1,0:T(8,128)(2,1)S(1)} %collective-permute-done.6.got) | copy-start | bytes 1966084
  188.8 1.6 copy-start.44
  190.3 1.3 copy-start.15
  199.3 1.0 copy-start.13
  200.4 3.7 %copy-start.10 = (bf16[640,512]{1,0:T(8,128)(2,1)S(1)}, bf16[640,512]{1,0:T(8,128)(2,1)}, u32[]{:S(2)}) copy-start(bf16[640,512]{1,0:T(8,128)(2,1)} %copy-done.9) | copy-start | bytes 1966084
  200.4 21.0 %copy-start.40 = (f32[128,2]{0,1:T(2,128)S(1)}, f32[128,2]{0,1:T(2,128)}, u32[]{:S(2)}) copy-start(f32[128,2]{0,1:T(2,128)} %param.21) | copy-start | bytes 3076
  200.4 21.0 %all-to-all-start.3 = ((bf16[8,48,1536]{2,1,0:T(8,128)(2,1)}), bf16[8,48,1536]{2,1,0:T(8,128)(2,1)S(1)}, u32[]{:S(2)}, u32[]{:S(2)}) async-start(bf16[8,48,1536]{2,1,0:T(8,128)(2,1)} %bitcast.15), calls=%async_computation.3 | async-start | bytes 2359296 | tf_op jit(solution)/shard_map/all_to_all | solution.py:512
Sparse Core Ops, SparseCore 0:
  71.1 49.7 all-gather.2
  135.3 30.6 all-gather.4

commit v7 on v6

--- a/solution.py
+++ b/solution.py
@@ -78,7 +78,7 @@
     return lax.optimization_barrier((value,) + earlier)[0]
 
 
-def call(kernel, outs, in_specs, scratch=(), flops=0, nbytes=0, limit=48):
+def call(kernel, outs, in_specs, scratch=(), flops=0, nbytes=0, limit=16):
     outs = [jax.ShapeDtypeStruct(shape, kind) for shape, kind in outs]
     return pl.pallas_call(
         kernel,
@@ -219,7 +219,7 @@
 STEP = 256
 
 
-def own_kernel(q, kv, start, ids, sum_out, max_out, den_out, slots_out, keys, values):
+def own_kernel(q, kv, start, ids, sum_out, stat_out, slots_out, keys, values):
     keys[...], values[...] = split_kv(kv)
     low_lane = lax.broadcasted_iota(I32, (STEP, 128), 1) < 64
     for block in range(ROWS // STEP):
@@ -238,8 +238,12 @@
             den = jnp.sum(weights, axis=-1, keepdims=True)
             part = jnp.dot(weights.astype(BF16), values[:span], preferred_element_type=F32)
             parts.append((part, top, den))
-        for out, one, two in zip((sum_out, max_out, den_out), *parts):
-            out[low:span] = jnp.where(low_lane, one, two)
+        sum_out[low:span] = jnp.where(low_lane, parts[0][0], parts[1][0])
+        lane = lax.broadcasted_iota(I32, (STEP, 128), 1)
+        stats = jnp.where(lane == 0, start[low:span, 0:1], parts[0][1])
+        for n, column_of in ((2, parts[1][1]), (3, parts[0][2]), (4, parts[1][2])):
+            stats = jnp.where(lane == n, column_of, stats)
+        stat_out[low:span] = stats
     choice = [ids[k : k + 1].astype(F32) for k in range(2)]
     down = [column(v) for v in choice]
     earlier = lax.broadcasted_iota(I32, (TOK, TOK), 0) < lax.broadcasted_iota(I32, (TOK, TOK), 1)
@@ -253,7 +257,7 @@
     slots_out[...] = jnp.where(row == 0, result[0], result[1])
 
 
-def before_kernel(q, kv, start, sums, maxes, dens, pages, out, keys, values):
+def before_kernel(q, kv, sums, stats, pages, out, keys, values):
     keys[...], values[...] = split_kv(kv)
     low_lane = lax.broadcasted_iota(I32, (STEP, 128), 1) < 64
     for block in range(ROWS // STEP):
@@ -262,21 +266,22 @@
         span = ROWS - low
         query = q[low:high]
         position = (low - ROWS + lax.broadcasted_iota(I32, (STEP, span), 1)).astype(F32)
-        allowed = position >= start[low:high, 0:1]
+        allowed = position >= stats[low:high, 0:1]
         parts = []
         for head in range(2):
             kept = jnp.where(low_lane if head == 0 else ~low_lane, query, jnp.zeros_like(query))
             scores = jnp.where(allowed, dot_nt(kept, keys[low:]) * 0.125, -1e30)
-            first = maxes[low:high, head * 64 : head * 64 + 1]
+            first = stats[low:high, 1 + head : 2 + head]
             top = jnp.maximum(first, jnp.max(scores, axis=-1, keepdims=True))
             weights = jnp.exp(scores - top)
             scale = jnp.exp(first - top)
             den = jnp.sum(weights, axis=-1, keepdims=True)
+            den += stats[low:high, 3 + head : 4 + head] * scale
             part = jnp.dot(weights.astype(BF16), values[low:], preferred_element_type=F32)
             parts.append((part, scale, den))
         part, scale, den = (jnp.where(low_lane, one, two) for one, two in zip(*parts))
         total = sums[low:high] * scale + part
-        result = (total / (dens[low:high] * scale + den)).astype(BF16)
+        result = (total / den).astype(BF16)
         for copy in range(4):
             out[copy, low:high, :] = result
     for k in range(4):
@@ -428,18 +433,20 @@
     near, piece = lax.optimization_barrier((near, swap_half(piece)))
     parts = gather(piece[:48], "y")
     across = swap_core(near)
+    beside = swap_near(piece[48:], 2)
+    gain, beside = lax.optimization_barrier((attn_gain[None, :], beside))
     q, kv, start, out_rows = call(
         project_kernel,
         [((ROWS, 128), BF16), ((ROWS, 128), BF16), ((ROWS, 128), F32), ((128, WIDTH), BF16)],
         [SMEM] + [VMEM] * 7,
         scratch=[pltpu.VMEM((256, WIDTH), BF16)],
-    )(meta, near, across, wq, wkv, w_out, parts, attn_gain[None, :])
+    )(meta, near, across, wq, wkv, w_out, parts, gain)
     out_all = lax.all_gather(out_rows, ROW, axis=0, tiled=True)
 
     partner = swap_half(kv)
-    sums, maxes, dens, slots = call(
+    sums, stats, slots = call(
         own_kernel,
-        [((ROWS, 128), F32)] * 3 + [((8, TOK), I32)],
+        [((ROWS, 128), F32)] * 2 + [((8, TOK), I32)],
         [VMEM] * 4,
         scratch=[pltpu.VMEM((ROWS, 128), BF16)] * 2,
         flops=4000000000,
@@ -456,8 +463,7 @@
     (own,) = call(order_kernel, [((768, WIDTH), BF16)], [VMEM] * 3, nbytes=5000000)(
         *(after(w, kv) for w in (w_gate, w_up, w_down))
     )
-    piece = after(piece[48:], kv)
-    pair = in_pair(piece, swap_near(piece, 2), zr)
+    pair = in_pair(after(piece[48:], kv), after(beside, kv), zr)
     four = in_pair(pair, swap_near(pair, 1), zp)
     partner, sums, pick, own, four, out_all = lax.optimization_barrier(
         (partner, sums, pick, own, four, out_all)
@@ -477,11 +483,11 @@
     (heads,) = call(
         before_kernel,
         [((4, ROWS + 256, 128), BF16)],
-        [VMEM] * 7,
+        [VMEM] * 5,
         scratch=[pltpu.VMEM((ROWS, 128), BF16)] * 2,
         flops=0,
         nbytes=0,
-    )(q, previous, start, sums, maxes, dens, pages)
+    )(q, previous, sums, stats, pages)
     heads = lax.all_to_all(heads, "x", split_axis=0, concat_axis=0, tiled=True)
     keep, give = call(
         split_kernel,
@@ -503,6 +509,7 @@
             pltpu.VMEM((2, 768, 512), BF16),
             pltpu.SemaphoreType.DMA((2,)),
         ],
+        limit=40,
         flops=0,
         nbytes=0,
     )(meta, keep, got, out_all, chosen, tokens, ffn_gain[None, :], own, other, given_a, given_b)

time: 232 us -> 225 us (0.970)
  waiting for transfers between devices: 78.2 us -> 71 us
  starting transfers between devices: 73.7 us -> 76.7 us
    all_to_all x1, waiting for transfers between devices: 8.07 us -> 0.01 us  [gather(): return lax.all_to_all(wide, axis, split_axis=0, concat_axis=0, tiled=True)]
    ppermute x9, starting transfers between devices: 56.2 us -> 59.1 us  [permute(): return lax.ppermute(block, AXES, route)]
    unnamed x94 -> x88, local copies, waits for them, and re-layouts: 25.7 us -> 24 us
  transfers between devices with their start and end apart: 15 -> 15, of which waited for: 8 -> 7; matrix products, arithmetic and copies ran while one was open for 1% -> 2% of each run, Pallas kernels for 8% -> 8%
where the time goes in v7:
time: 225 us; the launch traced here: 223 us
  starting transfers between devices  76.7 us (34%)
  waiting for transfers between devices  71 us (32%)
  Pallas kernels  32.5 us (14%)
  local copies, waits for them, and re-layouts  26.3 us (12%)
  between operations  14.5 us (6%)
    ppermute x9, starting transfers between devices, permute(): return lax.ppermute(block, AXES, route)  59.1 us
    ppermute x9, waiting for transfers between devices, permute(): return lax.ppermute(block, AXES, route)  39 us
    unnamed x88, local copies, waits for them, and re-layouts  24 us
    all_to_all x1, waiting for transfers between devices, body(): heads = lax.all_to_all(heads, 'x', split_axis=0, concat_axis=0, tiled=True)  16.1 us
    all_to_all x1, waiting for transfers between devices, body(): lax.all_to_all(expert_out.reshape(8, CAP, WIDTH), ROW, split_axis=0, conc...  15.9 us
    pallas_call x1, Pallas kernels, body(): call(expert_kernel, [((TOK, WIDTH), BF16), ((8 * CAP, WIDTH), BF16)], [SM...  6.52 us
    pallas_call x1, Pallas kernels, body(): call(before_kernel, [((4, ROWS + 256, 128), BF16)], [VMEM] * 5, scratch=[...  5.06 us
    all_to_all x1, starting transfers between devices, body(): heads = lax.all_to_all(heads, 'x', split_axis=0, concat_axis=0, tiled=True)  4.69 us
  transfers between devices with their start and end apart: 15, of which 7 were waited for; matrix products, arithmetic and copies ran while one was open for 2% of the time, Pallas kernels for 8%

profile of v7, /device:TPU:24, one launch (start us, length us, event | category | flops | bytes accessed | tf_op | source)
XLA Modules:
  0.0 223.1 jit_solution(2787174708728404595)
XLA Ops:
  7.2 0.1 stack.27.meta
  7.3 1.0 copy-done.11
  8.3 0.7 copy-done.35
  8.9 0.7 copy-done.38
  9.6 1.9 shard_map.140
  11.5 4.4 %all-to-all-start = ((bf16[4,144,1536]{2,1,0:T(8,128)(2,1)}), bf16[4,144,1536]{2,1,0:T(8,128)(2,1)S(1)}, u32[]{:S(2)}, u32[]{:S(2)}) async-start(bf16[4,144,1536]{2,1,0:T(8,128)(2,1)} %shard_map.140), calls=%async_computation | async-start | bytes 3538944 | tf_op jit(solution)/shard_map/all_to_all | solution.py:432
  16.0 1.1 copy-done.4
  17.1 1.1 copy-done.6
  18.2 0.9 shard_map.141
  19.2 15.7 %collective-permute-start = (bf16[96,1536]{1,0:T(8,128)(2,1)S(1)}, bf16[96,1536]{1,0:T(8,128)(2,1)S(1)}, u32[]{:S(2)}, u32[]{:S(2)}) collective-permute-start(bf16[96,1536]{1,0:T(8,128)(2,1)S(1)} %shard_map.141), channel_id=1, source_target_pairs={{0,8},{1,9},{2,10},{3,11},{4,12},{5,13},{6,14},{7,15},{8,0},{9,1},... | collective-permute-start | bytes 884744 | tf_op jit(solution)/shard_map/ppermute | solution.py:36
  34.9 11.3 %collective-permute-done = bf16[96,1536]{1,0:T(8,128)(2,1)S(1)} collective-permute-done((bf16[96,1536]{1,0:T(8,128)(2,1)S(1)}, bf16[96,1536]{1,0:T(8,128)(2,1)S(1)}, u32[]{:S(2)}, u32[]{:S(2)}) %collective-permute-start) | collective-permute-done | bytes 294944 | tf_op jit(solution)/shard_map/ppermute | solution.py:36
  46.2 1.9 collective-permute-start.1
  48.1 0.7 fusion
  48.7 0.9 broadcast_in_dim.16
  49.7 4.7 %all-to-all-start.1 = ((bf16[4,48,1536]{2,1,0:T(8,128)(2,1)}), bf16[4,48,1536]{2,1,0:T(8,128)(2,1)S(1)}, u32[]{:S(2)}, u32[]{:S(2)}) async-start(bf16[4,48,1536]{2,1,0:T(8,128)(2,1)} %broadcast_in_dim.16), calls=%async_computation.1 | async-start | bytes 1179648 | tf_op jit(solution)/shard_map/all_to_all | solution.py:74
  54.4 8.6 %collective-permute-start.2 = (bf16[48,1536]{1,0:T(8,128)(2,1)}, bf16[48,1536]{1,0:T(8,128)(2,1)}, u32[]{:S(2)}, u32[]{:S(2)}) collective-permute-start(bf16[48,1536]{1,0:T(8,128)(2,1)} %get-tuple-element.46), channel_id=1, source_target_pairs={{0,32},{1,33},{2,34},{3,35},{4,36},{5,37},{6,38},{7,39},{8,40},{9,... | collective-permute-start | bytes 442376 | tf_op jit(solution)/shard_map/ppermute | solution.py:36
  63.0 0.7 broadcast_in_dim.17.gain
  63.7 3.5 %collective-permute-done.2 = bf16[48,1536]{1,0:T(8,128)(2,1)} collective-permute-done((bf16[48,1536]{1,0:T(8,128)(2,1)}, bf16[48,1536]{1,0:T(8,128)(2,1)}, u32[]{:S(2)}, u32[]{:S(2)}) %collective-permute-start.2) | collective-permute-done | bytes 147488 | tf_op jit(solution)/shard_map/ppermute | solution.py:36
  67.3 0.9 copy-done.22
  68.2 3.9 %shard_map.142 = (bf16[1024,128]{1,0:T(8,128)(2,1)S(1)}, bf16[1024,128]{1,0:T(8,128)(2,1)S(1)}, f32[1024,128]{1,0:T(8,128)S(1)}, bf16[128,1536]{1,0:T(8,128)(2,1)S(1)}) custom-call(s32[6]{0:T(128)S(1)} %stack.27.meta, bf16[4,144,1536]{2,1,0:T(8,128)(2,1)S(1)} %all-to-all-done.near, bf16[4,144,1536]{2,1,0:T(8,128)(2,1)} %collective-permute-done.1.across, ...), custom_call_target="tpu_custom_call" | custom-call | tf_op jit(solution)/shard_map/pallas_call | solution.py:438
  72.1 0.7 copy-done.16
  72.8 0.7 copy-done.29
  73.6 0.7 copy-done.30
  74.3 0.8 copy-done.41
  75.2 24.0 %collective-permute-start.3 = (bf16[1024,128]{1,0:T(8,128)(2,1)}, bf16[1024,128]{1,0:T(8,128)(2,1)S(1)}, u32[]{:S(2)}, u32[]{:S(2)}) collective-permute-start(bf16[1024,128]{1,0:T(8,128)(2,1)} %copy-done.16), channel_id=1, source_target_pairs={{0,8},{1,9},{2,10},{3,11},{4,12},{5,13},{6,14},{7,15},{8,0},{9,1},... | collective-permute-start | bytes 786440 | tf_op jit(solution)/shard_map/ppermute | solution.py:36
  99.2 1.0 broadcast_select_fusion.5
  100.2 2.1 collective-permute-start.4
  102.4 1.1 copy-done.5
  103.5 1.2 copy-done.7
  104.7 0.2 shard_map.145.own
  104.9 3.3 %shard_map.144 = (bf16[384,128]{1,0:T(8,128)(2,1)S(1)}, bf16[384,128]{1,0:T(8,128)(2,1)S(1)}, bf16[384,1536]{1,0:T(8,128)(2,1)S(1)}) custom-call(s32[6]{0:T(128)S(1)} %stack.27.meta, bf16[4,144,1536]{2,1,0:T(8,128)(2,1)S(1)} %copy-done.1, bf16[4,144,1536]{2,1,0:T(8,128)(2,1)} %collective-permute-done.1.across), custom_call_target="tpu_custom_call" | custom-call | flops 2000000000 | bytes 5000000 | tf_op jit(solution)/shard_map/pallas_call | solution.py:455
  108.2 0.6 copy-done.33
  108.8 3.8 %shard_map.143 = (f32[1024,128]{1,0:T(8,128)S(1)}, f32[1024,128]{1,0:T(8,128)S(1)}, s32[8,128]{1,0:T(8,128)S(1)}) custom-call(bf16[1024,128]{1,0:T(8,128)(2,1)S(1)} %copy-done.31, bf16[1024,128]{1,0:T(8,128)(2,1)S(1)} %copy-done.17, f32[1024,128]{1,0:T(8,128)S(1)} %copy-done.42, s32[2,128]{1,0:T(2,128)S(1)} %bitcast.21), custom_call_target="tpu_custom_call" | custom-call | flops 4000000000 | bytes 3000000 | tf_op jit(solution)/shard_map/pallas_call | solution.py:447
  112.6 0.8 copy-done.23
  113.4 0.8 copy-done.25
  114.2 13.3 %collective-permute-done.4 = bf16[96,1536]{1,0:T(8,128)(2,1)S(1)} collective-permute-done((bf16[96,1536]{1,0:T(8,128)(2,1)S(1)}, bf16[96,1536]{1,0:T(8,128)(2,1)S(1)}, u32[]{:S(2)}, u32[]{:S(2)}) %collective-permute-start.4) | collective-permute-done | bytes 294944 | tf_op jit(solution)/shard_map/ppermute | solution.py:36
  127.6 0.1 broadcast_select_fusion.1
  127.7 0.9 pad_maximum_fusion
  128.7 2.1 collective-permute-start.5
  130.8 2.4 %shard_map.146.pages = bf16[1024,128]{1,0:T(8,128)(2,1)S(1)} custom-call(s32[6]{0:T(128)S(1)} %stack.27.meta, s32[1,128]{1,0:T(1,128)S(1)} %copy-done.39, bf16[1024,128]{1,0:T(8,128)(2,1)S(1)} %copy-done.18, bf16[1024,128]{1,0:T(8,128)(2,1)S(1)} %collective-permute-done.3.partner), custom_call_target="tpu_custom_call" | custom-call | tf_op jit(solution)/shard_map/pallas_call | solution.py:475
  133.2 7.7 %collective-permute-done.5 = bf16[1024,128]{1,0:T(8,128)(2,1)S(1)} collective-permute-done((bf16[1024,128]{1,0:T(8,128)(2,1)S(1)}, bf16[1024,128]{1,0:T(8,128)(2,1)S(1)}, u32[]{:S(2)}, u32[]{:S(2)}) %collective-permute-start.5) | collective-permute-done | bytes 262176 | tf_op jit(solution)/shard_map/ppermute | solution.py:36
  140.9 1.0 copy-done.24
  142.0 1.1 copy-done.26
  143.1 1.0 copy-done.32
  144.0 5.1 %shard_map.147 = bf16[4,1280,128]{2,1,0:T(8,128)(2,1)S(1)} custom-call(bf16[1024,128]{1,0:T(8,128)(2,1)S(1)} %copy-done.32, bf16[1024,128]{1,0:T(8,128)(2,1)S(1)} %broadcast_select_fusion.2.kv, f32[1024,128]{1,0:T(8,128)S(1)} %copy-done.24, f32[1024,128]{1,0:T(8,128)S(1)} %copy-done.26, bf16[1024,128]{1,0:T(8,128)(2,1)S(1)} %shard_map.146.pages), custom_call_target="tpu_custom_call" | custom-call | tf_op jit(solution)/shard_map/pallas_call | solution.py:483
  149.1 1.1 copy-done.2
  150.2 4.7 %all-to-all-start.2 = ((bf16[4,1280,128]{2,1,0:T(8,128)(2,1)}), bf16[4,1280,128]{2,1,0:T(8,128)(2,1)}, u32[]{:S(2)}, u32[]{:S(2)}) async-start(bf16[4,1280,128]{2,1,0:T(8,128)(2,1)} %copy-done.2), calls=%async_computation.2 | async-start | bytes 2621440 | tf_op jit(solution)/shard_map/all_to_all | solution.py:491
  154.8 1.3 collective-permute-start.7
  156.1 16.1 %all-to-all-done.2.heads = bf16[4,1280,128]{2,1,0:T(8,128)(2,1)} async-done(((bf16[4,1280,128]{2,1,0:T(8,128)(2,1)}), bf16[4,1280,128]{2,1,0:T(8,128)(2,1)}, u32[]{:S(2)}, u32[]{:S(2)}) %all-to-all-start.2) | async-done | bytes 1310752 | tf_op jit(solution)/shard_map/all_to_all | solution.py:491
  172.2 0.9 copy-done.34
  173.1 1.8 shard_map.148
  174.9 0.9 copy-done.40
  175.7 1.4 collective-permute-start.8
  177.2 1.9 collective-permute-start.6
  179.1 3.2 %collective-permute-done.6.got = bf16[640,512]{1,0:T(8,128)(2,1)S(1)} collective-permute-done((bf16[640,512]{1,0:T(8,128)(2,1)}, bf16[640,512]{1,0:T(8,128)(2,1)S(1)}, u32[]{:S(2)}, u32[]{:S(2)}) %collective-permute-start.6) | collective-permute-done | bytes 655392 | tf_op jit(solution)/shard_map/ppermute | solution.py:36
  182.3 1.9 copy-done.10
  184.2 1.3 copy-done.15
  185.5 6.5 %shard_map.149 = (bf16[128,1536]{1,0:T(8,128)(2,1)S(1)}, bf16[384,1536]{1,0:T(8,128)(2,1)S(1)}) custom-call(s32[6]{0:T(128)S(1)} %stack.27.meta, bf16[640,512]{1,0:T(8,128)(2,1)S(1)} %get-tuple-element.65.keep, bf16[640,512]{1,0:T(8,128)(2,1)S(1)} %collective-permute-done.6.got, bf16[1024,1536]{1,0:T(8,128)(2,1)} %all-gather.3.cloned.1.call-done.wo_all, ...), custom_call_target="tpu_custom_call" | custom-call | tf_op jit(solution)/shard_map/pallas_call | solution.py:502
  192.0 1.0 copy-done.13
  193.1 0.7 copy-done.27
  193.8 3.7 %all-to-all-start.3 = ((bf16[8,48,1536]{2,1,0:T(8,128)(2,1)}), bf16[8,48,1536]{2,1,0:T(8,128)(2,1)S(1)}, u32[]{:S(2)}, u32[]{:S(2)}) async-start(bf16[8,48,1536]{2,1,0:T(8,128)(2,1)} %bitcast.15), calls=%async_computation.3 | async-start | bytes 2359296 | tf_op jit(solution)/shard_map/all_to_all | solution.py:519
  197.6 1.4 shard_map.151
  199.0 15.9 %all-to-all-done.3 = bf16[8,48,1536]{2,1,0:T(8,128)(2,1)S(1)} async-done(((bf16[8,48,1536]{2,1,0:T(8,128)(2,1)}), bf16[8,48,1536]{2,1,0:T(8,128)(2,1)S(1)}, u32[]{:S(2)}, u32[]{:S(2)}) %all-to-all-start.3) | async-done | bytes 1179680 | tf_op jit(solution)/shard_map/all_to_all | solution.py:519
  214.8 1.4 shard_map.150
  (79 shorter events, 0.3 us)
Async XLA Ops:
  7.3 1.0 copy-start.11
  8.3 0.7 copy-start.35
  8.9 0.7 copy-start.38
  11.5 4.5 %copy-start.3 = (bf16[1536,256]{1,0:T(8,128)(2,1)S(1)}, bf16[1536,256]{1,0:T(8,128)(2,1)}, u32[]{:S(2)}) copy-start(bf16[1536,256]{1,0:T(8,128)(2,1)} %gate.2) | copy-start | bytes 2359300
  11.5 4.5 %copy-start.19 = (bf16[1536,64]{0,1:T(8,128)(2,1)S(1)}, bf16[1536,64]{0,1:T(8,128)(2,1)}, u32[]{:S(2)}) copy-start(bf16[1536,64]{0,1:T(8,128)(2,1)} %param.16) | copy-start | bytes 589828
  11.5 4.5 %copy-start.20 = (bf16[1536,64]{0,1:T(8,128)(2,1)S(1)}, bf16[1536,64]{0,1:T(8,128)(2,1)}, u32[]{:S(2)}) copy-start(bf16[1536,64]{0,1:T(8,128)(2,1)} %param.17) | copy-start | bytes 589828
  11.5 4.5 %copy-start.21 = (bf16[64,1536]{1,0:T(8,128)(2,1)S(1)}, bf16[64,1536]{1,0:T(8,128)(2,1)}, u32[]{:S(2)}) copy-start(bf16[64,1536]{1,0:T(8,128)(2,1)} %wo.3) | copy-start | bytes 589828
  11.5 34.6 %all-to-all-start = ((bf16[4,144,1536]{2,1,0:T(8,128)(2,1)}), bf16[4,144,1536]{2,1,0:T(8,128)(2,1)S(1)}, u32[]{:S(2)}, u32[]{:S(2)}) async-start(bf16[4,144,1536]{2,1,0:T(8,128)(2,1)} %shard_map.140), calls=%async_computation | async-start | bytes 3538944 | tf_op jit(solution)/shard_map/all_to_all | solution.py:432
  16.0 1.1 copy-start.4
  17.1 1.1 copy-start.6
  19.2 27.0 %collective-permute-start = (bf16[96,1536]{1,0:T(8,128)(2,1)S(1)}, bf16[96,1536]{1,0:T(8,128)(2,1)S(1)}, u32[]{:S(2)}, u32[]{:S(2)}) collective-permute-start(bf16[96,1536]{1,0:T(8,128)(2,1)S(1)} %shard_map.141), channel_id=1, source_target_pairs={{0,8},{1,9},{2,10},{3,11},{4,12},{5,13},{6,14},{7,15},{8,0},{9,1},... | collective-permute-start | bytes 884744 | tf_op jit(solution)/shard_map/ppermute | solution.py:36
  46.2 25.9 %copy-start = (bf16[4,144,1536]{2,1,0:T(8,128)(2,1)}, bf16[4,144,1536]{2,1,0:T(8,128)(2,1)S(1)}, u32[]{:S(2)}) copy-start(bf16[4,144,1536]{2,1,0:T(8,128)(2,1)S(1)} %all-to-all-done.near) | copy-start | bytes 5308420
  46.2 21.1 %collective-permute-start.1 = (bf16[4,144,1536]{2,1,0:T(8,128)(2,1)S(1)}, bf16[4,144,1536]{2,1,0:T(8,128)(2,1)}, u32[]{:S(2)}, u32[]{:S(2)}) collective-permute-start(bf16[4,144,1536]{2,1,0:T(8,128)(2,1)S(1)} %all-to-all-done.near), channel_id=1, source_target_pairs={{0,1},{1,0},{2,3},{3,2},{4,5},{5,4},{6,7},{7,6},{8,9},{9,8},{10,11... | collective-permute-start | bytes 5308424 | tf_op jit(solution)/shard_map/ppermute | solution.py:36
  49.7 17.6 %all-to-all-start.1 = ((bf16[4,48,1536]{2,1,0:T(8,128)(2,1)}), bf16[4,48,1536]{2,1,0:T(8,128)(2,1)S(1)}, u32[]{:S(2)}, u32[]{:S(2)}) async-start(bf16[4,48,1536]{2,1,0:T(8,128)(2,1)} %broadcast_in_dim.16), calls=%async_computation.1 | async-start | bytes 1179648 | tf_op jit(solution)/shard_map/all_to_all | solution.py:74
  54.3 74.2 %all-gather.3.cloned.1.call-start = ((), (), s32[]{:S(2)}) async-start(), calls=%async_computation.4 | async-start | bytes 3538944 | tf_op jit(solution)/shard_map/all_gather | solution.py:444
  54.4 12.9 %collective-permute-start.2 = (bf16[48,1536]{1,0:T(8,128)(2,1)}, bf16[48,1536]{1,0:T(8,128)(2,1)}, u32[]{:S(2)}, u32[]{:S(2)}) collective-permute-start(bf16[48,1536]{1,0:T(8,128)(2,1)} %get-tuple-element.46), channel_id=1, source_target_pairs={{0,32},{1,33},{2,34},{3,35},{4,36},{5,37},{6,38},{7,39},{8,40},{9,... | collective-permute-start | bytes 442376 | tf_op jit(solution)/shard_map/ppermute | solution.py:36
  67.3 0.9 copy-start.22
  72.1 0.7 copy-start.16
  72.8 0.7 copy-start.29
  73.6 0.7 copy-start.30
  74.3 0.8 copy-start.41
  75.1 100.6 %all-gather.5.cloned.1.call-start = ((), (), s32[]{:S(2)}) async-start(), calls=%async_computation.5 | async-start | bytes 2949120 | tf_op jit(solution)/shard_map/all_gather | solution.py:474
  75.2 53.4 %collective-permute-start.3 = (bf16[1024,128]{1,0:T(8,128)(2,1)}, bf16[1024,128]{1,0:T(8,128)(2,1)S(1)}, u32[]{:S(2)}, u32[]{:S(2)}) collective-permute-start(bf16[1024,128]{1,0:T(8,128)(2,1)} %copy-done.16), channel_id=1, source_target_pairs={{0,8},{1,9},{2,10},{3,11},{4,12},{5,13},{6,14},{7,15},{8,0},{9,1},... | collective-permute-start | bytes 786440 | tf_op jit(solution)/shard_map/ppermute | solution.py:36
  100.2 4.6 %copy-start.1 = (bf16[4,144,1536]{2,1,0:T(8,128)(2,1)S(1)}, bf16[4,144,1536]{2,1,0:T(8,128)(2,1)}, u32[]{:S(2)}) copy-start(bf16[4,144,1536]{2,1,0:T(8,128)(2,1)} %copy-done) | copy-start | bytes 5308420
  100.2 27.3 %collective-permute-start.4 = (bf16[96,1536]{1,0:T(8,128)(2,1)S(1)}, bf16[96,1536]{1,0:T(8,128)(2,1)S(1)}, u32[]{:S(2)}, u32[]{:S(2)}) collective-permute-start(bf16[96,1536]{1,0:T(8,128)(2,1)S(1)} %pad_maximum_fusion.1), channel_id=1, source_target_pairs={{0,16},{1,17},{2,18},{3,19},{4,20},{5,21},{6,22},{7,23},{8,24},{9,... | collective-permute-start | bytes 884744 | tf_op jit(solution)/shard_map/ppermute | solution.py:36
  102.4 1.1 copy-start.5
  103.5 1.2 copy-start.7
  104.8 4.0 %copy-start.17 = (bf16[1024,128]{1,0:T(8,128)(2,1)S(1)}, bf16[1024,128]{1,0:T(8,128)(2,1)}, u32[]{:S(2)}) copy-start(bf16[1024,128]{1,0:T(8,128)(2,1)} %copy-done.16) | copy-start | bytes 786436
  104.8 4.0 %copy-start.31 = (bf16[1024,128]{1,0:T(8,128)(2,1)S(1)}, bf16[1024,128]{1,0:T(8,128)(2,1)}, u32[]{:S(2)}) copy-start(bf16[1024,128]{1,0:T(8,128)(2,1)} %copy-done.30) | copy-start | bytes 786436
  104.8 4.0 %copy-start.36 = (s32[128,2]{0,1:T(2,128)S(1)}, s32[128,2]{0,1:T(2,128)}, u32[]{:S(2)}) copy-start(s32[128,2]{0,1:T(2,128)} %param.20) | copy-start | bytes 3076
  104.9 4.0 %copy-start.42 = (f32[1024,128]{1,0:T(8,128)S(1)}, f32[1024,128]{1,0:T(8,128)}, u32[]{:S(2)}) copy-start(f32[1024,128]{1,0:T(8,128)} %copy-done.41) | copy-start | bytes 1572868
  108.2 0.6 copy-start.33
  108.8 3.8 %copy-start.14 = (bf16[384,1536]{1,0:T(8,128)(2,1)}, bf16[384,1536]{1,0:T(8,128)(2,1)S(1)}, u32[]{:S(2)}) copy-start(bf16[384,1536]{1,0:T(8,128)(2,1)S(1)} %get-tuple-element.58.rows) | copy-start | bytes 3538948
  112.6 0.8 copy-start.23
  113.4 0.8 copy-start.25
  114.2 14.4 %copy-start.18 = (bf16[1024,128]{1,0:T(8,128)(2,1)S(1)}, bf16[1024,128]{1,0:T(8,128)(2,1)}, u32[]{:S(2)}) copy-start(bf16[1024,128]{1,0:T(8,128)(2,1)} %copy-done.16) | copy-start | bytes 786436
  114.2 16.6 %copy-start.39 = (s32[1,128]{1,0:T(1,128)S(1)}, s32[1,128]{1,0:T(1,128)}, u32[]{:S(2)}) copy-start(s32[1,128]{1,0:T(1,128)} %table.1) | copy-start | bytes 1540
  128.7 12.2 %collective-permute-start.5 = (bf16[1024,128]{1,0:T(8,128)(2,1)S(1)}, bf16[1024,128]{1,0:T(8,128)(2,1)S(1)}, u32[]{:S(2)}, u32[]{:S(2)}) collective-permute-start(bf16[1024,128]{1,0:T(8,128)(2,1)S(1)} %broadcast_select_fusion.3), channel_id=1, source_target_pairs={{0,16},{1,17},{2,18},{3,19},{4,20},{5,21},{6,22},{7,23},{16,32},{1... | collective-permute-start | bytes 786440 | tf_op jit(solution)/shard_map/ppermute | solution.py:36
  140.9 1.0 copy-start.24
  142.0 1.1 copy-start.26
  143.1 1.0 copy-start.32
  149.1 1.1 copy-start.2
  150.2 28.9 %copy-start.43 = (f32[1536]{0:T(1024)S(1)}, f32[1536]{0:T(1024)}, u32[]{:S(2)}) copy-start(f32[1536]{0:T(1024)} %param.15) | copy-start | bytes 18436
  150.2 32.2 %copy-start.12 = (bf16[128,1536]{1,0:T(8,128)(2,1)S(1)}, bf16[128,1536]{1,0:T(8,128)(2,1)}, u32[]{:S(2)}) copy-start(bf16[128,1536]{1,0:T(8,128)(2,1)} %tokens.3) | copy-start | bytes 1179652
  150.2 22.0 %all-to-all-start.2 = ((bf16[4,1280,128]{2,1,0:T(8,128)(2,1)}), bf16[4,1280,128]{2,1,0:T(8,128)(2,1)}, u32[]{:S(2)}, u32[]{:S(2)}) async-start(bf16[4,1280,128]{2,1,0:T(8,128)(2,1)} %copy-done.2), calls=%async_computation.2 | async-start | bytes 2621440 | tf_op jit(solution)/shard_map/all_to_all | solution.py:491
  154.8 27.5 %collective-permute-start.7 = (bf16[768,1536]{1,0:T(8,128)(2,1)S(1)}, bf16[768,1536]{1,0:T(8,128)(2,1)}, u32[]{:S(2)}, u32[]{:S(2)}) collective-permute-start(bf16[768,1536]{1,0:T(8,128)(2,1)S(1)} %shard_map.145.own), channel_id=1, source_target_pairs={{1,0},{3,2},{5,4},{7,6},{8,9},{10,11},{12,13},{14,15},{17,16},{19,... | collective-permute-start | bytes 7077896 | tf_op jit(solution)/shard_map/ppermute | solution.py:36
  172.2 0.9 copy-start.34
  174.9 0.9 copy-start.40
  175.7 6.6 %collective-permute-start.8 = (bf16[768,1536]{1,0:T(8,128)(2,1)}, bf16[768,1536]{1,0:T(8,128)(2,1)S(1)}, u32[]{:S(2)}, u32[]{:S(2)}) collective-permute-start(bf16[768,1536]{1,0:T(8,128)(2,1)} %all-gather.5.cloned.1.call-done.other), channel_id=1, source_target_pairs={{0,1},{2,3},{4,5},{6,7},{9,8},{11,10},{13,12},{15,14},{16,17},{18,... | collective-permute-start | bytes 7077896 | tf_op jit(solution)/shard_map/ppermute | solution.py:36
  177.2 5.1 %collective-permute-start.6 = (bf16[640,512]{1,0:T(8,128)(2,1)}, bf16[640,512]{1,0:T(8,128)(2,1)S(1)}, u32[]{:S(2)}, u32[]{:S(2)}) collective-permute-start(bf16[640,512]{1,0:T(8,128)(2,1)} %copy-done.40), channel_id=1, source_target_pairs={{0,1},{1,0},{2,3},{3,2},{4,5},{5,4},{6,7},{7,6},{8,9},{9,8},{10,11... | collective-permute-start | bytes 1966088 | tf_op jit(solution)/shard_map/ppermute | solution.py:36
  182.3 9.7 %copy-start.8 = (bf16[640,512]{1,0:T(8,128)(2,1)}, bf16[640,512]{1,0:T(8,128)(2,1)S(1)}, u32[]{:S(2)}) copy-start(bf16[640,512]{1,0:T(8,128)(2,1)S(1)} %collective-permute-done.6.got) | copy-start | bytes 1966084
  182.3 1.9 copy-start.10
  184.2 1.3 copy-start.15
  192.0 1.1 copy-start.13
  193.1 0.7 copy-start.27
  193.8 3.7 %copy-start.9 = (bf16[640,512]{1,0:T(8,128)(2,1)S(1)}, bf16[640,512]{1,0:T(8,128)(2,1)}, u32[]{:S(2)}) copy-start(bf16[640,512]{1,0:T(8,128)(2,1)} %copy-done.8) | copy-start | bytes 1966084
  193.8 21.0 %copy-start.28 = (bf16[128,1536]{1,0:T(8,128)(2,1)S(1)}, bf16[128,1536]{1,0:T(8,128)(2,1)}, u32[]{:S(2)}) copy-start(bf16[128,1536]{1,0:T(8,128)(2,1)} %copy-done.27) | copy-start | bytes 1179652
  193.8 21.0 %copy-start.37 = (f32[128,2]{0,1:T(2,128)S(1)}, f32[128,2]{0,1:T(2,128)}, u32[]{:S(2)}) copy-start(f32[128,2]{0,1:T(2,128)} %param.21) | copy-start | bytes 3076
  193.8 21.0 %all-to-all-start.3 = ((bf16[8,48,1536]{2,1,0:T(8,128)(2,1)}), bf16[8,48,1536]{2,1,0:T(8,128)(2,1)S(1)}, u32[]{:S(2)}, u32[]{:S(2)}) async-start(bf16[8,48,1536]{2,1,0:T(8,128)(2,1)} %bitcast.15), calls=%async_computation.3 | async-start | bytes 2359296 | tf_op jit(solution)/shard_map/all_to_all | solution.py:519
Sparse Core Ops, SparseCore 0:
  75.3 48.1 all-gather.2
  128.7 35.7 all-gather.4

commit v8 on v7

--- a/solution.py
+++ b/solution.py
@@ -428,6 +428,7 @@
         [((96, WIDTH), BF16)],
         [SMEM] + [HBM] * 6,
         scratch=[pltpu.SemaphoreType.DMA((10,))],
+        limit=60,
     )(meta, wq, wkv, w_out, w_gate, w_up, w_down)
     near = lax.all_to_all(block, "x", split_axis=0, concat_axis=0, tiled=True)
     near, piece = lax.optimization_barrier((near, swap_half(piece)))
@@ -487,6 +488,7 @@
         scratch=[pltpu.VMEM((ROWS, 128), BF16)] * 2,
         flops=0,
         nbytes=0,
+        limit=60,
     )(q, previous, sums, stats, pages)
     heads = lax.all_to_all(heads, "x", split_axis=0, concat_axis=0, tiled=True)
     keep, give = call(
@@ -495,6 +497,7 @@
         [SMEM] + [VMEM] * 3,
         flops=0,
         nbytes=0,
+        limit=60,
     )(meta, heads, pick, other_pick)
     got = swap_core(give)
     other = after(other, give)
@@ -509,7 +512,7 @@
             pltpu.VMEM((2, 768, 512), BF16),
             pltpu.SemaphoreType.DMA((2,)),
         ],
-        limit=40,
+        limit=60,
         flops=0,
         nbytes=0,
     )(meta, keep, got, out_all, chosen, tokens, ffn_gain[None, :], own, other, given_a, given_b)

time: 225 us -> 218 us (0.969)
  local copies, waits for them, and re-layouts: 26.3 us -> 11 us
  Pallas kernels: 32.5 us -> 40.9 us
    unnamed x88 -> x74, local copies, waits for them, and re-layouts: 24 us -> 9.45 us
    pallas_call x1, Pallas kernels: 5.06 us -> 7.75 us  [body(): call(before_kernel, [((4, ROWS + 256, 128), BF16)], [VMEM] * 5, scratch=[...]
  transfers between devices with their start and end apart: 15 -> 15, of which waited for: 7 -> 7; matrix products, arithmetic and copies ran while one was open for 2% -> 2% of each run, Pallas kernels for 8% -> 11%
where the time goes in v8:
time: 218 us; the launch traced here: 217 us
  starting transfers between devices  78 us (36%)
  waiting for transfers between devices  69.9 us (32%)
  Pallas kernels  40.9 us (19%)
  between operations  14.6 us (7%)
  local copies, waits for them, and re-layouts  11 us (5%)
  other arithmetic  2.75 us (1%)
    ppermute x9, starting transfers between devices, permute(): return lax.ppermute(block, AXES, route)  60.7 us
    ppermute x9, waiting for transfers between devices, permute(): return lax.ppermute(block, AXES, route)  38 us
    all_to_all x1, waiting for transfers between devices, body(): heads = lax.all_to_all(heads, 'x', split_axis=0, concat_axis=0, tiled=True)  16 us
    all_to_all x1, waiting for transfers between devices, body(): lax.all_to_all(expert_out.reshape(8, CAP, WIDTH), ROW, split_axis=0, conc...  15.9 us
    unnamed x74, local copies, waits for them, and re-layouts  9.45 us
    pallas_call x1, Pallas kernels, body(): call(expert_kernel, [((TOK, WIDTH), BF16), ((8 * CAP, WIDTH), BF16)], [SM...  8.16 us
    pallas_call x1, Pallas kernels, body(): call(before_kernel, [((4, ROWS + 256, 128), BF16)], [VMEM] * 5, scratch=[...  7.75 us
    all_to_all x1, starting transfers between devices, gather(): return lax.all_to_all(wide, axis, split_axis=0, concat_axis=0, tiled=True)  4.68 us
  transfers between devices with their start and end apart: 15, of which 7 were waited for; matrix products, arithmetic and copies ran while one was open for 2% of the time, Pallas kernels for 11%

profile of v8, /device:TPU:24, one launch (start us, length us, event | category | flops | bytes accessed | tf_op | source)
XLA Modules:
  0.0 217.2 jit_solution(15880143228005076552)
XLA Ops:
  7.2 0.1 stack.27.meta
  7.3 1.0 copy-done.9
  8.3 0.7 copy-done.27
  9.0 0.7 copy-done.30
  9.6 1.9 shard_map.140
  11.5 4.3 %all-to-all-start = ((bf16[4,144,1536]{2,1,0:T(8,128)(2,1)}), bf16[4,144,1536]{2,1,0:T(8,128)(2,1)S(1)}, u32[]{:S(2)}, u32[]{:S(2)}) async-start(bf16[4,144,1536]{2,1,0:T(8,128)(2,1)} %shard_map.140), calls=%async_computation | async-start | bytes 3538944 | tf_op jit(solution)/shard_map/all_to_all | solution.py:433
  15.8 2.3 %shard_map.141 = bf16[96,1536]{1,0:T(8,128)(2,1)} custom-call(s32[6]{0:T(128)} %copy-done.24, bf16[64,1536]{1,0:T(8,128)(2,1)} %bitcast.15, bf16[64,1536]{1,0:T(8,128)(2,1)} %bitcast.17, bf16[64,1536]{1,0:T(8,128)(2,1)} %wo.3, bf16[1536,256]{1,0:T(8,128)(2,1)} %gate.2, bf16[1536,256]{1,0:T(8,128)(2,1)} %up.2, bf16[256,1536]{1,0:T(8,128)(2,1)} %down.2), custom_call_target="tpu_custom_call" | custom-call | tf_op jit(solution)/shard_map/pallas_call | solution.py:426
  18.1 0.0 copy-start.35
  18.2 0.0 copy-start.14
  18.2 0.0 copy-start.15
  18.2 0.0 copy-start.16
  18.2 15.9 %collective-permute-start = (bf16[96,1536]{1,0:T(8,128)(2,1)}, bf16[96,1536]{1,0:T(8,128)(2,1)S(1)}, u32[]{:S(2)}, u32[]{:S(2)}) collective-permute-start(bf16[96,1536]{1,0:T(8,128)(2,1)} %shard_map.141), channel_id=1, source_target_pairs={{0,8},{1,9},{2,10},{3,11},{4,12},{5,13},{6,14},{7,15},{8,0},{9,1},... | collective-permute-start | bytes 884744 | tf_op jit(solution)/shard_map/ppermute | solution.py:36
  34.1 11.5 %collective-permute-done = bf16[96,1536]{1,0:T(8,128)(2,1)S(1)} collective-permute-done((bf16[96,1536]{1,0:T(8,128)(2,1)}, bf16[96,1536]{1,0:T(8,128)(2,1)S(1)}, u32[]{:S(2)}, u32[]{:S(2)}) %collective-permute-start) | collective-permute-done | bytes 294944 | tf_op jit(solution)/shard_map/ppermute | solution.py:36
  45.5 0.0 all-to-all-done.near
  45.5 1.9 collective-permute-start.1
  47.5 0.9 broadcast_in_dim.16
  48.4 4.7 %all-to-all-start.1 = ((bf16[4,48,1536]{2,1,0:T(8,128)(2,1)}), bf16[4,48,1536]{2,1,0:T(8,128)(2,1)S(1)}, u32[]{:S(2)}, u32[]{:S(2)}) async-start(bf16[4,48,1536]{2,1,0:T(8,128)(2,1)} %broadcast_in_dim.16), calls=%async_computation.1 | async-start | bytes 1179648 | tf_op jit(solution)/shard_map/all_to_all | solution.py:74
  53.1 8.6 %collective-permute-start.2 = (bf16[48,1536]{1,0:T(8,128)(2,1)S(1)}, bf16[48,1536]{1,0:T(8,128)(2,1)}, u32[]{:S(2)}, u32[]{:S(2)}) collective-permute-start(bf16[48,1536]{1,0:T(8,128)(2,1)S(1)} %get-tuple-element.46), channel_id=1, source_target_pairs={{0,32},{1,33},{2,34},{3,35},{4,36},{5,37},{6,38},{7,39},{8,40},{9,... | collective-permute-start | bytes 442376 | tf_op jit(solution)/shard_map/ppermute | solution.py:36
  61.7 4.0 %collective-permute-done.2 = bf16[48,1536]{1,0:T(8,128)(2,1)} collective-permute-done((bf16[48,1536]{1,0:T(8,128)(2,1)S(1)}, bf16[48,1536]{1,0:T(8,128)(2,1)}, u32[]{:S(2)}, u32[]{:S(2)}) %collective-permute-start.2) | collective-permute-done | bytes 147488 | tf_op jit(solution)/shard_map/ppermute | solution.py:36
  65.8 4.6 %shard_map.142 = (bf16[1024,128]{1,0:T(8,128)(2,1)S(1)}, bf16[1024,128]{1,0:T(8,128)(2,1)S(1)}, f32[1024,128]{1,0:T(8,128)S(1)}, bf16[128,1536]{1,0:T(8,128)(2,1)}) custom-call(s32[6]{0:T(128)S(1)} %copy-done.25, bf16[4,144,1536]{2,1,0:T(8,128)(2,1)S(1)} %all-to-all-done.near, bf16[4,144,1536]{2,1,0:T(8,128)(2,1)} %collective-permute-done.1.across, ...), custom_call_target="tpu_custom_call" | custom-call | tf_op jit(solution)/shard_map/pallas_call | solution.py:439
  70.4 0.7 copy-done.12
  71.1 0.7 copy-done.20
  71.9 0.8 copy-done.32
  72.7 0.0 all-gather.3.cloned.1.call-update
  72.7 0.0 all-gather.5.cloned.1.call-start
  72.8 24.1 %collective-permute-start.3 = (bf16[1024,128]{1,0:T(8,128)(2,1)}, bf16[1024,128]{1,0:T(8,128)(2,1)S(1)}, u32[]{:S(2)}, u32[]{:S(2)}) collective-permute-start(bf16[1024,128]{1,0:T(8,128)(2,1)} %copy-done.12), channel_id=1, source_target_pairs={{0,8},{1,9},{2,10},{3,11},{4,12},{5,13},{6,14},{7,15},{8,0},{9,1},... | collective-permute-start | bytes 786440 | tf_op jit(solution)/shard_map/ppermute | solution.py:36
  96.9 1.0 broadcast_select_fusion.5
  97.9 2.1 collective-permute-start.4
  100.0 0.0 copy-start.4
  100.0 1.1 copy-done.4
  101.2 1.2 copy-done.5
  102.3 0.2 shard_map.145.own
  102.5 0.0 copy-start.21
  102.5 0.0 copy-start.28
  102.5 4.1 %shard_map.144 = (bf16[384,128]{1,0:T(8,128)(2,1)S(1)}, bf16[384,128]{1,0:T(8,128)(2,1)S(1)}, bf16[384,1536]{1,0:T(8,128)(2,1)S(1)}) custom-call(s32[6]{0:T(128)S(1)} %copy-done.25, bf16[4,144,1536]{2,1,0:T(8,128)(2,1)S(1)} %copy-done.2, bf16[4,144,1536]{2,1,0:T(8,128)(2,1)} %collective-permute-done.1.across), custom_call_target="tpu_custom_call" | custom-call | flops 2000000000 | bytes 5000000 | tf_op jit(solution)/shard_map/pallas_call | solution.py:456
  106.6 0.0 copy-start.10
  106.7 3.8 %shard_map.143 = (f32[1024,128]{1,0:T(8,128)S(1)}, f32[1024,128]{1,0:T(8,128)S(1)}, s32[8,128]{1,0:T(8,128)S(1)}) custom-call(bf16[1024,128]{1,0:T(8,128)(2,1)S(1)} %copy-done.21, bf16[1024,128]{1,0:T(8,128)(2,1)S(1)} %copy-done.13, f32[1024,128]{1,0:T(8,128)S(1)} %copy-done.33, s32[2,128]{1,0:T(2,128)S(1)} %bitcast.20), custom_call_target="tpu_custom_call" | custom-call | flops 4000000000 | bytes 3000000 | tf_op jit(solution)/shard_map/pallas_call | solution.py:448
  110.5 0.8 copy-done.17
  111.3 0.8 copy-done.18
  112.1 13.2 %collective-permute-done.4 = bf16[96,1536]{1,0:T(8,128)(2,1)S(1)} collective-permute-done((bf16[96,1536]{1,0:T(8,128)(2,1)S(1)}, bf16[96,1536]{1,0:T(8,128)(2,1)S(1)}, u32[]{:S(2)}, u32[]{:S(2)}) %collective-permute-start.4) | collective-permute-done | bytes 294944 | tf_op jit(solution)/shard_map/ppermute | solution.py:36
  125.3 0.1 broadcast_select_fusion.1
  125.4 0.9 pad_maximum_fusion
  126.2 0.0 all-gather.5.cloned.1.call-update
  126.3 2.1 collective-permute-start.5
  128.4 2.4 %shard_map.146.pages = bf16[1024,128]{1,0:T(8,128)(2,1)S(1)} custom-call(s32[6]{0:T(128)S(1)} %copy-done.25, s32[1,128]{1,0:T(1,128)S(1)} %copy-done.31, bf16[1024,128]{1,0:T(8,128)(2,1)S(1)} %copy-done.13, bf16[1024,128]{1,0:T(8,128)(2,1)S(1)} %collective-permute-done.3.partner), custom_call_target="tpu_custom_call" | custom-call | tf_op jit(solution)/shard_map/pallas_call | solution.py:476
  130.9 7.7 %collective-permute-done.5 = bf16[1024,128]{1,0:T(8,128)(2,1)S(1)} collective-permute-done((bf16[1024,128]{1,0:T(8,128)(2,1)S(1)}, bf16[1024,128]{1,0:T(8,128)(2,1)S(1)}, u32[]{:S(2)}, u32[]{:S(2)}) %collective-permute-start.5) | collective-permute-done | bytes 262176 | tf_op jit(solution)/shard_map/ppermute | solution.py:36
  138.5 0.7 broadcast_select_fusion.2.kv
  139.3 7.8 %shard_map.147 = bf16[4,1280,128]{2,1,0:T(8,128)(2,1)} custom-call(bf16[1024,128]{1,0:T(8,128)(2,1)} %copy-done.20, bf16[1024,128]{1,0:T(8,128)(2,1)} %broadcast_select_fusion.2.kv, f32[1024,128]{1,0:T(8,128)} %copy-done.17, f32[1024,128]{1,0:T(8,128)} %copy-done.18, bf16[1024,128]{1,0:T(8,128)(2,1)} %copy-done.11), custom_call_target="tpu_custom_call" | custom-call | tf_op jit(solution)/shard_map/pallas_call | solution.py:484
  147.0 4.6 %all-to-all-start.2 = ((bf16[4,1280,128]{2,1,0:T(8,128)(2,1)}), bf16[4,1280,128]{2,1,0:T(8,128)(2,1)}, u32[]{:S(2)}, u32[]{:S(2)}) async-start(bf16[4,1280,128]{2,1,0:T(8,128)(2,1)} %shard_map.147), calls=%async_computation.2 | async-start | bytes 2621440 | tf_op jit(solution)/shard_map/all_to_all | solution.py:493
  151.7 1.3 collective-permute-start.7
  153.0 16.0 %all-to-all-done.2.heads = bf16[4,1280,128]{2,1,0:T(8,128)(2,1)} async-done(((bf16[4,1280,128]{2,1,0:T(8,128)(2,1)}), bf16[4,1280,128]{2,1,0:T(8,128)(2,1)}, u32[]{:S(2)}, u32[]{:S(2)}) %all-to-all-start.2) | async-done | bytes 1310752 | tf_op jit(solution)/shard_map/all_to_all | solution.py:493
  169.0 2.9 %shard_map.148 = (bf16[640,512]{1,0:T(8,128)(2,1)}, bf16[640,512]{1,0:T(8,128)(2,1)}) custom-call(s32[6]{0:T(128)} %copy-done.24, bf16[4,1280,128]{2,1,0:T(8,128)(2,1)} %all-to-all-done.2.heads, bf16[384,128]{1,0:T(8,128)(2,1)} %copy-done.22, bf16[384,128]{1,0:T(8,128)(2,1)} %copy-done.23), custom_call_target="tpu_custom_call" | custom-call | tf_op jit(solution)/shard_map/pallas_call | solution.py:494
  171.9 2.8 %collective-permute-start.8 = (bf16[768,1536]{1,0:T(8,128)(2,1)}, bf16[768,1536]{1,0:T(8,128)(2,1)}, u32[]{:S(2)}, u32[]{:S(2)}) collective-permute-start(bf16[768,1536]{1,0:T(8,128)(2,1)} %all-gather.5.cloned.1.call-done.other), channel_id=1, source_target_pairs={{0,1},{2,3},{4,5},{6,7},{9,8},{11,10},{13,12},{15,14},{16,17},{18,... | collective-permute-start | bytes 7077896 | tf_op jit(solution)/shard_map/ppermute | solution.py:36
  174.7 1.9 collective-permute-start.6
  176.6 0.6 broadcast_in_dim.18.gain
  177.2 1.7 collective-permute-done.6.got
  178.9 0.8 copy-done.7
  179.7 8.2 %shard_map.149 = (bf16[128,1536]{1,0:T(8,128)(2,1)}, bf16[384,1536]{1,0:T(8,128)(2,1)}) custom-call(s32[6]{0:T(128)} %copy-done.24, bf16[640,512]{1,0:T(8,128)(2,1)} %get-tuple-element.65.keep, bf16[640,512]{1,0:T(8,128)(2,1)} %copy-done.7, bf16[1024,1536]{1,0:T(8,128)(2,1)} %all-gather.3.cloned.1.call-done.wo_all, bf16[384,1536]{1,0:T(8,128)(2,1)} %copy-done.10, ...), custom_call_target="tpu_custom_call" | custom-call | tf_op jit(solution)/shard_map/pallas_call | solution.py:505
  187.9 0.0 copy-start.19
  187.9 0.0 copy-start.29
  187.9 3.7 %all-to-all-start.3 = ((bf16[8,48,1536]{2,1,0:T(8,128)(2,1)}), bf16[8,48,1536]{2,1,0:T(8,128)(2,1)S(1)}, u32[]{:S(2)}, u32[]{:S(2)}) async-start(bf16[8,48,1536]{2,1,0:T(8,128)(2,1)} %bitcast.23), calls=%async_computation.3 | async-start | bytes 2359296 | tf_op jit(solution)/shard_map/all_to_all | solution.py:522
  191.7 1.4 shard_map.151
  193.1 15.9 %all-to-all-done.3 = bf16[8,48,1536]{2,1,0:T(8,128)(2,1)S(1)} async-done(((bf16[8,48,1536]{2,1,0:T(8,128)(2,1)}), bf16[8,48,1536]{2,1,0:T(8,128)(2,1)S(1)}, u32[]{:S(2)}, u32[]{:S(2)}) %all-to-all-start.3) | async-done | bytes 1179680 | tf_op jit(solution)/shard_map/all_to_all | solution.py:522
  209.0 1.4 shard_map.150
  (65 shorter events, 0.2 us)
Async XLA Ops:
  7.3 4.2 %copy-start.24 = (s32[6]{0:T(128)}, s32[6]{0:T(128)S(1)}, u32[]{:S(2)}) copy-start(s32[6]{0:T(128)S(1)} %stack.27.meta) | copy-start | bytes 76
  7.3 1.0 copy-start.9
  8.3 0.7 copy-start.27
  9.0 0.7 copy-start.30
  11.5 34.0 %all-to-all-start = ((bf16[4,144,1536]{2,1,0:T(8,128)(2,1)}), bf16[4,144,1536]{2,1,0:T(8,128)(2,1)S(1)}, u32[]{:S(2)}, u32[]{:S(2)}) async-start(bf16[4,144,1536]{2,1,0:T(8,128)(2,1)} %shard_map.140), calls=%async_computation | async-start | bytes 3538944 | tf_op jit(solution)/shard_map/all_to_all | solution.py:433
  18.1 43.6 %copy-start.35 = (f32[1536]{0:T(1024)S(1)}, f32[1536]{0:T(1024)}, u32[]{:S(2)}) copy-start(f32[1536]{0:T(1024)} %param.14) | copy-start | bytes 18436
  18.2 47.6 %copy-start.14 = (bf16[1536,64]{0,1:T(8,128)(2,1)S(1)}, bf16[1536,64]{0,1:T(8,128)(2,1)}, u32[]{:S(2)}) copy-start(bf16[1536,64]{0,1:T(8,128)(2,1)} %param.16) | copy-start | bytes 589828
  18.2 47.6 %copy-start.15 = (bf16[1536,64]{0,1:T(8,128)(2,1)S(1)}, bf16[1536,64]{0,1:T(8,128)(2,1)}, u32[]{:S(2)}) copy-start(bf16[1536,64]{0,1:T(8,128)(2,1)} %param.17) | copy-start | bytes 589828
  18.2 47.6 %copy-start.16 = (bf16[64,1536]{1,0:T(8,128)(2,1)S(1)}, bf16[64,1536]{1,0:T(8,128)(2,1)}, u32[]{:S(2)}) copy-start(bf16[64,1536]{1,0:T(8,128)(2,1)} %wo.3) | copy-start | bytes 589828
  18.2 47.6 %copy-start.25 = (s32[6]{0:T(128)S(1)}, s32[6]{0:T(128)}, u32[]{:S(2)}) copy-start(s32[6]{0:T(128)} %copy-done.24) | copy-start | bytes 76
  18.2 27.3 %collective-permute-start = (bf16[96,1536]{1,0:T(8,128)(2,1)}, bf16[96,1536]{1,0:T(8,128)(2,1)S(1)}, u32[]{:S(2)}, u32[]{:S(2)}) collective-permute-start(bf16[96,1536]{1,0:T(8,128)(2,1)} %shard_map.141), channel_id=1, source_target_pairs={{0,8},{1,9},{2,10},{3,11},{4,12},{5,13},{6,14},{7,15},{8,0},{9,1},... | collective-permute-start | bytes 884744 | tf_op jit(solution)/shard_map/ppermute | solution.py:36
  45.5 24.9 %copy-start.1 = (bf16[4,144,1536]{2,1,0:T(8,128)(2,1)}, bf16[4,144,1536]{2,1,0:T(8,128)(2,1)S(1)}, u32[]{:S(2)}) copy-start(bf16[4,144,1536]{2,1,0:T(8,128)(2,1)S(1)} %all-to-all-done.near) | copy-start | bytes 5308420
  45.5 20.2 %collective-permute-start.1 = (bf16[4,144,1536]{2,1,0:T(8,128)(2,1)S(1)}, bf16[4,144,1536]{2,1,0:T(8,128)(2,1)}, u32[]{:S(2)}, u32[]{:S(2)}) collective-permute-start(bf16[4,144,1536]{2,1,0:T(8,128)(2,1)S(1)} %all-to-all-done.near), channel_id=1, source_target_pairs={{0,1},{1,0},{2,3},{3,2},{4,5},{5,4},{6,7},{7,6},{8,9},{9,8},{10,11... | collective-permute-start | bytes 5308424 | tf_op jit(solution)/shard_map/ppermute | solution.py:36
  47.5 18.3 %copy-start.34 = (bf16[48,1536]{1,0:T(8,128)(2,1)}, bf16[48,1536]{1,0:T(8,128)(2,1)S(1)}, u32[]{:S(2)}) copy-start(bf16[48,1536]{1,0:T(8,128)(2,1)S(1)} %get-tuple-element.46) | copy-start | bytes 442372
  48.4 17.4 %all-to-all-start.1 = ((bf16[4,48,1536]{2,1,0:T(8,128)(2,1)}), bf16[4,48,1536]{2,1,0:T(8,128)(2,1)S(1)}, u32[]{:S(2)}, u32[]{:S(2)}) async-start(bf16[4,48,1536]{2,1,0:T(8,128)(2,1)} %broadcast_in_dim.16), calls=%async_computation.1 | async-start | bytes 1179648 | tf_op jit(solution)/shard_map/all_to_all | solution.py:74
  53.1 73.2 %all-gather.3.cloned.1.call-start = ((), (), s32[]{:S(2)}) async-start(), calls=%async_computation.4 | async-start | bytes 3538944 | tf_op jit(solution)/shard_map/all_gather | solution.py:445
  53.1 12.7 %collective-permute-start.2 = (bf16[48,1536]{1,0:T(8,128)(2,1)S(1)}, bf16[48,1536]{1,0:T(8,128)(2,1)}, u32[]{:S(2)}, u32[]{:S(2)}) collective-permute-start(bf16[48,1536]{1,0:T(8,128)(2,1)S(1)} %get-tuple-element.46), channel_id=1, source_target_pairs={{0,32},{1,33},{2,34},{3,35},{4,36},{5,37},{6,38},{7,39},{8,40},{9,... | collective-permute-start | bytes 442376 | tf_op jit(solution)/shard_map/ppermute | solution.py:36
  70.4 0.7 copy-start.12
  71.1 0.7 copy-start.20
  71.8 0.8 copy-start.32
  72.7 27.3 %copy-start.3 = (bf16[1536,256]{1,0:T(8,128)(2,1)S(1)}, bf16[1536,256]{1,0:T(8,128)(2,1)}, u32[]{:S(2)}) copy-start(bf16[1536,256]{1,0:T(8,128)(2,1)} %gate.2) | copy-start | bytes 2359300
  72.7 99.2 %all-gather.5.cloned.1.call-start = ((), (), s32[]{:S(2)}) async-start(), calls=%async_computation.5 | async-start | bytes 2949120 | tf_op jit(solution)/shard_map/all_gather | solution.py:475
  72.8 53.5 %collective-permute-start.3 = (bf16[1024,128]{1,0:T(8,128)(2,1)}, bf16[1024,128]{1,0:T(8,128)(2,1)S(1)}, u32[]{:S(2)}, u32[]{:S(2)}) collective-permute-start(bf16[1024,128]{1,0:T(8,128)(2,1)} %copy-done.12), channel_id=1, source_target_pairs={{0,8},{1,9},{2,10},{3,11},{4,12},{5,13},{6,14},{7,15},{8,0},{9,1},... | collective-permute-start | bytes 786440 | tf_op jit(solution)/shard_map/ppermute | solution.py:36
  97.9 4.5 %copy-start.2 = (bf16[4,144,1536]{2,1,0:T(8,128)(2,1)S(1)}, bf16[4,144,1536]{2,1,0:T(8,128)(2,1)}, u32[]{:S(2)}) copy-start(bf16[4,144,1536]{2,1,0:T(8,128)(2,1)} %copy-done.1) | copy-start | bytes 5308420
  97.9 27.3 %collective-permute-start.4 = (bf16[96,1536]{1,0:T(8,128)(2,1)S(1)}, bf16[96,1536]{1,0:T(8,128)(2,1)S(1)}, u32[]{:S(2)}, u32[]{:S(2)}) collective-permute-start(bf16[96,1536]{1,0:T(8,128)(2,1)S(1)} %pad_maximum_fusion.1), channel_id=1, source_target_pairs={{0,16},{1,17},{2,18},{3,19},{4,20},{5,21},{6,22},{7,23},{8,24},{9,... | collective-permute-start | bytes 884744 | tf_op jit(solution)/shard_map/ppermute | solution.py:36
  100.0 1.1 copy-start.4
  101.2 1.2 copy-start.5
  102.5 49.2 %copy-start = (bf16[768,1536]{1,0:T(8,128)(2,1)}, bf16[768,1536]{1,0:T(8,128)(2,1)S(1)}, u32[]{:S(2)}) copy-start(bf16[768,1536]{1,0:T(8,128)(2,1)S(1)} %shard_map.145.own) | copy-start | bytes 7077892
  102.5 4.2 %copy-start.13 = (bf16[1024,128]{1,0:T(8,128)(2,1)S(1)}, bf16[1024,128]{1,0:T(8,128)(2,1)}, u32[]{:S(2)}) copy-start(bf16[1024,128]{1,0:T(8,128)(2,1)} %copy-done.12) | copy-start | bytes 786436
  102.5 4.2 %copy-start.21 = (bf16[1024,128]{1,0:T(8,128)(2,1)S(1)}, bf16[1024,128]{1,0:T(8,128)(2,1)}, u32[]{:S(2)}) copy-start(bf16[1024,128]{1,0:T(8,128)(2,1)} %copy-done.20) | copy-start | bytes 786436
  102.5 4.2 %copy-start.28 = (s32[128,2]{0,1:T(2,128)S(1)}, s32[128,2]{0,1:T(2,128)}, u32[]{:S(2)}) copy-start(s32[128,2]{0,1:T(2,128)} %param.20) | copy-start | bytes 3076
  102.5 4.2 %copy-start.33 = (f32[1024,128]{1,0:T(8,128)S(1)}, f32[1024,128]{1,0:T(8,128)}, u32[]{:S(2)}) copy-start(f32[1024,128]{1,0:T(8,128)} %copy-done.32) | copy-start | bytes 1572868
  106.6 3.8 %copy-start.10 = (bf16[384,1536]{1,0:T(8,128)(2,1)}, bf16[384,1536]{1,0:T(8,128)(2,1)S(1)}, u32[]{:S(2)}) copy-start(bf16[384,1536]{1,0:T(8,128)(2,1)S(1)} %get-tuple-element.58.rows) | copy-start | bytes 3538948
  106.7 3.8 %copy-start.22 = (bf16[384,128]{1,0:T(8,128)(2,1)}, bf16[384,128]{1,0:T(8,128)(2,1)S(1)}, u32[]{:S(2)}) copy-start(bf16[384,128]{1,0:T(8,128)(2,1)S(1)} %get-tuple-element.53.pick) | copy-start | bytes 294916
  106.7 3.8 %copy-start.23 = (bf16[384,128]{1,0:T(8,128)(2,1)}, bf16[384,128]{1,0:T(8,128)(2,1)S(1)}, u32[]{:S(2)}) copy-start(bf16[384,128]{1,0:T(8,128)(2,1)S(1)} %get-tuple-element.54.other) | copy-start | bytes 294916
  110.5 0.8 copy-start.17
  111.3 0.8 copy-start.18
  112.1 16.3 %copy-start.31 = (s32[1,128]{1,0:T(1,128)S(1)}, s32[1,128]{1,0:T(1,128)}, u32[]{:S(2)}) copy-start(s32[1,128]{1,0:T(1,128)} %table.1) | copy-start | bytes 1540
  126.3 12.2 %collective-permute-start.5 = (bf16[1024,128]{1,0:T(8,128)(2,1)S(1)}, bf16[1024,128]{1,0:T(8,128)(2,1)S(1)}, u32[]{:S(2)}, u32[]{:S(2)}) collective-permute-start(bf16[1024,128]{1,0:T(8,128)(2,1)S(1)} %broadcast_select_fusion.3), channel_id=1, source_target_pairs={{0,16},{1,17},{2,18},{3,19},{4,20},{5,21},{6,22},{7,23},{16,32},{1... | collective-permute-start | bytes 786440 | tf_op jit(solution)/shard_map/ppermute | solution.py:36
  130.9 8.4 %copy-start.11 = (bf16[1024,128]{1,0:T(8,128)(2,1)}, bf16[1024,128]{1,0:T(8,128)(2,1)S(1)}, u32[]{:S(2)}) copy-start(bf16[1024,128]{1,0:T(8,128)(2,1)S(1)} %shard_map.146.pages) | copy-start | bytes 786436
  147.0 29.6 %copy-start.36 = (f32[1536]{0:T(1024)S(1)}, f32[1536]{0:T(1024)}, u32[]{:S(2)}) copy-start(f32[1536]{0:T(1024)} %param.15) | copy-start | bytes 18436
  147.0 22.0 %all-to-all-start.2 = ((bf16[4,1280,128]{2,1,0:T(8,128)(2,1)}), bf16[4,1280,128]{2,1,0:T(8,128)(2,1)}, u32[]{:S(2)}, u32[]{:S(2)}) async-start(bf16[4,1280,128]{2,1,0:T(8,128)(2,1)} %shard_map.147), calls=%async_computation.2 | async-start | bytes 2621440 | tf_op jit(solution)/shard_map/all_to_all | solution.py:493
  151.7 27.2 %collective-permute-start.7 = (bf16[768,1536]{1,0:T(8,128)(2,1)S(1)}, bf16[768,1536]{1,0:T(8,128)(2,1)}, u32[]{:S(2)}, u32[]{:S(2)}) collective-permute-start(bf16[768,1536]{1,0:T(8,128)(2,1)S(1)} %shard_map.145.own), channel_id=1, source_target_pairs={{1,0},{3,2},{5,4},{7,6},{8,9},{10,11},{12,13},{14,15},{17,16},{19,... | collective-permute-start | bytes 7077896 | tf_op jit(solution)/shard_map/ppermute | solution.py:36
  171.9 7.0 %collective-permute-start.8 = (bf16[768,1536]{1,0:T(8,128)(2,1)}, bf16[768,1536]{1,0:T(8,128)(2,1)}, u32[]{:S(2)}, u32[]{:S(2)}) collective-permute-start(bf16[768,1536]{1,0:T(8,128)(2,1)} %all-gather.5.cloned.1.call-done.other), channel_id=1, source_target_pairs={{0,1},{2,3},{4,5},{6,7},{9,8},{11,10},{13,12},{15,14},{16,17},{18,... | collective-permute-start | bytes 7077896 | tf_op jit(solution)/shard_map/ppermute | solution.py:36
  174.7 4.2 %collective-permute-start.6 = (bf16[640,512]{1,0:T(8,128)(2,1)}, bf16[640,512]{1,0:T(8,128)(2,1)S(1)}, u32[]{:S(2)}, u32[]{:S(2)}) collective-permute-start(bf16[640,512]{1,0:T(8,128)(2,1)} %get-tuple-element.56), channel_id=1, source_target_pairs={{0,1},{1,0},{2,3},{3,2},{4,5},{5,4},{6,7},{7,6},{8,9},{9,8},{10,11... | collective-permute-start | bytes 1966088 | tf_op jit(solution)/shard_map/ppermute | solution.py:36
  178.9 0.9 copy-start.7
  187.9 3.8 %copy-start.6 = (bf16[640,512]{1,0:T(8,128)(2,1)S(1)}, bf16[640,512]{1,0:T(8,128)(2,1)}, u32[]{:S(2)}) copy-start(bf16[640,512]{1,0:T(8,128)(2,1)} %get-tuple-element.65.keep) | copy-start | bytes 1966084
  187.9 3.8 %copy-start.8 = (bf16[640,512]{1,0:T(8,128)(2,1)S(1)}, bf16[640,512]{1,0:T(8,128)(2,1)}, u32[]{:S(2)}) copy-start(bf16[640,512]{1,0:T(8,128)(2,1)} %copy-done.7) | copy-start | bytes 1966084
  187.9 3.8 %copy-start.26 = (s32[6]{0:T(128)S(1)}, s32[6]{0:T(128)}, u32[]{:S(2)}) copy-start(s32[6]{0:T(128)} %copy-done.24) | copy-start | bytes 76
  187.9 21.0 %copy-start.19 = (bf16[128,1536]{1,0:T(8,128)(2,1)S(1)}, bf16[128,1536]{1,0:T(8,128)(2,1)}, u32[]{:S(2)}) copy-start(bf16[128,1536]{1,0:T(8,128)(2,1)} %get-tuple-element.63.mid) | copy-start | bytes 1179652
  187.9 21.0 %copy-start.29 = (f32[128,2]{0,1:T(2,128)S(1)}, f32[128,2]{0,1:T(2,128)}, u32[]{:S(2)}) copy-start(f32[128,2]{0,1:T(2,128)} %param.21) | copy-start | bytes 3076
  187.9 21.0 %all-to-all-start.3 = ((bf16[8,48,1536]{2,1,0:T(8,128)(2,1)}), bf16[8,48,1536]{2,1,0:T(8,128)(2,1)S(1)}, u32[]{:S(2)}, u32[]{:S(2)}) async-start(bf16[8,48,1536]{2,1,0:T(8,128)(2,1)} %bitcast.23), calls=%async_computation.3 | async-start | bytes 2359296 | tf_op jit(solution)/shard_map/all_to_all | solution.py:522
Sparse Core Ops, SparseCore 0:
  72.8 48.1 all-gather.2
  126.4 35.6 all-gather.4
